TPU v7x, 32 devices: a whole 2x2x4 slice. The times are simulated.
32 devices in a mesh: groups: 2 (over x), seq: 16 (over z, y, core).
Axes of the slice: x: 2, y: 2, z: 4, core: 2. Of those that a mesh axis runs over, the one named last changes fastest.
Arguments:
- video: bfloat16 [32, 32, 1408], P(('groups', 'seq')), parts along dimension 0, may hold values from -6 to 6
- spatial_qkv: bfloat16 [1408, 2112], P('seq'), may hold values from -1 to 1
- spatial_out: bfloat16 [704, 1408], P(None, 'seq'), may hold values from -0.21875 to 0.21875
- temporal_qkv: bfloat16 [1408, 2112], P('seq'), may hold values from -1 to 1
- temporal_out: bfloat16 [704, 1408], P(None, 'seq'), may hold values from -0.21875 to 0.21875
Outputs:
- result: bfloat16 [32, 32, 1408], P(('groups', 'seq')), parts along dimension 0
There are 2 independent parts, one for each index of `groups`. A program takes and returns all parts, laid end to end along the dimension named above; an argument that names none is the same for every part. Nothing has to cross between parts.
All inputs are finite; a program needn't handle non-finite values.
Results may differ from a plain program's by a relative error of at most 0.0065.
Values may be sent and summed in bfloat16 or wider, within the bound.
No kernel may reach another device: no remote copies, remote signals or barrier semaphores. Data moves between devices by JAX's collectives and lax.ppermute only.
A program may use at most 128 MiB of HBM per device.

v0:
```python
import jax
import jax.numpy as jnp
from jax import lax
from jax.sharding import PartitionSpec as P

HEADS = 8
HEAD_DIM = 88


def normalize(tokens):
    values = tokens.astype(jnp.float32)
    center = values - jnp.mean(values, axis=-1, keepdims=True)
    variance = jnp.mean(center * center, axis=-1, keepdims=True)
    return (center * lax.rsqrt(variance + 1e-06)).astype(jnp.bfloat16)


def attend(queries, keys_in, values_in):
    scores = jnp.einsum(
        "bqhe,bkhe->bhqk", queries, keys_in, preferred_element_type=jnp.float32
    ) * HEAD_DIM ** (-0.5)
    weights = jax.nn.softmax(scores, axis=-1).astype(jnp.bfloat16)
    return jnp.einsum(
        "bhqk,bkhe->bqhe", weights, values_in, preferred_element_type=jnp.float32
    ).astype(jnp.bfloat16)


def body(video, spatial_qkv, spatial_out, temporal_qkv, temporal_out):
    frames, patches, model_width = video.shape
    head_total = HEADS * HEAD_DIM
    flat = video.reshape(-1, model_width)
    normed = normalize(flat)
    gathered = (
        lax.all_gather(spatial_qkv, "seq", axis=0, tiled=True),
        lax.all_gather(spatial_out, "seq", axis=1, tiled=True),
        lax.all_gather(temporal_qkv, "seq", axis=0, tiled=True),
        lax.all_gather(temporal_out, "seq", axis=1, tiled=True),
    )
    packed = (
        jnp.dot(normed, gathered[0], preferred_element_type=jnp.float32)
        .astype(jnp.bfloat16)
        .reshape(frames, patches, 3, HEADS, HEAD_DIM)
    )
    spatial = attend(packed[:, :, 0], packed[:, :, 1], packed[:, :, 2]).reshape(-1, head_total)
    mixed = (
        flat.astype(jnp.float32) + jnp.dot(spatial, gathered[1], preferred_element_type=jnp.float32)
    ).astype(jnp.bfloat16)
    mixed = mixed.reshape(frames, patches, model_width)
    moved = lax.all_to_all(mixed, "seq", split_axis=1, concat_axis=0, tiled=True)
    all_frames, local_patches = (moved.shape[0], moved.shape[1])
    normed_two = normalize(moved.reshape(-1, model_width))
    packed_two = jnp.dot(normed_two, gathered[2], preferred_element_type=jnp.float32).astype(
        jnp.bfloat16
    )
    packed_two = packed_two.reshape(all_frames, local_patches, 3, HEADS, HEAD_DIM).transpose(
        1, 0, 2, 3, 4
    )
    temporal = attend(packed_two[:, :, 0], packed_two[:, :, 1], packed_two[:, :, 2])
    temporal = temporal.transpose(1, 0, 2, 3).reshape(all_frames, local_patches, head_total)
    update = jnp.dot(
        temporal.reshape(-1, head_total), gathered[3], preferred_element_type=jnp.float32
    ).reshape(all_frames, local_patches, model_width)
    finished = (moved.astype(jnp.float32) + update).astype(jnp.bfloat16)
    return lax.all_to_all(finished, "seq", split_axis=0, concat_axis=1, tiled=True)


def solution(mesh):
    in_specs = (
        P(("groups", "seq"), None, None),
        P("seq", None),
        P(None, "seq"),
        P("seq", None),
        P(None, "seq"),
    )
    out_specs = P(("groups", "seq"), None, None)
    return jax.shard_map(body, mesh=mesh, in_specs=in_specs, out_specs=out_specs, check_vma=False)
```

profile of v0, /device:TPU:0, one launch (start us, length us, event | category | flops | bytes accessed | tf_op | source)
XLA Modules:
  0.0 240.3 jit_solution(134062477656876005)
XLA Ops:
  6.5 0.0 copy-start
  6.5 0.0 all-gather.5.cloned.1.call-start
  6.5 0.7 all-gather.5.cloned.1.call-update
  7.3 0.0 all-gather.7.cloned.1.call-start
  7.3 0.7 all-gather.7.cloned.1.call-update
  8.0 0.0 all-gather.9.cloned.1.call-start
  8.1 0.7 all-gather.9.cloned.1.call-update
  8.7 0.0 all-gather.11.cloned.1.call-start
  8.8 0.5 all-gather.11.cloned.1.call-update
  9.3 1.0 convert_reduce_fusion
  10.3 1.1 fusion.15
  11.4 61.6 %all-gather.5.cloned.1.call-done = bf16[1408,2112]{1,0:T(8,128)(2,1)} async-done(((bf16[88,2112]{1,0:T(8,128)(2,1)}), bf16[1408,2112]{1,0:T(8,128)(2,1)}) %all-gather.5.cloned.1.call-update) | async-done | bytes 5947408 | tf_op jit(solution)/shard_map/all_gather | solution.py:33
  73.0 4.0 %convolution_convert_fusion.1 = bf16[32,2112]{1,0:T(8,128)(2,1)S(1)} fusion(bf16[1408,2112]{1,0:T(8,128)(2,1)} %all-gather.5.cloned.1.call-done, bf16[1,32,1408]{2,1,0:T(8,128)(2,1)} %param.5, f32[32]{0:T(128)S(1)} %add_rsqrt_fusion.1, f32[32]{0:T(128)S(1)} %broadcast_multiply_fusion.1), kind=kOutput, calls=%fused_computation.3 | convolution fusion | flops 190564352 | bytes 6172928 | tf_op jit(solution)/shard_map/dot_general | solution.py:39
  77.0 0.3 reshape.86
  77.3 0.2 fusion.29
  77.5 0.2 fusion.10
  77.8 0.1 reshape.90
  77.9 37.5 %all-gather.7.cloned.1.call-done = bf16[704,1408]{0,1:T(8,128)(2,1)} async-done(((bf16[704,88]{0,1:T(8,128)(2,1)}), bf16[704,1408]{0,1:T(8,128)(2,1)}) %all-gather.7.cloned.1.call-update) | async-done | bytes 1982480 | tf_op jit(solution)/shard_map/all_gather | solution.py:34
  115.4 0.0 copy-done
  115.4 2.3 fusion.4
  117.7 0.2 copy.79
  117.9 0.5 broadcast.58
  118.4 1.2 reduce.8
  119.6 10.8 %all_to_all.21 = bf16[16,2,1408]{2,1,0:T(2,128)(2,1)S(1)} all-to-all(bf16[16,2,1408]{2,1,0:T(2,128)(2,1)S(1)} %reshape.96), channel_id=1, replica_groups=mesh['groups'=2,'seq'=16] {'seq'}, dimensions={0} | all-to-all | bytes 180224 | tf_op jit(solution)/shard_map/all_to_all | solution.py:48
  130.5 0.1 reshape.97
  130.5 1.0 convert_reduce_fusion.2
  131.5 0.2 bitcast_convert_fusion
  131.7 0.2 multiply_reduce_fusion
  131.9 45.7 %all-gather.9.cloned.1.call-done = bf16[1408,2112]{1,0:T(8,128)(2,1)} async-done(((bf16[88,2112]{1,0:T(8,128)(2,1)}), bf16[1408,2112]{1,0:T(8,128)(2,1)}) %all-gather.9.cloned.1.call-update) | async-done | bytes 5947408 | tf_op jit(solution)/shard_map/all_gather | solution.py:35
  177.7 3.9 %convolution_convert_fusion = bf16[32,2112]{1,0:T(8,128)(2,1)S(1)} fusion(bf16[1408,2112]{1,0:T(8,128)(2,1)} %all-gather.9.cloned.1.call-done, f32[1,32,1408]{2,0,1:T(1,128)S(1)} %bitcast_convert_fusion, f32[32]{0:T(128)S(1)} %add_rsqrt_fusion, f32[32]{0:T(128)S(1)} %broadcast_multiply_fusion), kind=kOutput, calls=%fused_computation.2 | convolution fusion | flops 190519296 | bytes 6263040 | tf_op jit(solution)/shard_map/dot_general | solution.py:51
  181.6 0.3 reshape.92
  181.9 0.1 copy.78
  182.0 0.2 fusion.30
  182.2 0.2 convolution_multiply_fusion
  182.3 0.2 fusion.11
  182.6 0.1 dot_general.33
  182.7 0.1 reshape.93
  182.8 37.1 %all-gather.11.cloned.1.call-done = bf16[704,1408]{0,1:T(8,128)(2,1)} async-done(((bf16[704,88]{0,1:T(8,128)(2,1)}), bf16[704,1408]{0,1:T(8,128)(2,1)}) %all-gather.11.cloned.1.call-update) | async-done | bytes 1982480 | tf_op jit(solution)/shard_map/all_gather | solution.py:36
  220.0 2.3 fusion.3
  222.3 0.1 copy.43
  222.4 10.7 %all_to_all.22 = bf16[16,2,1408]{2,1,0:T(2,128)(2,1)S(1)} all-to-all(bf16[16,2,1408]{2,1,0:T(2,128)(2,1)S(1)} %copy.43), channel_id=1, replica_groups=mesh['groups'=2,'seq'=16] {'seq'}, dimensions={0} | all-to-all | bytes 180224 | tf_op jit(solution)/shard_map/all_to_all | solution.py:63
  233.1 0.7 all_to_all.8
  (8 shorter events, 0.2 us)
Async XLA Ops:
  6.5 108.9 %copy-start = (bf16[1,32,1408]{2,1,0:T(8,128)(2,1)S(1)}, bf16[1,32,1408]{2,1,0:T(8,128)(2,1)}, u32[]{:S(2)}) copy-start(bf16[1,32,1408]{2,1,0:T(8,128)(2,1)} %param.5) | copy-start | bytes 270340
  6.5 66.5 %all-gather.5.cloned.1.call-start = ((), (), s32[]{:S(2)}) async-start(), calls=%async_computation.2 | async-start | bytes 6510592 | tf_op jit(solution)/shard_map/all_gather | solution.py:33
  7.3 108.2 %all-gather.7.cloned.1.call-start = ((), (), s32[]{:S(2)}) async-start(), calls=%async_computation.3 | async-start | bytes 2297856 | tf_op jit(solution)/shard_map/all_gather | solution.py:34
  8.0 169.7 %all-gather.9.cloned.1.call-start = ((), (), s32[]{:S(2)}) async-start(), calls=%async_computation.4 | async-start | bytes 6510592 | tf_op jit(solution)/shard_map/all_gather | solution.py:35
  8.7 211.2 %all-gather.11.cloned.1.call-start = ((), (), s32[]{:S(2)}) async-start(), calls=%async_computation.5 | async-start | bytes 2297856 | tf_op jit(solution)/shard_map/all_gather | solution.py:36
Sparse Core Ops, SparseCore 0:
  9.5 63.4 all-gather.4
  75.3 40.1 all-gather.6
  117.6 60.0 all-gather.8
  179.8 40.1 all-gather.10
where the time goes:
time: 241 us; the launch traced here: 240 us
  waiting for transfers between devices  185 us (77%)
  blocking collectives  21.5 us (9%)
  matrix products  13.6 us (6%)
  between operations  13.3 us (6%)
  other arithmetic  4.66 us (2%)
  local copies, waits for them, and re-layouts  2.59 us (1%)
    all_gather x1, waiting for transfers between devices, body(): lax.all_gather(spatial_qkv, 'seq', axis=0, tiled=True)  61.6 us
    all_gather x1, waiting for transfers between devices, body(): lax.all_gather(temporal_qkv, 'seq', axis=0, tiled=True)  45.7 us
    all_gather x1, waiting for transfers between devices, body(): lax.all_gather(spatial_out, 'seq', axis=1, tiled=True)  37.5 us
    all_gather x1, waiting for transfers between devices, body(): lax.all_gather(temporal_out, 'seq', axis=1, tiled=True)  37.1 us
    all_to_all x1, blocking collectives, body(): lax.all_to_all(mixed, 'seq', split_axis=1, concat_axis=0, tiled=True)  10.8 us
    all_to_all x1, blocking collectives, body(): lax.all_to_all(finished, 'seq', split_axis=0, concat_axis=1, tiled=True)  10.7 us
  transfers between devices with their start and end apart: 4, of which 4 were waited for; matrix products, arithmetic and copies ran while one was open for 7% of the time, Pallas kernels for 0%

commit v1 on v0

--- a/solution.py
+++ b/solution.py
@@ -1,6 +1,8 @@
 import jax
 import jax.numpy as jnp
 from jax import lax
+from jax.experimental import pallas as pl
+from jax.experimental.pallas import tpu as pltpu
 from jax.sharding import PartitionSpec as P
 
 HEADS = 8
@@ -24,7 +26,7 @@
     ).astype(jnp.bfloat16)
 
 
-def body(video, spatial_qkv, spatial_out, temporal_qkv, temporal_out):
+def gathered_weights_body(video, spatial_qkv, spatial_out, temporal_qkv, temporal_out):
     frames, patches, model_width = video.shape
     head_total = HEADS * HEAD_DIM
     flat = video.reshape(-1, model_width)
@@ -63,6 +65,110 @@
     return lax.all_to_all(finished, "seq", split_axis=0, concat_axis=1, tiled=True)
 
 
+COLUMNS = [[4 * z + 2 * y + k for z in range(4) for k in range(2)] for y in range(2)]
+ACROSS_Y = [(i, i ^ 2) for i in range(16)]
+
+
+def pack(w):
+    w = w.reshape(11, 8, 3, HEADS, HEAD_DIM)
+    return w.transpose(3, 1, 0, 2, 4).reshape(HEADS, 8, 11 * 3 * HEAD_DIM)
+
+
+def unpack(y, mine_ref, theirs_ref, wide_ref):
+    for half, ref in ((y, mine_ref), (1 - y, theirs_ref)):
+        for j in range(8):
+            slab = ref[j].astype(jnp.float32)
+            first = pl.multiple_of(88 * (4 * (j // 2) + 2 * half + j % 2), 8)
+            for g in range(11):
+                wide_ref[pl.ds(first + 8 * g, 8), :] = slab[:, 264 * g : 264 * (g + 1)]
+    return wide_ref[...].astype(jnp.bfloat16)
+
+
+def masked_attention(packed, same):
+    q, k, v = packed[:, :88], packed[:, 88:176], packed[:, 176:]
+    scores = lax.dot_general(q, k, (((1,), (1,)), ((), ())), preferred_element_type=jnp.float32) * HEAD_DIM ** (-0.5)
+    scores = jnp.where(same, scores, -jnp.inf)
+    top = jnp.max(scores, axis=-1, keepdims=True)
+    e = jnp.exp(scores - top)
+    weights = (e / jnp.sum(e, axis=-1, keepdims=True)).astype(jnp.bfloat16)
+    return jnp.dot(weights, v, preferred_element_type=jnp.float32).astype(jnp.bfloat16)
+
+
+def spatial_kernel(y_ref, tokens_ref, mine_ref, theirs_ref, out_ref, wide_ref):
+    w = unpack(y_ref[0], mine_ref, theirs_ref, wide_ref)
+    packed = jnp.dot(normalize(tokens_ref[...]), w, preferred_element_type=jnp.float32).astype(jnp.bfloat16)
+    n = packed.shape[0]
+    row = lax.broadcasted_iota(jnp.int32, (n, n), 0) // 32
+    col = lax.broadcasted_iota(jnp.int32, (n, n), 1) // 32
+    out_ref[...] = masked_attention(packed, row == col)
+
+
+def middle_kernel(y_ref, tokens_ref, spatial_ref, out_one_ref, mine_ref, theirs_ref, mixed_ref, two_ref, wide_ref):
+    w = unpack(y_ref[0], mine_ref, theirs_ref, wide_ref)
+    heads = jnp.concatenate([spatial_ref[h] for h in range(8)], axis=1)
+    update = lax.dot_general(heads, out_one_ref[...], (((1,), (1,)), ((), ())), preferred_element_type=jnp.float32)
+    mixed = (tokens_ref[...].astype(jnp.float32) + update).astype(jnp.bfloat16)
+    mixed_ref[...] = mixed
+    two_ref[...] = jnp.dot(normalize(mixed), w, preferred_element_type=jnp.float32).astype(jnp.bfloat16)
+
+
+def temporal_kernel(packed_ref, out_ref):
+    n = packed_ref.shape[0]
+    row = lax.broadcasted_iota(jnp.int32, (n, n), 0) % 16
+    col = lax.broadcasted_iota(jnp.int32, (n, n), 1) % 16
+    out_ref[...] = masked_attention(packed_ref[...], row == col)
+
+
+VM = pl.BlockSpec(memory_space=pltpu.VMEM)
+SM = pl.BlockSpec(memory_space=pltpu.SMEM)
+
+
+def kernel_call(body, shapes, n_in, scratch=(), scalar=False):
+    return pl.pallas_call(
+        body,
+        out_shape=shapes,
+        in_specs=([SM] if scalar else []) + [VM] * n_in,
+        out_specs=jax.tree.map(lambda _: VM, shapes),
+        scratch_shapes=scratch,
+        compiler_params=pltpu.CompilerParams(vmem_limit_bytes=40 * 1024 * 1024),
+    )
+
+
+def head_body(video, spatial_qkv, spatial_out, temporal_qkv, temporal_out):
+    _, patches, D = video.shape
+    bf = jnp.bfloat16
+    y = (lax.axis_index("seq") // 2) % 2
+    ys = y.reshape(1)
+    out_one = lax.all_gather(spatial_out.T, "seq", axis=0, tiled=True)
+    one = lax.all_to_all(pack(spatial_qkv), "seq", 0, 0, tiled=True, axis_index_groups=COLUMNS)
+    tokens = lax.all_gather(video.reshape(patches, D), "seq", axis=0, tiled=True, axis_index_groups=COLUMNS)
+    one, tokens, two_p = lax.optimization_barrier((one, tokens, pack(temporal_qkv)))
+    one_o = lax.ppermute(one, "seq", ACROSS_Y)
+    two_w = lax.all_to_all(two_p, "seq", 0, 0, tiled=True, axis_index_groups=COLUMNS)
+    wide = [pltpu.VMEM((D, 264), jnp.float32)]
+    spatial = kernel_call(spatial_kernel, jax.ShapeDtypeStruct((256, 88), bf), 3, wide, True)(ys, tokens, one, one_o)
+    spatial, two_w, t_out = lax.optimization_barrier((spatial, two_w, temporal_out.T))
+    out_two = lax.all_gather(t_out, "seq", axis=0, tiled=True)
+    two_o = lax.ppermute(two_w, "seq", ACROSS_Y)
+    spatial = lax.all_gather(spatial, "seq", axis=0, tiled=False, axis_index_groups=COLUMNS)
+    mixed, two = kernel_call(
+        middle_kernel, (jax.ShapeDtypeStruct((256, D), bf), jax.ShapeDtypeStruct((256, 264), bf)), 5, wide, True
+    )(ys, tokens, spatial, out_one, two_w, two_o)
+    two = two.reshape(8, 2, patches // 2, 264)
+    keep = jnp.where(y == 0, two[:, 0], two[:, 1])
+    send = jnp.where(y == 0, two[:, 1], two[:, 0])
+    other = lax.ppermute(send, "seq", ACROSS_Y)
+    both = jnp.where(y == 0, jnp.stack([keep, other], 1), jnp.stack([other, keep], 1))
+    both = both.reshape(4, 2, 2, patches // 2, 264).transpose(0, 2, 1, 3, 4).reshape(256, 264)
+    temporal = kernel_call(temporal_kernel, jax.ShapeDtypeStruct((256, 88), bf), 1)(both).reshape(16, patches // 2, 88)
+    temporal = lax.all_to_all(temporal, "seq", 0, 0, tiled=True)
+    temporal = temporal.reshape(4, 2, 2, patches // 2, 88).transpose(1, 3, 0, 2, 4).reshape(patches, 704)
+    me = 2 * (lax.axis_index("seq") // 4) + lax.axis_index("seq") % 2
+    own = lax.dynamic_slice_in_dim(mixed, me * patches, patches, axis=0)
+    result = own.astype(jnp.float32) + lax.dot_general(temporal, out_two, (((1,), (1,)), ((), ())), preferred_element_type=jnp.float32)
+    return result.astype(jnp.bfloat16).reshape(1, patches, D)
+
+
 def solution(mesh):
     in_specs = (
         P(("groups", "seq"), None, None),
@@ -72,4 +178,5 @@
         P(None, "seq"),
     )
     out_specs = P(("groups", "seq"), None, None)
+    body = head_body if mesh.shape["seq"] == 16 else gathered_weights_body
     return jax.shard_map(body, mesh=mesh, in_specs=in_specs, out_specs=out_specs, check_vma=False)

time: 241 us -> 115 us (0.48)
  waiting for transfers between devices: 185 us -> 27.3 us
  starting transfers between devices: 0.12 us -> 19.6 us
  blocking collectives: 21.5 us -> 39 us
  matrix products: 13.6 us -> 2.99 us
  Pallas kernels: 0 us -> 4.91 us
  other arithmetic: 4.66 us -> 0.08 us
  local copies, waits for them, and re-layouts: 2.59 us -> 6.85 us
    all_gather x4 -> x2, waiting for transfers between devices: 182 us -> 2.76 us  [the longest x1 2.76 us: head_body(): out_two = lax.all_gather(t_out, 'seq', axis=0, tiled=True)]
    all_gather x0 -> x2, blocking collectives: none -> 39 us  [the longest x1 23.2 us: head_body(): lax.all_gather(video.reshape(patches, D), 'seq', axis=0, tiled=True, axis...]
    all_to_all x2 -> x0, blocking collectives: 21.5 us -> none  [the longest x1 10.8 us: body(): lax.all_to_all(mixed, 'seq', split_axis=1, concat_axis=0, tiled=True)]
    all_to_all x0 -> x3, starting transfers between devices: none -> 15 us  [the longest x1 6.46 us: head_body(): lax.all_to_all(pack(spatial_qkv), 'seq', 0, 0, tiled=True, axis_index_gro...]
    ppermute x0 -> x3, waiting for transfers between devices: none -> 13.1 us  [the longest x1 9.42 us: head_body(): one_o = lax.ppermute(one, 'seq', ACROSS_Y)]
    all_to_all x0 -> x3, waiting for transfers between devices: none -> 10.7 us  [the longest x1 7.92 us: head_body(): temporal = lax.all_to_all(temporal, 'seq', 0, 0, tiled=True)]
    dot_general x7 -> x1, matrix products: 13.1 us -> 2.99 us  [head_body(): lax.dot_general(temporal, out_two, (((1,), (1,)), ((), ())), preferred_el...]
    pallas_call x0 -> x3, Pallas kernels: none -> 4.91 us  [the longest x1 1.84 us: head_body(): kernel_call(spatial_kernel, jax.ShapeDtypeStruct((256, 88), bf), 3, wide,...]
  transfers between devices with their start and end apart: 4 -> 8, of which waited for: 4 -> 5; matrix products, arithmetic and copies ran while one was open for 7% -> 5% of each run, Pallas kernels for 0% -> 4%
where the time goes in v1:
time: 115 us; the launch traced here: 114 us
  blocking collectives  39 us (34%)
  waiting for transfers between devices  27.3 us (24%)
  starting transfers between devices  19.6 us (17%)
  between operations  13.5 us (12%)
  local copies, waits for them, and re-layouts  6.85 us (6%)
  Pallas kernels  4.91 us (4%)
  matrix products  2.99 us (3%)
    all_gather x1, blocking collectives, head_body(): lax.all_gather(video.reshape(patches, D), 'seq', axis=0, tiled=True, axis...  23.2 us
    all_gather x1, blocking collectives, head_body(): lax.all_gather(spatial, 'seq', axis=0, tiled=False, axis_index_groups=COL...  15.8 us
    ppermute x1, waiting for transfers between devices, head_body(): one_o = lax.ppermute(one, 'seq', ACROSS_Y)  9.42 us
    all_to_all x1, waiting for transfers between devices, head_body(): temporal = lax.all_to_all(temporal, 'seq', 0, 0, tiled=True)  7.92 us
    all_to_all x1, starting transfers between devices, head_body(): lax.all_to_all(pack(spatial_qkv), 'seq', 0, 0, tiled=True, axis_index_gro...  6.46 us
    all_to_all x1, starting transfers between devices, head_body(): lax.all_to_all(two_p, 'seq', 0, 0, tiled=True, axis_index_groups=COLUMNS)  4.64 us
    all_to_all x1, starting transfers between devices, head_body(): temporal = lax.all_to_all(temporal, 'seq', 0, 0, tiled=True)  3.86 us
    ppermute x1, waiting for transfers between devices, head_body(): other = lax.ppermute(send, 'seq', ACROSS_Y)  3.67 us
  transfers between devices with their start and end apart: 8, of which 5 were waited for; matrix products, arithmetic and copies ran while one was open for 5% of the time, Pallas kernels for 4%

profile of v1, /device:TPU:0, one launch (start us, length us, event | category | flops | bytes accessed | tf_op | source)
XLA Modules:
  0.0 114.2 jit_solution(1346931626519628271)
XLA Ops:
  6.5 0.0 copy-start.1
  6.5 0.0 all-gather.5.cloned.1.call-start
  6.5 0.7 all-gather.5.cloned.1.call-update
  7.3 1.6 %reshape.46 = bf16[11,8,3,8,88]{4,3,2,1,0:T(8,128)(2,1)S(1)} reshape(bf16[88,2112]{1,0:T(8,128)(2,1)} %param.6) | data formatting | bytes 743424 | tf_op jit(solution)/shard_map/reshape | solution.py:73
  8.9 0.3 copy.16
  9.2 1.1 reshape.47
  10.3 0.0 copy-start.2
  10.3 6.5 %all-to-all-start = ((bf16[8,8,2904]{2,1,0:T(8,128)(2,1)}), bf16[8,8,2904]{2,1,0:T(8,128)(2,1)S(1)}, u32[]{:S(2)}, u32[]{:S(2)}) async-start(bf16[8,8,2904]{2,1,0:T(8,128)(2,1)} %reshape.47), calls=%async_computation | async-start | bytes 753664 | tf_op jit(solution)/shard_map/all_to_all | solution.py:143
  16.8 0.0 copy-done.1
  16.8 0.7 reshape.49
  17.4 0.3 copy.15
  17.7 1.1 reshape.50
  18.8 0.0 copy-done.2
  18.8 23.2 %all-gather = bf16[1,256,1408]{2,1,0:T(8,128)(2,1)S(1)} all-gather(bf16[1,32,1408]{2,1,0:T(8,128)(2,1)S(1)} %copy-done.2), channel_id=2, replica_groups={{0,1,4,5,8,9,12,13},{2,3,6,7,10,11,14,15},{16,17,20,21,24,25,28,29},{18..., dimensions={1}, use_global_device_ids=true | all-gather | bytes 811008 | tf_op jit(solution)/shard_map/all_gather | solution.py:144
  42.0 0.0 all-to-all-done.mine_ref
  42.0 4.6 %all-to-all-start.1 = ((bf16[8,8,2904]{2,1,0:T(8,128)(2,1)}), bf16[8,8,2904]{2,1,0:T(8,128)(2,1)S(1)}, u32[]{:S(2)}, u32[]{:S(2)}) async-start(bf16[8,8,2904]{2,1,0:T(8,128)(2,1)} %reshape.50), calls=%async_computation.1 | async-start | bytes 753664 | tf_op jit(solution)/shard_map/all_to_all | solution.py:147
  46.6 0.0 all-gather.7.cloned.1.call-start
  46.7 1.7 %collective-permute-start = (bf16[8,8,2904]{2,1,0:T(8,128)(2,1)S(1)}, bf16[8,8,2904]{2,1,0:T(8,128)(2,1)S(1)}, u32[]{:S(2)}, u32[]{:S(2)}) collective-permute-start(bf16[8,8,2904]{2,1,0:T(8,128)(2,1)S(1)} %all-to-all-done.mine_ref), channel_id=1, source_target_pairs={{0,2},{1,3},{2,0},{3,1},{4,6},{5,7},{6,4},{7,5},{8,10},{9,11},{10,... | collective-permute-start | bytes 1115144 | tf_op jit(solution)/shard_map/ppermute | solution.py:146
  48.4 9.4 %collective-permute-done.theirs_ref = bf16[8,8,2904]{2,1,0:T(8,128)(2,1)S(1)} collective-permute-done((bf16[8,8,2904]{2,1,0:T(8,128)(2,1)S(1)}, bf16[8,8,2904]{2,1,0:T(8,128)(2,1)S(1)}, u32[]{:S(2)}, u32[]{:S(2)}) %collective-permute-start) | collective-permute-done | bytes 371744 | tf_op jit(solution)/shard_map/ppermute | solution.py:146
  57.9 1.8 %shard_map.55 = bf16[256,88]{1,0:T(8,128)(2,1)S(1)} custom-call(s32[1]{0:T(128)} %bitcast.y_ref, bf16[256,1408]{1,0:T(8,128)(2,1)S(1)} %bitcast.27, bf16[8,8,2904]{2,1,0:T(8,128)(2,1)S(1)} %all-to-all-done.mine_ref, bf16[8,8,2904]{2,1,0:T(8,128)(2,1)S(1)} %collective-permute-done.theirs_ref), custom_call_target="tpu_custom_call" | custom-call | tf_op jit(solution)/shard_map/pallas_call | solution.py:149
  59.7 2.8 %all-to-all-done.1.mine_ref = bf16[8,8,2904]{2,1,0:T(8,128)(2,1)S(1)} async-done(((bf16[8,8,2904]{2,1,0:T(8,128)(2,1)}), bf16[8,8,2904]{2,1,0:T(8,128)(2,1)S(1)}, u32[]{:S(2)}, u32[]{:S(2)}) %all-to-all-start.1) | async-done | bytes 371744 | tf_op jit(solution)/shard_map/all_to_all | solution.py:147
  62.5 0.0 all-gather.7.cloned.1.call-update
  62.5 1.2 %collective-permute-start.1 = (bf16[8,8,2904]{2,1,0:T(8,128)(2,1)S(1)}, bf16[8,8,2904]{2,1,0:T(8,128)(2,1)S(1)}, u32[]{:S(2)}, u32[]{:S(2)}) collective-permute-start(bf16[8,8,2904]{2,1,0:T(8,128)(2,1)S(1)} %all-to-all-done.1.mine_ref), channel_id=1, source_target_pairs={{0,2},{1,3},{2,0},{3,1},{4,6},{5,7},{6,4},{7,5},{8,10},{9,11},{10,... | collective-permute-start | bytes 1115144 | tf_op jit(solution)/shard_map/ppermute | solution.py:152
  63.7 15.8 %all-gather.1 = bf16[2048,88]{1,0:T(8,128)(2,1)S(1)} all-gather(bf16[256,88]{1,0:T(8,128)(2,1)S(1)} %shard_map.55), channel_id=3, replica_groups={{0,1,4,5,8,9,12,13},{2,3,6,7,10,11,14,15},{16,17,20,21,24,25,28,29},{18..., dimensions={0}, use_global_device_ids=true | all-gather | bytes 405504 | tf_op jit(solution)/shard_map/all_gather | solution.py:153
  79.5 0.0 collective-permute-done.1.theirs_ref
  79.5 0.0 all-gather.5.cloned.1.call-done.out_one_ref
  79.5 0.0 copy-start
  79.5 1.6 %copy-done = bf16[1408,704]{1,0:T(8,128)(2,1)S(1)} copy-done((bf16[1408,704]{1,0:T(8,128)(2,1)S(1)}, bf16[1408,704]{1,0:T(8,128)(2,1)}, u32[]{:S(2)}) %copy-start) | copy-done | bytes 1982488
  81.1 1.8 %shard_map.56 = (bf16[256,1408]{1,0:T(8,128)(2,1)S(1)}, bf16[256,264]{1,0:T(8,128)(2,1)S(1)}) custom-call(s32[1]{0:T(128)} %bitcast.y_ref, bf16[256,1408]{1,0:T(8,128)(2,1)S(1)} %bitcast.28, bf16[8,256,88]{2,1,0:T(8,128)(2,1)S(1)} %bitcast.29, bf16[1408,704]{1,0:T(8,128)(2,1)S(1)} %copy-done, bf16[8,8,2904]{2,1,0:T(8,128)(2,1)S(1)} %all-to-all-done.1.mine_ref, ...), custom_call_target="tpu_custom_call" | custom-call | tf_op jit(solution)/shard_map/pallas_call | solution.py:154
  82.9 1.7 %collective-permute-start.2 = (bf16[8,16,264]{2,1,0:T(8,128)(2,1)S(1)}, bf16[8,16,264]{2,1,0:T(8,128)(2,1)S(1)}, u32[]{:S(2)}, u32[]{:S(2)}) collective-permute-start(bf16[8,16,264]{2,1,0:T(8,128)(2,1)S(1)} %get-tuple-element.22), channel_id=1, source_target_pairs={{0,2},{1,3},{2,0},{3,1},{4,6},{5,7},{6,4},{7,5},{8,10},{9,11},{10,... | collective-permute-start | bytes 202760 | tf_op jit(solution)/shard_map/ppermute | solution.py:160
  84.6 3.7 %collective-permute-done.2 = bf16[8,16,264]{2,1,0:T(8,128)(2,1)S(1)} collective-permute-done((bf16[8,16,264]{2,1,0:T(8,128)(2,1)S(1)}, bf16[8,16,264]{2,1,0:T(8,128)(2,1)S(1)}, u32[]{:S(2)}, u32[]{:S(2)}) %collective-permute-start.2) | collective-permute-done | bytes 67616 | tf_op jit(solution)/shard_map/ppermute | solution.py:160
  88.3 0.1 maximum_select_fusion
  88.4 1.3 %shard_map.57 = bf16[256,88]{1,0:T(8,128)(2,1)} custom-call(bf16[256,264]{1,0:T(8,128)(2,1)S(1)} %bitcast.30), custom_call_target="tpu_custom_call" | custom-call | tf_op jit(solution)/shard_map/pallas_call | solution.py:163
  89.6 3.9 %all-to-all-start.2 = ((bf16[16,16,88]{2,1,0:T(8,128)(2,1)}), bf16[16,16,88]{2,1,0:T(8,128)(2,1)S(1)}, u32[]{:S(2)}, u32[]{:S(2)}) async-start(bf16[16,16,88]{2,1,0:T(8,128)(2,1)} %bitcast.13), calls=%async_computation.2 | async-start | bytes 131072 | tf_op jit(solution)/shard_map/all_to_all | solution.py:164
  93.5 7.9 %all-to-all-done.2 = bf16[16,16,88]{2,1,0:T(8,128)(2,1)S(1)} async-done(((bf16[16,16,88]{2,1,0:T(8,128)(2,1)}), bf16[16,16,88]{2,1,0:T(8,128)(2,1)S(1)}, u32[]{:S(2)}, u32[]{:S(2)}) %all-to-all-start.2) | async-done | bytes 45088 | tf_op jit(solution)/shard_map/all_to_all | solution.py:164
  101.4 0.1 copy.12
  101.5 0.1 reshape.55
  101.6 2.8 %all-gather.7.cloned.1.call-done = bf16[1408,704]{1,0:T(8,128)(2,1)} async-done(((bf16[88,704]{1,0:T(8,128)(2,1)}), bf16[1408,704]{1,0:T(8,128)(2,1)}) %all-gather.7.cloned.1.call-update) | async-done | bytes 1982480 | tf_op jit(solution)/shard_map/all_gather | solution.py:151
  104.4 3.0 %fusion = bf16[1,32,1408]{2,1,0:T(8,128)(2,1)} fusion(bf16[256,1408]{1,0:T(8,128)(2,1)S(1)} %get-tuple-element.18, s32[]{:T(128)S(6)} %select_n.50, bf16[32,704]{1,0:T(8,128)(2,1)S(1)} %reshape.55, bf16[1408,704]{1,0:T(8,128)(2,1)} %all-gather.7.cloned.1.call-done), kind=kOutput, calls=%fused_computation.6 | convolution fusion | flops 63574016 | bytes 2207748 | tf_op jit(solution)/shard_map/dot_general | solution.py:168
  (1 shorter events, 0.0 us)
Async XLA Ops:
  6.5 10.2 %copy-start.1 = (bf16[88,2112]{1,0:T(8,128)(2,1)S(1)}, bf16[88,2112]{1,0:T(8,128)(2,1)}, u32[]{:S(2)}) copy-start(bf16[88,2112]{1,0:T(8,128)(2,1)} %param.8) | copy-start | bytes 1115140
  6.5 72.9 %all-gather.5.cloned.1.call-start = ((), (), s32[]{:S(2)}) async-start(), calls=%async_computation.3 | async-start | bytes 2297856 | tf_op jit(solution)/shard_map/all_gather | solution.py:142
  10.3 8.5 %copy-start.2 = (bf16[1,32,1408]{2,1,0:T(8,128)(2,1)S(1)}, bf16[1,32,1408]{2,1,0:T(8,128)(2,1)}, u32[]{:S(2)}) copy-start(bf16[1,32,1408]{2,1,0:T(8,128)(2,1)} %param.5) | copy-start | bytes 270340
  10.3 31.7 %all-to-all-start = ((bf16[8,8,2904]{2,1,0:T(8,128)(2,1)}), bf16[8,8,2904]{2,1,0:T(8,128)(2,1)S(1)}, u32[]{:S(2)}, u32[]{:S(2)}) async-start(bf16[8,8,2904]{2,1,0:T(8,128)(2,1)} %reshape.47), calls=%async_computation | async-start | bytes 753664 | tf_op jit(solution)/shard_map/all_to_all | solution.py:143
  42.0 20.4 %all-to-all-start.1 = ((bf16[8,8,2904]{2,1,0:T(8,128)(2,1)}), bf16[8,8,2904]{2,1,0:T(8,128)(2,1)S(1)}, u32[]{:S(2)}, u32[]{:S(2)}) async-start(bf16[8,8,2904]{2,1,0:T(8,128)(2,1)} %reshape.50), calls=%async_computation.1 | async-start | bytes 753664 | tf_op jit(solution)/shard_map/all_to_all | solution.py:147
  46.6 57.7 %all-gather.7.cloned.1.call-start = ((), (), s32[]{:S(2)}) async-start(), calls=%async_computation.4 | async-start | bytes 2297856 | tf_op jit(solution)/shard_map/all_gather | solution.py:151
  46.7 11.2 %collective-permute-start = (bf16[8,8,2904]{2,1,0:T(8,128)(2,1)S(1)}, bf16[8,8,2904]{2,1,0:T(8,128)(2,1)S(1)}, u32[]{:S(2)}, u32[]{:S(2)}) collective-permute-start(bf16[8,8,2904]{2,1,0:T(8,128)(2,1)S(1)} %all-to-all-done.mine_ref), channel_id=1, source_target_pairs={{0,2},{1,3},{2,0},{3,1},{4,6},{5,7},{6,4},{7,5},{8,10},{9,11},{10,... | collective-permute-start | bytes 1115144 | tf_op jit(solution)/shard_map/ppermute | solution.py:146
  62.5 17.0 %collective-permute-start.1 = (bf16[8,8,2904]{2,1,0:T(8,128)(2,1)S(1)}, bf16[8,8,2904]{2,1,0:T(8,128)(2,1)S(1)}, u32[]{:S(2)}, u32[]{:S(2)}) collective-permute-start(bf16[8,8,2904]{2,1,0:T(8,128)(2,1)S(1)} %all-to-all-done.1.mine_ref), channel_id=1, source_target_pairs={{0,2},{1,3},{2,0},{3,1},{4,6},{5,7},{6,4},{7,5},{8,10},{9,11},{10,... | collective-permute-start | bytes 1115144 | tf_op jit(solution)/shard_map/ppermute | solution.py:152
  79.5 1.6 %copy-start = (bf16[1408,704]{1,0:T(8,128)(2,1)S(1)}, bf16[1408,704]{1,0:T(8,128)(2,1)}, u32[]{:S(2)}) copy-start(bf16[1408,704]{1,0:T(8,128)(2,1)} %all-gather.5.cloned.1.call-done.out_one_ref) | copy-start | bytes 5947396
  82.9 5.4 %collective-permute-start.2 = (bf16[8,16,264]{2,1,0:T(8,128)(2,1)S(1)}, bf16[8,16,264]{2,1,0:T(8,128)(2,1)S(1)}, u32[]{:S(2)}, u32[]{:S(2)}) collective-permute-start(bf16[8,16,264]{2,1,0:T(8,128)(2,1)S(1)} %get-tuple-element.22), channel_id=1, source_target_pairs={{0,2},{1,3},{2,0},{3,1},{4,6},{5,7},{6,4},{7,5},{8,10},{9,11},{10,... | collective-permute-start | bytes 202760 | tf_op jit(solution)/shard_map/ppermute | solution.py:160
  89.6 11.8 %all-to-all-start.2 = ((bf16[16,16,88]{2,1,0:T(8,128)(2,1)}), bf16[16,16,88]{2,1,0:T(8,128)(2,1)S(1)}, u32[]{:S(2)}, u32[]{:S(2)}) async-start(bf16[16,16,88]{2,1,0:T(8,128)(2,1)} %bitcast.13), calls=%async_computation.2 | async-start | bytes 131072 | tf_op jit(solution)/shard_map/all_to_all | solution.py:164
Sparse Core Ops, SparseCore 0:
  9.6 49.8 all-gather.4
  62.6 41.7 all-gather.6

commit v2 on v1

--- a/solution.py
+++ b/solution.py
@@ -74,6 +74,20 @@
     return w.transpose(3, 1, 0, 2, 4).reshape(HEADS, 8, 11 * 3 * HEAD_DIM)
 
 
+def pack_kernel(w_ref, out_ref):
+    for g in range(11):
+        rows = w_ref[8 * g : 8 * (g + 1), :].astype(jnp.float32)
+        for h in range(HEADS):
+            for c in range(3):
+                at = 264 * g + 88 * c
+                piece = rows[:, 704 * c + 88 * h : 704 * c + 88 * (h + 1)]
+                out_ref[h, :, at : at + 88] = piece.astype(jnp.bfloat16)
+
+
+def pack_call(w):
+    return kernel_call(pack_kernel, jax.ShapeDtypeStruct((HEADS, 8, 11 * 264), jnp.bfloat16), 1)(w)
+
+
 def unpack(y, mine_ref, theirs_ref, wide_ref):
     for half, ref in ((y, mine_ref), (1 - y, theirs_ref)):
         for j in range(8):
@@ -94,29 +108,106 @@
     return jnp.dot(weights, v, preferred_element_type=jnp.float32).astype(jnp.bfloat16)
 
 
-def spatial_kernel(y_ref, tokens_ref, mine_ref, theirs_ref, out_ref, wide_ref):
-    w = unpack(y_ref[0], mine_ref, theirs_ref, wide_ref)
-    packed = jnp.dot(normalize(tokens_ref[...]), w, preferred_element_type=jnp.float32).astype(jnp.bfloat16)
+def assemble(at_ref, same_ref, cross_ref, all_ref):
+    z, k = at_ref[1], at_ref[2]
+    for d in range(4):
+        first = 2 * (z ^ d)
+        all_ref[first + k] = same_ref[d]
+        all_ref[first + 1 - k] = cross_ref[d]
+
+
+def heads_of(all_ref):
+    parts = []
+    for r in range(4):
+        parts.append(jnp.concatenate([all_ref[h][:, 88 * r : 88 * (r + 1)] for h in range(HEADS)], axis=1))
+    return jnp.concatenate(parts, axis=0)
+
+
+def fold(rows):
+    return jnp.concatenate([rows[64 * r : 64 * (r + 1)] for r in range(4)], axis=1)
+
+
+def tokens_kernel(at_ref, same_ref, cross_ref, normed_ref, picked_ref, all_ref):
+    assemble(at_ref, same_ref, cross_ref, all_ref)
+    y, z, k = at_ref[0], at_ref[1], at_ref[2]
+    n = all_ref.shape[2]
+    row = lax.broadcasted_iota(jnp.int32, (n, 176), 0)
+    col = lax.broadcasted_iota(jnp.int32, (n, 176), 1)
+    first = 88 * (4 * z + k)
+    place = jnp.where(col < 88, first + col, first + 88 + col)
+    chosen = (row == place).astype(jnp.float32).astype(jnp.bfloat16)
+    tokens = jnp.concatenate([all_ref[j] for j in range(8)], axis=0)
+    normed_ref[...] = normalize(tokens)
+    picked_ref[...] = jnp.dot(tokens, chosen, preferred_element_type=jnp.float32).astype(jnp.bfloat16)
+
+
+def spatial_kernel(at_ref, normed_ref, mine_ref, theirs_ref, out_ref, wide_ref):
+    w = unpack(at_ref[0], mine_ref, theirs_ref, wide_ref)
+    packed = jnp.dot(normed_ref[...], w, preferred_element_type=jnp.float32).astype(jnp.bfloat16)
     n = packed.shape[0]
     row = lax.broadcasted_iota(jnp.int32, (n, n), 0) // 32
     col = lax.broadcasted_iota(jnp.int32, (n, n), 1) // 32
-    out_ref[...] = masked_attention(packed, row == col)
-
-
-def middle_kernel(y_ref, tokens_ref, spatial_ref, out_one_ref, mine_ref, theirs_ref, mixed_ref, two_ref, wide_ref):
-    w = unpack(y_ref[0], mine_ref, theirs_ref, wide_ref)
-    heads = jnp.concatenate([spatial_ref[h] for h in range(8)], axis=1)
-    update = lax.dot_general(heads, out_one_ref[...], (((1,), (1,)), ((), ())), preferred_element_type=jnp.float32)
-    mixed = (tokens_ref[...].astype(jnp.float32) + update).astype(jnp.bfloat16)
-    mixed_ref[...] = mixed
-    two_ref[...] = jnp.dot(normalize(mixed), w, preferred_element_type=jnp.float32).astype(jnp.bfloat16)
-
-
-def temporal_kernel(packed_ref, out_ref):
-    n = packed_ref.shape[0]
+    out_ref[...] = fold(masked_attention(packed, row == col))
+
+
+def columns(y, own_ref, other_ref):
+    own, other = own_ref[...], other_ref[...]
+    return jnp.concatenate([jnp.where(y == 0, own, other), jnp.where(y == 0, other, own)], axis=1)
+
+
+def mixed_kernel(at_ref, same_ref, cross_ref, picked_ref, own_ref, other_ref, keep_ref, send_ref, all_ref):
+    y = at_ref[0]
+    assemble(at_ref, same_ref, cross_ref, all_ref)
+    update = jnp.dot(heads_of(all_ref), columns(y, own_ref, other_ref), preferred_element_type=jnp.float32)
+    mixed = picked_ref[...].astype(jnp.float32) + update
+    for j in range(8):
+        low, high = mixed[32 * j : 32 * j + 16], mixed[32 * j + 16 : 32 * j + 32]
+        keep_ref[16 * j : 16 * j + 16, :] = jnp.where(y == 0, low, high).astype(jnp.bfloat16)
+        send_ref[16 * j : 16 * j + 16, :] = jnp.where(y == 0, high, low).astype(jnp.bfloat16)
+
+
+def rows_kernel(at_ref, mine_ref, theirs_ref, out_ref, wide_ref):
+    y = at_ref[0]
+    for half, ref in ((y, mine_ref), (1 - y, theirs_ref)):
+        for j in range(8):
+            slab = ref[j].astype(jnp.float32)
+            first = pl.multiple_of(176 * j + 88 * half, 8)
+            for g in range(11):
+                wide_ref[pl.ds(first + 8 * g, 8), :] = slab[:, 264 * g : 264 * (g + 1)]
+    out_ref[...] = wide_ref[...].astype(jnp.bfloat16)
+
+
+def temporal_kernel(at_ref, same_ref, cross_ref, w_ref, out_ref, all_ref):
+    assemble(at_ref, same_ref, cross_ref, all_ref)
+    own = jnp.concatenate([all_ref[j][:, :176] for j in range(8)], axis=1)
+    other = jnp.concatenate([all_ref[j][:, 176:] for j in range(8)], axis=1)
+    mixed = jnp.concatenate([own, other], axis=0)
+    packed = jnp.dot(normalize(mixed), w_ref[...], preferred_element_type=jnp.float32).astype(jnp.bfloat16)
+    n = packed.shape[0]
     row = lax.broadcasted_iota(jnp.int32, (n, n), 0) % 16
     col = lax.broadcasted_iota(jnp.int32, (n, n), 1) % 16
-    out_ref[...] = masked_attention(packed_ref[...], row == col)
+    out_ref[...] = fold(masked_attention(packed, row == col))
+
+
+def result_kernel(at_ref, same_ref, cross_ref, mixed_ref, own_ref, other_ref, out_ref, all_ref):
+    y = at_ref[0]
+    assemble(at_ref, same_ref, cross_ref, all_ref)
+    update = jnp.dot(heads_of(all_ref), columns(y, own_ref, other_ref), preferred_element_type=jnp.float32)
+    for half in range(2):
+        for j in range(8):
+            frame = 4 * (j // 2) + 2 * (y if half == 0 else 1 - y) + j % 2
+            residual = mixed_ref[16 * j : 16 * j + 16, 176 * half : 176 * (half + 1)].astype(jnp.float32)
+            at = 128 * half + 16 * j
+            out_ref[frame] = (residual + update[at : at + 16]).astype(jnp.bfloat16)
+
+
+def finish_kernel(blocks_ref, out_ref):
+    for i in range(16):
+        z, y, k = i // 4, (i // 2) % 2, i % 2
+        block = blocks_ref[i]
+        for other in range(2):
+            at = 88 * (4 * z + 2 * other + k)
+            out_ref[16 * y : 16 * y + 16, at : at + 88] = block[:, 88 * other : 88 * (other + 1)]
 
 
 VM = pl.BlockSpec(memory_space=pltpu.VMEM)
@@ -134,39 +225,52 @@
     )
 
 
+def to(mask):
+    return [(i, i ^ mask) for i in range(16)]
+
+
 def head_body(video, spatial_qkv, spatial_out, temporal_qkv, temporal_out):
     _, patches, D = video.shape
     bf = jnp.bfloat16
-    y = (lax.axis_index("seq") // 2) % 2
-    ys = y.reshape(1)
-    out_one = lax.all_gather(spatial_out.T, "seq", axis=0, tiled=True)
-    one = lax.all_to_all(pack(spatial_qkv), "seq", 0, 0, tiled=True, axis_index_groups=COLUMNS)
-    tokens = lax.all_gather(video.reshape(patches, D), "seq", axis=0, tiled=True, axis_index_groups=COLUMNS)
-    one, tokens, two_p = lax.optimization_barrier((one, tokens, pack(temporal_qkv)))
-    one_o = lax.ppermute(one, "seq", ACROSS_Y)
-    two_w = lax.all_to_all(two_p, "seq", 0, 0, tiled=True, axis_index_groups=COLUMNS)
-    wide = [pltpu.VMEM((D, 264), jnp.float32)]
-    spatial = kernel_call(spatial_kernel, jax.ShapeDtypeStruct((256, 88), bf), 3, wide, True)(ys, tokens, one, one_o)
-    spatial, two_w, t_out = lax.optimization_barrier((spatial, two_w, temporal_out.T))
-    out_two = lax.all_gather(t_out, "seq", axis=0, tiled=True)
-    two_o = lax.ppermute(two_w, "seq", ACROSS_Y)
-    spatial = lax.all_gather(spatial, "seq", axis=0, tiled=False, axis_index_groups=COLUMNS)
-    mixed, two = kernel_call(
-        middle_kernel, (jax.ShapeDtypeStruct((256, D), bf), jax.ShapeDtypeStruct((256, 264), bf)), 5, wide, True
-    )(ys, tokens, spatial, out_one, two_w, two_o)
-    two = two.reshape(8, 2, patches // 2, 264)
-    keep = jnp.where(y == 0, two[:, 0], two[:, 1])
-    send = jnp.where(y == 0, two[:, 1], two[:, 0])
-    other = lax.ppermute(send, "seq", ACROSS_Y)
-    both = jnp.where(y == 0, jnp.stack([keep, other], 1), jnp.stack([other, keep], 1))
-    both = both.reshape(4, 2, 2, patches // 2, 264).transpose(0, 2, 1, 3, 4).reshape(256, 264)
-    temporal = kernel_call(temporal_kernel, jax.ShapeDtypeStruct((256, 88), bf), 1)(both).reshape(16, patches // 2, 88)
-    temporal = lax.all_to_all(temporal, "seq", 0, 0, tiled=True)
-    temporal = temporal.reshape(4, 2, 2, patches // 2, 88).transpose(1, 3, 0, 2, 4).reshape(patches, 704)
-    me = 2 * (lax.axis_index("seq") // 4) + lax.axis_index("seq") % 2
-    own = lax.dynamic_slice_in_dim(mixed, me * patches, patches, axis=0)
-    result = own.astype(jnp.float32) + lax.dot_general(temporal, out_two, (((1,), (1,)), ((), ())), preferred_element_type=jnp.float32)
-    return result.astype(jnp.bfloat16).reshape(1, patches, D)
+    place = lax.axis_index("seq")
+    at = jnp.stack([(place // 2) % 2, place // 4, place % 2])
+    scatter = lambda a: lax.all_to_all(a, "seq", 0, 0, tiled=True, axis_index_groups=COLUMNS)
+    across = lambda a: lax.ppermute(a, "seq", ACROSS_Y)
+
+    def gather(a):
+        far, mid, near = (lax.ppermute(a, "seq", to(m)) for m in (12, 8, 4))
+        same = jnp.stack([a, near, mid, far])
+        return same, lax.ppermute(same, "seq", to(1))
+
+    def call(body, shapes, *args, scratch=()):
+        return kernel_call(body, shapes, len(args), list(scratch), True)(at, *args)
+
+    S = lambda *shape: jax.ShapeDtypeStruct(shape, bf)
+    wide = pltpu.VMEM((D, 264), jnp.float32)
+    heads = pltpu.VMEM((8, 64, 352), bf)
+
+    so, to_ = spatial_out, temporal_out
+    packed_one, frame = lax.optimization_barrier((pack_call(spatial_qkv), video.reshape(patches, D)))
+    one = scatter(packed_one)
+    tokens = gather(frame)
+    so_o, to_o = across(so), across(to_)
+    normed, picked = call(tokens_kernel, (S(256, D), S(256, 176)), *tokens, scratch=[pltpu.VMEM((8, patches, D), bf)])
+    one, so_o, to_o, normed, two_r = lax.optimization_barrier((one, so_o, to_o, normed, temporal_qkv))
+    one_o = across(one)
+    two_w = scatter(pack_call(two_r))
+    spatial = call(spatial_kernel, S(64, 352), normed, one, one_o, scratch=[wide])
+    same, cross = gather(spatial)
+    same, two_w = lax.optimization_barrier((same, two_w))
+    two_o = across(two_w)
+    keep, send = call(mixed_kernel, (S(128, 176), S(128, 176)), same, cross, picked, so, so_o, scratch=[heads])
+    mixed = jnp.concatenate([keep, across(send)], axis=1)
+    rows = call(rows_kernel, S(D, 264), two_w, two_o, scratch=[wide])
+    temporal = call(
+        temporal_kernel, S(64, 352), *gather(mixed), rows, scratch=[pltpu.VMEM((8, 128, 352), bf)]
+    )
+    result = call(result_kernel, S(16, 16, 176), *gather(temporal), mixed, to_, to_o, scratch=[heads])
+    result = lax.all_to_all(result, "seq", 0, 0, tiled=True)
+    return kernel_call(finish_kernel, S(patches, D), 1)(result).reshape(1, patches, D)
 
 
 def solution(mesh):

time: 115 us -> 93.3 us (0.81)
  blocking collectives: 39 us -> 10.5 us
  starting transfers between devices: 19.6 us -> 33.9 us
  between operations: 13.5 us -> 0.13 us
  waiting for transfers between devices: 27.3 us -> 34.6 us
  Pallas kernels: 4.91 us -> 11.9 us
  local copies, waits for them, and re-layouts: 6.85 us -> 1.33 us
  matrix products: 2.99 us -> 0 us
    all_gather x2 -> x0, blocking collectives: 39 us -> none  [the longest x1 23.2 us: head_body(): lax.all_gather(video.reshape(patches, D), 'seq', axis=0, tiled=True, axis...]
    ppermute x3 -> x21, waiting for transfers between devices: 13.1 us -> 34.6 us  [the longest x12 16.9 us: gather(): far, mid, near = (lax.ppermute(a, 'seq', to(m)) for m in (12, 8, 4))]
    ppermute x3 -> x21, starting transfers between devices: 4.65 us -> 25 us  [the longest x12 18.9 us: gather(): far, mid, near = (lax.ppermute(a, 'seq', to(m)) for m in (12, 8, 4))]
    all_to_all x3 -> x2, waiting for transfers between devices: 10.7 us -> 0.01 us  [head_body(): lax.all_to_all(a, 'seq', 0, 0, tiled=True, axis_index_groups=COLUMNS)]
    all_to_all x0 -> x1, blocking collectives: none -> 10.5 us  [head_body(): result = lax.all_to_all(result, 'seq', 0, 0, tiled=True)]
    pallas_call x3 -> x9, Pallas kernels: 4.91 us -> 11.9 us  [the longest x6 8.99 us: call(): return kernel_call(body, shapes, len(args), list(scratch), True)(at, *args)]
    all_to_all x3 -> x2, starting transfers between devices: 15 us -> 8.9 us  [head_body(): lax.all_to_all(a, 'seq', 0, 0, tiled=True, axis_index_groups=COLUMNS)]
    reshape x7 -> x0, local copies, waits for them, and re-layouts: 5.18 us -> none  [the longest x4 2.87 us: pack(): w = w.reshape(11, 8, 3, HEADS, HEAD_DIM)]
  transfers between devices with their start and end apart: 8 -> 23, of which waited for: 5 -> 14; matrix products, arithmetic and copies ran while one was open for 5% -> 1% of each run, Pallas kernels for 4% -> 6%
where the time goes in v2:
time: 93.3 us; the launch traced here: 92.9 us
  waiting for transfers between devices  34.6 us (37%)
  starting transfers between devices  33.9 us (36%)
  Pallas kernels  11.9 us (13%)
  blocking collectives  10.5 us (11%)
  local copies, waits for them, and re-layouts  1.33 us (1%)
    ppermute x12, starting transfers between devices, gather(): far, mid, near = (lax.ppermute(a, 'seq', to(m)) for m in (12, 8, 4))  18.9 us
    ppermute x12, waiting for transfers between devices, gather(): far, mid, near = (lax.ppermute(a, 'seq', to(m)) for m in (12, 8, 4))  16.9 us
    ppermute x5, waiting for transfers between devices, head_body(): across = lambda a: lax.ppermute(a, 'seq', ACROSS_Y)  14.2 us
    all_to_all x1, blocking collectives, head_body(): result = lax.all_to_all(result, 'seq', 0, 0, tiled=True)  10.5 us
    pallas_call x6, Pallas kernels, call(): return kernel_call(body, shapes, len(args), list(scratch), True)(at, *args)  8.99 us
    all_to_all x2, starting transfers between devices, head_body(): lax.all_to_all(a, 'seq', 0, 0, tiled=True, axis_index_groups=COLUMNS)  8.9 us
    ppermute x5, starting transfers between devices, head_body(): across = lambda a: lax.ppermute(a, 'seq', ACROSS_Y)  5.78 us
    ppermute x4, waiting for transfers between devices, gather(): return (same, lax.ppermute(same, 'seq', to(1)))  3.5 us
  transfers between devices with their start and end apart: 23, of which 14 were waited for; matrix products, arithmetic and copies ran while one was open for 1% of the time, Pallas kernels for 6%

profile of v2, /device:TPU:0, one launch (start us, length us, event | category | flops | bytes accessed | tf_op | source)
XLA Modules:
  0.0 92.9 jit_solution(9143835777625291364)
XLA Ops:
  0.0 1.0 %copy-done = bf16[88,2112]{1,0:T(8,128)(2,1)S(1)} copy-done((bf16[88,2112]{1,0:T(8,128)(2,1)S(1)}, bf16[88,2112]{1,0:T(8,128)(2,1)}, u32[]{:S(2)}) %copy-start) | copy-done | bytes 371736
  1.0 1.1 %shard_map.55 = bf16[8,8,2904]{2,1,0:T(8,128)(2,1)} custom-call(bf16[88,2112]{1,0:T(8,128)(2,1)S(1)} %copy-done), custom_call_target="tpu_custom_call" | custom-call | tf_op jit(solution)/shard_map/pallas_call | solution.py:88
  2.1 5.0 %collective-permute-start.4 = (bf16[32,1408]{1,0:T(8,128)(2,1)}, bf16[32,1408]{1,0:T(8,128)(2,1)S(1)}, u32[]{:S(2)}, u32[]{:S(2)}) collective-permute-start(bf16[32,1408]{1,0:T(8,128)(2,1)} %bitcast.27), channel_id=1, source_target_pairs={{0,12},{1,13},{2,14},{3,15},{4,8},{5,9},{6,10},{7,11},{8,4},{9,5},... | collective-permute-start | bytes 270344 | tf_op jit(solution)/shard_map/ppermute | solution.py:241
  7.1 0.0 collective-permute-start.3
  7.1 0.6 collective-permute-start.2
  7.7 5.1 %all-to-all-start = ((bf16[8,8,2904]{2,1,0:T(8,128)(2,1)}), bf16[8,8,2904]{2,1,0:T(8,128)(2,1)S(1)}, u32[]{:S(2)}, u32[]{:S(2)}) async-start(bf16[8,8,2904]{2,1,0:T(8,128)(2,1)} %shard_map.55), calls=%async_computation | async-start | bytes 753664 | tf_op jit(solution)/shard_map/all_to_all | solution.py:237
  12.8 0.0 collective-permute-done.4
  12.8 2.1 %collective-permute-done.3 = bf16[32,1408]{1,0:T(8,128)(2,1)S(1)} collective-permute-done((bf16[32,1408]{1,0:T(8,128)(2,1)}, bf16[32,1408]{1,0:T(8,128)(2,1)S(1)}, u32[]{:S(2)}, u32[]{:S(2)}) %collective-permute-start.3) | collective-permute-done | bytes 90144 | tf_op jit(solution)/shard_map/ppermute | solution.py:241
  14.9 0.0 collective-permute-done.2
  14.9 0.1 pad_maximum_fusion.1.same_ref
  15.0 0.1 collective-permute-start.5
  15.1 0.2 copy.7.own_ref
  15.2 1.6 %collective-permute-start.1 = (bf16[704,88]{1,0:T(8,128)(2,1)S(1)}, bf16[704,88]{1,0:T(8,128)(2,1)S(1)}, u32[]{:S(2)}, u32[]{:S(2)}) collective-permute-start(bf16[704,88]{1,0:T(8,128)(2,1)S(1)} %copy.7.own_ref), channel_id=1, source_target_pairs={{0,2},{1,3},{2,0},{3,1},{4,6},{5,7},{6,4},{7,5},{8,10},{9,11},{10,... | collective-permute-start | bytes 371720 | tf_op jit(solution)/shard_map/ppermute | solution.py:238
  16.8 0.2 copy.6.own_ref
  17.0 0.6 collective-permute-start
  17.6 0.1 pad_add_fusion.at_ref
  17.6 0.0 collective-permute-done.5.cross_ref
  17.6 1.2 %shard_map.56 = (bf16[256,1408]{1,0:T(8,128)(2,1)S(1)}, bf16[256,176]{1,0:T(8,128)(2,1)S(1)}) custom-call(s32[3]{0:T(128)S(1)} %pad_add_fusion.at_ref, bf16[4,32,1408]{2,1,0:T(8,128)(2,1)S(1)} %pad_maximum_fusion.1.same_ref, bf16[4,32,1408]{2,1,0:T(8,128)(2,1)S(1)} %collective-permute-done.5.cross_ref), custom_call_target="tpu_custom_call" | custom-call | tf_op jit(solution)/shard_map/pallas_call | solution.py:246
  18.8 3.8 %collective-permute-done.1.other_ref = bf16[704,88]{1,0:T(8,128)(2,1)S(1)} collective-permute-done((bf16[704,88]{1,0:T(8,128)(2,1)S(1)}, bf16[704,88]{1,0:T(8,128)(2,1)S(1)}, u32[]{:S(2)}, u32[]{:S(2)}) %collective-permute-start.1) | collective-permute-done | bytes 123936 | tf_op jit(solution)/shard_map/ppermute | solution.py:238
  22.6 3.5 %collective-permute-done.other_ref = bf16[704,88]{1,0:T(8,128)(2,1)S(1)} collective-permute-done((bf16[704,88]{1,0:T(8,128)(2,1)S(1)}, bf16[704,88]{1,0:T(8,128)(2,1)S(1)}, u32[]{:S(2)}, u32[]{:S(2)}) %collective-permute-start) | collective-permute-done | bytes 123936 | tf_op jit(solution)/shard_map/ppermute | solution.py:238
  26.1 0.0 all-to-all-done.mine_ref
  26.1 1.5 %collective-permute-start.6 = (bf16[8,8,2904]{2,1,0:T(8,128)(2,1)S(1)}, bf16[8,8,2904]{2,1,0:T(8,128)(2,1)S(1)}, u32[]{:S(2)}, u32[]{:S(2)}) collective-permute-start(bf16[8,8,2904]{2,1,0:T(8,128)(2,1)S(1)} %all-to-all-done.mine_ref), channel_id=1, source_target_pairs={{0,2},{1,3},{2,0},{3,1},{4,6},{5,7},{6,4},{7,5},{8,10},{9,11},{10,... | collective-permute-start | bytes 1115144 | tf_op jit(solution)/shard_map/ppermute | solution.py:238
  27.6 1.1 %shard_map.58 = bf16[8,8,2904]{2,1,0:T(8,128)(2,1)} custom-call(bf16[88,2112]{1,0:T(8,128)(2,1)S(1)} %copy-done.1), custom_call_target="tpu_custom_call" | custom-call | tf_op jit(solution)/shard_map/pallas_call | solution.py:88
  28.7 3.8 %all-to-all-start.1 = ((bf16[8,8,2904]{2,1,0:T(8,128)(2,1)}), bf16[8,8,2904]{2,1,0:T(8,128)(2,1)S(1)}, u32[]{:S(2)}, u32[]{:S(2)}) async-start(bf16[8,8,2904]{2,1,0:T(8,128)(2,1)} %shard_map.58), calls=%async_computation.1 | async-start | bytes 753664 | tf_op jit(solution)/shard_map/all_to_all | solution.py:237
  32.5 4.0 %collective-permute-done.6.theirs_ref = bf16[8,8,2904]{2,1,0:T(8,128)(2,1)S(1)} collective-permute-done((bf16[8,8,2904]{2,1,0:T(8,128)(2,1)S(1)}, bf16[8,8,2904]{2,1,0:T(8,128)(2,1)S(1)}, u32[]{:S(2)}, u32[]{:S(2)}) %collective-permute-start.6) | collective-permute-done | bytes 371744 | tf_op jit(solution)/shard_map/ppermute | solution.py:238
  36.5 2.1 %shard_map.57 = bf16[64,352]{1,0:T(8,128)(2,1)S(1)} custom-call(s32[3]{0:T(128)S(1)} %pad_add_fusion.at_ref, bf16[256,1408]{1,0:T(8,128)(2,1)S(1)} %get-tuple-element.21.normed_ref, bf16[8,8,2904]{2,1,0:T(8,128)(2,1)S(1)} %all-to-all-done.mine_ref, bf16[8,8,2904]{2,1,0:T(8,128)(2,1)S(1)} %collective-permute-done.6.theirs_ref), custom_call_target="tpu_custom_call" | custom-call | tf_op jit(solution)/shard_map/pallas_call | solution.py:246
  38.6 2.6 %collective-permute-start.9 = (bf16[64,352]{1,0:T(8,128)(2,1)S(1)}, bf16[64,352]{1,0:T(8,128)(2,1)S(1)}, u32[]{:S(2)}, u32[]{:S(2)}) collective-permute-start(bf16[64,352]{1,0:T(8,128)(2,1)S(1)} %shard_map.57), channel_id=1, source_target_pairs={{0,12},{1,13},{2,14},{3,15},{4,8},{5,9},{6,10},{7,11},{8,4},{9,5},... | collective-permute-start | bytes 135176 | tf_op jit(solution)/shard_map/ppermute | solution.py:241
  41.1 0.0 collective-permute-start.8
  41.1 1.9 %collective-permute-start.7 = (bf16[64,352]{1,0:T(8,128)(2,1)S(1)}, bf16[64,352]{1,0:T(8,128)(2,1)S(1)}, u32[]{:S(2)}, u32[]{:S(2)}) collective-permute-start(bf16[64,352]{1,0:T(8,128)(2,1)S(1)} %shard_map.57), channel_id=1, source_target_pairs={{0,4},{1,5},{2,6},{3,7},{4,0},{5,1},{6,2},{7,3},{8,12},{9,13},{10,... | collective-permute-start | bytes 135176 | tf_op jit(solution)/shard_map/ppermute | solution.py:241
  43.0 2.3 %collective-permute-done.9 = bf16[64,352]{1,0:T(8,128)(2,1)S(1)} collective-permute-done((bf16[64,352]{1,0:T(8,128)(2,1)S(1)}, bf16[64,352]{1,0:T(8,128)(2,1)S(1)}, u32[]{:S(2)}, u32[]{:S(2)}) %collective-permute-start.9) | collective-permute-done | bytes 45088 | tf_op jit(solution)/shard_map/ppermute | solution.py:241
  45.3 3.7 %collective-permute-done.8 = bf16[64,352]{1,0:T(8,128)(2,1)S(1)} collective-permute-done((bf16[64,352]{1,0:T(8,128)(2,1)S(1)}, bf16[64,352]{1,0:T(8,128)(2,1)S(1)}, u32[]{:S(2)}, u32[]{:S(2)}) %collective-permute-start.8) | collective-permute-done | bytes 45088 | tf_op jit(solution)/shard_map/ppermute | solution.py:241
  48.9 0.0 collective-permute-done.7
  49.0 0.1 collective-permute-start.10
  49.1 0.0 all-to-all-done.1.mine_ref
  49.1 1.4 %collective-permute-done.10.cross_ref = bf16[4,64,352]{2,1,0:T(8,128)(2,1)S(1)} collective-permute-done((bf16[4,64,352]{2,1,0:T(8,128)(2,1)S(1)}, bf16[4,64,352]{2,1,0:T(8,128)(2,1)S(1)}, u32[]{:S(2)}, u32[]{:S(2)}) %collective-permute-start.10) | collective-permute-done | bytes 180256 | tf_op jit(solution)/shard_map/ppermute | solution.py:243
  50.5 1.0 %shard_map.59 = (bf16[128,176]{1,0:T(8,128)(2,1)S(1)}, bf16[128,176]{1,0:T(8,128)(2,1)S(1)}) custom-call(s32[3]{0:T(128)S(1)} %pad_add_fusion.at_ref, bf16[4,64,352]{2,1,0:T(8,128)(2,1)S(1)} %pad_maximum_fusion.2.same_ref, bf16[4,64,352]{2,1,0:T(8,128)(2,1)S(1)} %collective-permute-done.10.cross_ref, bf16[256,176]{1,0:T(8,128)(2,1)S(1)} %get-tuple-element.25.picked_ref, ...), custom_call_target="tpu_custom_call" | custom-call | tf_op jit(solution)/shard_map/pallas_call | solution.py:246
  51.5 0.6 collective-permute-start.11
  52.1 1.5 %collective-permute-start.16 = (bf16[8,8,2904]{2,1,0:T(8,128)(2,1)S(1)}, bf16[8,8,2904]{2,1,0:T(8,128)(2,1)S(1)}, u32[]{:S(2)}, u32[]{:S(2)}) collective-permute-start(bf16[8,8,2904]{2,1,0:T(8,128)(2,1)S(1)} %all-to-all-done.1.mine_ref), channel_id=1, source_target_pairs={{0,2},{1,3},{2,0},{3,1},{4,6},{5,7},{6,4},{7,5},{8,10},{9,11},{10,... | collective-permute-start | bytes 1115144 | tf_op jit(solution)/shard_map/ppermute | solution.py:238
  53.6 2.9 %collective-permute-done.11 = bf16[128,176]{1,0:T(8,128)(2,1)S(1)} collective-permute-done((bf16[128,176]{1,0:T(8,128)(2,1)S(1)}, bf16[128,176]{1,0:T(8,128)(2,1)S(1)}, u32[]{:S(2)}, u32[]{:S(2)}) %collective-permute-start.11) | collective-permute-done | bytes 45088 | tf_op jit(solution)/shard_map/ppermute | solution.py:238
  56.5 0.1 pad_maximum_fusion.4.mixed_ref
  56.6 1.3 %collective-permute-start.14 = (bf16[128,352]{1,0:T(8,128)(2,1)S(1)}, bf16[128,352]{1,0:T(8,128)(2,1)S(1)}, u32[]{:S(2)}, u32[]{:S(2)}) collective-permute-start(bf16[128,352]{1,0:T(8,128)(2,1)S(1)} %pad_maximum_fusion.4.mixed_ref), channel_id=1, source_target_pairs={{0,12},{1,13},{2,14},{3,15},{4,8},{5,9},{6,10},{7,11},{8,4},{9,5},... | collective-permute-start | bytes 270344 | tf_op jit(solution)/shard_map/ppermute | solution.py:241
  58.0 0.2 collective-permute-start.13
  58.1 2.9 %collective-permute-start.12 = (bf16[128,352]{1,0:T(8,128)(2,1)S(1)}, bf16[128,352]{1,0:T(8,128)(2,1)S(1)}, u32[]{:S(2)}, u32[]{:S(2)}) collective-permute-start(bf16[128,352]{1,0:T(8,128)(2,1)S(1)} %pad_maximum_fusion.4.mixed_ref), channel_id=1, source_target_pairs={{0,4},{1,5},{2,6},{3,7},{4,0},{5,1},{6,2},{7,3},{8,12},{9,13},{10,... | collective-permute-start | bytes 270344 | tf_op jit(solution)/shard_map/ppermute | solution.py:241
  61.1 0.1 fusion
  61.2 2.6 %collective-permute-done.14 = bf16[128,352]{1,0:T(8,128)(2,1)S(1)} collective-permute-done((bf16[128,352]{1,0:T(8,128)(2,1)S(1)}, bf16[128,352]{1,0:T(8,128)(2,1)S(1)}, u32[]{:S(2)}, u32[]{:S(2)}) %collective-permute-start.14) | collective-permute-done | bytes 90144 | tf_op jit(solution)/shard_map/ppermute | solution.py:241
  63.8 3.0 %collective-permute-done.13 = bf16[128,352]{1,0:T(8,128)(2,1)S(1)} collective-permute-done((bf16[128,352]{1,0:T(8,128)(2,1)S(1)}, bf16[128,352]{1,0:T(8,128)(2,1)S(1)}, u32[]{:S(2)}, u32[]{:S(2)}) %collective-permute-start.13) | collective-permute-done | bytes 90144 | tf_op jit(solution)/shard_map/ppermute | solution.py:241
  66.8 0.0 collective-permute-done.12
  66.8 0.1 pad_maximum_fusion.same_ref
  66.9 0.1 collective-permute-start.15
  66.9 0.0 collective-permute-done.16.theirs_ref
  66.9 1.0 %shard_map.60.w_ref = bf16[1408,264]{1,0:T(8,128)(2,1)S(1)} custom-call(s32[3]{0:T(128)S(1)} %pad_add_fusion.at_ref, bf16[8,8,2904]{2,1,0:T(8,128)(2,1)S(1)} %all-to-all-done.1.mine_ref, bf16[8,8,2904]{2,1,0:T(8,128)(2,1)S(1)} %collective-permute-done.16.theirs_ref), custom_call_target="tpu_custom_call" | custom-call | tf_op jit(solution)/shard_map/pallas_call | solution.py:246
  68.0 0.7 collective-permute-done.15.cross_ref
  68.6 2.5 %shard_map.61 = bf16[64,352]{1,0:T(8,128)(2,1)S(1)} custom-call(s32[3]{0:T(128)S(1)} %pad_add_fusion.at_ref, bf16[4,128,352]{2,1,0:T(8,128)(2,1)S(1)} %pad_maximum_fusion.same_ref, bf16[4,128,352]{2,1,0:T(8,128)(2,1)S(1)} %collective-permute-done.15.cross_ref, bf16[1408,264]{1,0:T(8,128)(2,1)S(1)} %shard_map.60.w_ref), custom_call_target="tpu_custom_call" | custom-call | tf_op jit(solution)/shard_map/pallas_call | solution.py:246
  71.2 1.3 %collective-permute-start.19 = (bf16[64,352]{1,0:T(8,128)(2,1)S(1)}, bf16[64,352]{1,0:T(8,128)(2,1)S(1)}, u32[]{:S(2)}, u32[]{:S(2)}) collective-permute-start(bf16[64,352]{1,0:T(8,128)(2,1)S(1)} %shard_map.61), channel_id=1, source_target_pairs={{0,12},{1,13},{2,14},{3,15},{4,8},{5,9},{6,10},{7,11},{8,4},{9,5},... | collective-permute-start | bytes 135176 | tf_op jit(solution)/shard_map/ppermute | solution.py:241
  72.4 3.1 %collective-permute-start.17 = (bf16[64,352]{1,0:T(8,128)(2,1)S(1)}, bf16[64,352]{1,0:T(8,128)(2,1)S(1)}, u32[]{:S(2)}, u32[]{:S(2)}) collective-permute-start(bf16[64,352]{1,0:T(8,128)(2,1)S(1)} %shard_map.61), channel_id=1, source_target_pairs={{0,4},{1,5},{2,6},{3,7},{4,0},{5,1},{6,2},{7,3},{8,12},{9,13},{10,... | collective-permute-start | bytes 135176 | tf_op jit(solution)/shard_map/ppermute | solution.py:241
  75.6 2.0 %collective-permute-done.19 = bf16[64,352]{1,0:T(8,128)(2,1)S(1)} collective-permute-done((bf16[64,352]{1,0:T(8,128)(2,1)S(1)}, bf16[64,352]{1,0:T(8,128)(2,1)S(1)}, u32[]{:S(2)}, u32[]{:S(2)}) %collective-permute-start.19) | collective-permute-done | bytes 45088 | tf_op jit(solution)/shard_map/ppermute | solution.py:241
  77.6 1.3 %collective-permute-done.18 = bf16[64,352]{1,0:T(8,128)(2,1)S(1)} collective-permute-done((bf16[64,352]{1,0:T(8,128)(2,1)S(1)}, bf16[64,352]{1,0:T(8,128)(2,1)S(1)}, u32[]{:S(2)}, u32[]{:S(2)}) %collective-permute-start.18) | collective-permute-done | bytes 45088 | tf_op jit(solution)/shard_map/ppermute | solution.py:241
  78.9 0.0 collective-permute-done.17
  78.9 0.1 pad_maximum_fusion.3.same_ref
  78.9 0.1 collective-permute-start.20
  79.0 1.4 %collective-permute-done.20.cross_ref = bf16[4,64,352]{2,1,0:T(8,128)(2,1)S(1)} collective-permute-done((bf16[4,64,352]{2,1,0:T(8,128)(2,1)S(1)}, bf16[4,64,352]{2,1,0:T(8,128)(2,1)S(1)}, u32[]{:S(2)}, u32[]{:S(2)}) %collective-permute-start.20) | collective-permute-done | bytes 180256 | tf_op jit(solution)/shard_map/ppermute | solution.py:243
  80.5 1.1 %shard_map.62 = bf16[16,16,176]{2,1,0:T(8,128)(2,1)S(1)} custom-call(s32[3]{0:T(128)S(1)} %pad_add_fusion.at_ref, bf16[4,64,352]{2,1,0:T(8,128)(2,1)S(1)} %pad_maximum_fusion.3.same_ref, bf16[4,64,352]{2,1,0:T(8,128)(2,1)S(1)} %collective-permute-done.20.cross_ref, bf16[128,352]{1,0:T(8,128)(2,1)S(1)} %pad_maximum_fusion.4.mixed_ref, ...), custom_call_target="tpu_custom_call" | custom-call | tf_op jit(solution)/shard_map/pallas_call | solution.py:246
  81.6 10.5 %all_to_all.15.blocks_ref = bf16[16,16,176]{2,1,0:T(8,128)(2,1)S(1)} all-to-all(bf16[16,16,176]{2,1,0:T(8,128)(2,1)S(1)} %shard_map.62), channel_id=1, replica_groups=mesh['groups'=2,'seq'=16] {'seq'}, dimensions={0} | all-to-all | bytes 180224 | tf_op jit(solution)/shard_map/all_to_all | solution.py:272
  92.1 0.8 shard_map.63
  (11 shorter events, 0.1 us)
Async XLA Ops:
  0.0 1.0 %copy-start = (bf16[88,2112]{1,0:T(8,128)(2,1)S(1)}, bf16[88,2112]{1,0:T(8,128)(2,1)}, u32[]{:S(2)}) copy-start(bf16[88,2112]{1,0:T(8,128)(2,1)} %w_ref.1) | copy-start | bytes 1115140
  1.0 13.9 %copy-start.4 = (bf16[1,32,1408]{2,1,0:T(8,128)(2,1)S(1)}, bf16[1,32,1408]{2,1,0:T(8,128)(2,1)}, u32[]{:S(2)}) copy-start(bf16[1,32,1408]{2,1,0:T(8,128)(2,1)} %param.5) | copy-start | bytes 270340
  1.0 14.1 %copy-start.2 = (bf16[704,88]{0,1:T(8,128)(2,1)S(1)}, bf16[704,88]{0,1:T(8,128)(2,1)}, u32[]{:S(2)}) copy-start(bf16[704,88]{0,1:T(8,128)(2,1)} %param.9) | copy-start | bytes 371716
  2.1 14.7 %copy-start.3 = (bf16[704,88]{0,1:T(8,128)(2,1)S(1)}, bf16[704,88]{0,1:T(8,128)(2,1)}, u32[]{:S(2)}) copy-start(bf16[704,88]{0,1:T(8,128)(2,1)} %param.7) | copy-start | bytes 371716
  2.1 10.7 %collective-permute-start.4 = (bf16[32,1408]{1,0:T(8,128)(2,1)}, bf16[32,1408]{1,0:T(8,128)(2,1)S(1)}, u32[]{:S(2)}, u32[]{:S(2)}) collective-permute-start(bf16[32,1408]{1,0:T(8,128)(2,1)} %bitcast.27), channel_id=1, source_target_pairs={{0,12},{1,13},{2,14},{3,15},{4,8},{5,9},{6,10},{7,11},{8,4},{9,5},... | collective-permute-start | bytes 270344 | tf_op jit(solution)/shard_map/ppermute | solution.py:241
  7.1 7.8 %collective-permute-start.3 = (bf16[32,1408]{1,0:T(8,128)(2,1)}, bf16[32,1408]{1,0:T(8,128)(2,1)S(1)}, u32[]{:S(2)}, u32[]{:S(2)}) collective-permute-start(bf16[32,1408]{1,0:T(8,128)(2,1)} %bitcast.28), channel_id=1, source_target_pairs={{0,8},{1,9},{2,10},{3,11},{4,12},{5,13},{6,14},{7,15},{8,0},{9,1},... | collective-permute-start | bytes 270344 | tf_op jit(solution)/shard_map/ppermute | solution.py:241
  7.1 7.8 %collective-permute-start.2 = (bf16[32,1408]{1,0:T(8,128)(2,1)}, bf16[32,1408]{1,0:T(8,128)(2,1)S(1)}, u32[]{:S(2)}, u32[]{:S(2)}) collective-permute-start(bf16[32,1408]{1,0:T(8,128)(2,1)} %bitcast.29), channel_id=1, source_target_pairs={{0,4},{1,5},{2,6},{3,7},{4,0},{5,1},{6,2},{7,3},{8,12},{9,13},{10,... | collective-permute-start | bytes 270344 | tf_op jit(solution)/shard_map/ppermute | solution.py:241
  7.7 18.4 %all-to-all-start = ((bf16[8,8,2904]{2,1,0:T(8,128)(2,1)}), bf16[8,8,2904]{2,1,0:T(8,128)(2,1)S(1)}, u32[]{:S(2)}, u32[]{:S(2)}) async-start(bf16[8,8,2904]{2,1,0:T(8,128)(2,1)} %shard_map.55), calls=%async_computation | async-start | bytes 753664 | tf_op jit(solution)/shard_map/all_to_all | solution.py:237
  14.9 12.7 %copy-start.1 = (bf16[88,2112]{1,0:T(8,128)(2,1)S(1)}, bf16[88,2112]{1,0:T(8,128)(2,1)}, u32[]{:S(2)}) copy-start(bf16[88,2112]{1,0:T(8,128)(2,1)} %w_ref.2) | copy-start | bytes 1115140
  15.0 2.6 %collective-permute-start.5 = (bf16[4,32,1408]{2,1,0:T(8,128)(2,1)S(1)}, bf16[4,32,1408]{2,1,0:T(8,128)(2,1)S(1)}, u32[]{:S(2)}, u32[]{:S(2)}) collective-permute-start(bf16[4,32,1408]{2,1,0:T(8,128)(2,1)S(1)} %pad_maximum_fusion.1.same_ref), channel_id=1, source_target_pairs={{0,1},{1,0},{2,3},{3,2},{4,5},{5,4},{6,7},{7,6},{8,9},{9,8},{10,11... | collective-permute-start | bytes 1081352 | tf_op jit(solution)/shard_map/ppermute | solution.py:243
  15.2 7.4 %collective-permute-start.1 = (bf16[704,88]{1,0:T(8,128)(2,1)S(1)}, bf16[704,88]{1,0:T(8,128)(2,1)S(1)}, u32[]{:S(2)}, u32[]{:S(2)}) collective-permute-start(bf16[704,88]{1,0:T(8,128)(2,1)S(1)} %copy.7.own_ref), channel_id=1, source_target_pairs={{0,2},{1,3},{2,0},{3,1},{4,6},{5,7},{6,4},{7,5},{8,10},{9,11},{10,... | collective-permute-start | bytes 371720 | tf_op jit(solution)/shard_map/ppermute | solution.py:238
  17.0 9.1 %collective-permute-start = (bf16[704,88]{1,0:T(8,128)(2,1)S(1)}, bf16[704,88]{1,0:T(8,128)(2,1)S(1)}, u32[]{:S(2)}, u32[]{:S(2)}) collective-permute-start(bf16[704,88]{1,0:T(8,128)(2,1)S(1)} %copy.6.own_ref), channel_id=1, source_target_pairs={{0,2},{1,3},{2,0},{3,1},{4,6},{5,7},{6,4},{7,5},{8,10},{9,11},{10,... | collective-permute-start | bytes 371720 | tf_op jit(solution)/shard_map/ppermute | solution.py:238
  26.1 10.4 %collective-permute-start.6 = (bf16[8,8,2904]{2,1,0:T(8,128)(2,1)S(1)}, bf16[8,8,2904]{2,1,0:T(8,128)(2,1)S(1)}, u32[]{:S(2)}, u32[]{:S(2)}) collective-permute-start(bf16[8,8,2904]{2,1,0:T(8,128)(2,1)S(1)} %all-to-all-done.mine_ref), channel_id=1, source_target_pairs={{0,2},{1,3},{2,0},{3,1},{4,6},{5,7},{6,4},{7,5},{8,10},{9,11},{10,... | collective-permute-start | bytes 1115144 | tf_op jit(solution)/shard_map/ppermute | solution.py:238
  28.7 20.4 %all-to-all-start.1 = ((bf16[8,8,2904]{2,1,0:T(8,128)(2,1)}), bf16[8,8,2904]{2,1,0:T(8,128)(2,1)S(1)}, u32[]{:S(2)}, u32[]{:S(2)}) async-start(bf16[8,8,2904]{2,1,0:T(8,128)(2,1)} %shard_map.58), calls=%async_computation.1 | async-start | bytes 753664 | tf_op jit(solution)/shard_map/all_to_all | solution.py:237
  38.6 6.7 %collective-permute-start.9 = (bf16[64,352]{1,0:T(8,128)(2,1)S(1)}, bf16[64,352]{1,0:T(8,128)(2,1)S(1)}, u32[]{:S(2)}, u32[]{:S(2)}) collective-permute-start(bf16[64,352]{1,0:T(8,128)(2,1)S(1)} %shard_map.57), channel_id=1, source_target_pairs={{0,12},{1,13},{2,14},{3,15},{4,8},{5,9},{6,10},{7,11},{8,4},{9,5},... | collective-permute-start | bytes 135176 | tf_op jit(solution)/shard_map/ppermute | solution.py:241
  41.1 7.8 %collective-permute-start.8 = (bf16[64,352]{1,0:T(8,128)(2,1)S(1)}, bf16[64,352]{1,0:T(8,128)(2,1)S(1)}, u32[]{:S(2)}, u32[]{:S(2)}) collective-permute-start(bf16[64,352]{1,0:T(8,128)(2,1)S(1)} %shard_map.57), channel_id=1, source_target_pairs={{0,8},{1,9},{2,10},{3,11},{4,12},{5,13},{6,14},{7,15},{8,0},{9,1},... | collective-permute-start | bytes 135176 | tf_op jit(solution)/shard_map/ppermute | solution.py:241
  41.1 7.8 %collective-permute-start.7 = (bf16[64,352]{1,0:T(8,128)(2,1)S(1)}, bf16[64,352]{1,0:T(8,128)(2,1)S(1)}, u32[]{:S(2)}, u32[]{:S(2)}) collective-permute-start(bf16[64,352]{1,0:T(8,128)(2,1)S(1)} %shard_map.57), channel_id=1, source_target_pairs={{0,4},{1,5},{2,6},{3,7},{4,0},{5,1},{6,2},{7,3},{8,12},{9,13},{10,... | collective-permute-start | bytes 135176 | tf_op jit(solution)/shard_map/ppermute | solution.py:241
  49.0 1.5 %collective-permute-start.10 = (bf16[4,64,352]{2,1,0:T(8,128)(2,1)S(1)}, bf16[4,64,352]{2,1,0:T(8,128)(2,1)S(1)}, u32[]{:S(2)}, u32[]{:S(2)}) collective-permute-start(bf16[4,64,352]{2,1,0:T(8,128)(2,1)S(1)} %pad_maximum_fusion.2.same_ref), channel_id=1, source_target_pairs={{0,1},{1,0},{2,3},{3,2},{4,5},{5,4},{6,7},{7,6},{8,9},{9,8},{10,11... | collective-permute-start | bytes 540680 | tf_op jit(solution)/shard_map/ppermute | solution.py:243
  51.5 5.0 %collective-permute-start.11 = (bf16[128,176]{1,0:T(8,128)(2,1)S(1)}, bf16[128,176]{1,0:T(8,128)(2,1)S(1)}, u32[]{:S(2)}, u32[]{:S(2)}) collective-permute-start(bf16[128,176]{1,0:T(8,128)(2,1)S(1)} %get-tuple-element.28), channel_id=1, source_target_pairs={{0,2},{1,3},{2,0},{3,1},{4,6},{5,7},{6,4},{7,5},{8,10},{9,11},{10,... | collective-permute-start | bytes 135176 | tf_op jit(solution)/shard_map/ppermute | solution.py:238
  52.1 14.9 %collective-permute-start.16 = (bf16[8,8,2904]{2,1,0:T(8,128)(2,1)S(1)}, bf16[8,8,2904]{2,1,0:T(8,128)(2,1)S(1)}, u32[]{:S(2)}, u32[]{:S(2)}) collective-permute-start(bf16[8,8,2904]{2,1,0:T(8,128)(2,1)S(1)} %all-to-all-done.1.mine_ref), channel_id=1, source_target_pairs={{0,2},{1,3},{2,0},{3,1},{4,6},{5,7},{6,4},{7,5},{8,10},{9,11},{10,... | collective-permute-start | bytes 1115144 | tf_op jit(solution)/shard_map/ppermute | solution.py:238
  56.6 7.2 %collective-permute-start.14 = (bf16[128,352]{1,0:T(8,128)(2,1)S(1)}, bf16[128,352]{1,0:T(8,128)(2,1)S(1)}, u32[]{:S(2)}, u32[]{:S(2)}) collective-permute-start(bf16[128,352]{1,0:T(8,128)(2,1)S(1)} %pad_maximum_fusion.4.mixed_ref), channel_id=1, source_target_pairs={{0,12},{1,13},{2,14},{3,15},{4,8},{5,9},{6,10},{7,11},{8,4},{9,5},... | collective-permute-start | bytes 270344 | tf_op jit(solution)/shard_map/ppermute | solution.py:241
  58.0 8.8 %collective-permute-start.13 = (bf16[128,352]{1,0:T(8,128)(2,1)S(1)}, bf16[128,352]{1,0:T(8,128)(2,1)S(1)}, u32[]{:S(2)}, u32[]{:S(2)}) collective-permute-start(bf16[128,352]{1,0:T(8,128)(2,1)S(1)} %pad_maximum_fusion.4.mixed_ref), channel_id=1, source_target_pairs={{0,8},{1,9},{2,10},{3,11},{4,12},{5,13},{6,14},{7,15},{8,0},{9,1},... | collective-permute-start | bytes 270344 | tf_op jit(solution)/shard_map/ppermute | solution.py:241
  58.1 8.6 %collective-permute-start.12 = (bf16[128,352]{1,0:T(8,128)(2,1)S(1)}, bf16[128,352]{1,0:T(8,128)(2,1)S(1)}, u32[]{:S(2)}, u32[]{:S(2)}) collective-permute-start(bf16[128,352]{1,0:T(8,128)(2,1)S(1)} %pad_maximum_fusion.4.mixed_ref), channel_id=1, source_target_pairs={{0,4},{1,5},{2,6},{3,7},{4,0},{5,1},{6,2},{7,3},{8,12},{9,13},{10,... | collective-permute-start | bytes 270344 | tf_op jit(solution)/shard_map/ppermute | solution.py:241
  66.9 1.8 %collective-permute-start.15 = (bf16[4,128,352]{2,1,0:T(8,128)(2,1)S(1)}, bf16[4,128,352]{2,1,0:T(8,128)(2,1)S(1)}, u32[]{:S(2)}, u32[]{:S(2)}) collective-permute-start(bf16[4,128,352]{2,1,0:T(8,128)(2,1)S(1)} %pad_maximum_fusion.same_ref), channel_id=1, source_target_pairs={{0,1},{1,0},{2,3},{3,2},{4,5},{5,4},{6,7},{7,6},{8,9},{9,8},{10,11... | collective-permute-start | bytes 1081352 | tf_op jit(solution)/shard_map/ppermute | solution.py:243
  71.2 6.5 %collective-permute-start.19 = (bf16[64,352]{1,0:T(8,128)(2,1)S(1)}, bf16[64,352]{1,0:T(8,128)(2,1)S(1)}, u32[]{:S(2)}, u32[]{:S(2)}) collective-permute-start(bf16[64,352]{1,0:T(8,128)(2,1)S(1)} %shard_map.61), channel_id=1, source_target_pairs={{0,12},{1,13},{2,14},{3,15},{4,8},{5,9},{6,10},{7,11},{8,4},{9,5},... | collective-permute-start | bytes 135176 | tf_op jit(solution)/shard_map/ppermute | solution.py:241
  72.4 6.4 %collective-permute-start.18 = (bf16[64,352]{1,0:T(8,128)(2,1)S(1)}, bf16[64,352]{1,0:T(8,128)(2,1)S(1)}, u32[]{:S(2)}, u32[]{:S(2)}) collective-permute-start(bf16[64,352]{1,0:T(8,128)(2,1)S(1)} %shard_map.61), channel_id=1, source_target_pairs={{0,8},{1,9},{2,10},{3,11},{4,12},{5,13},{6,14},{7,15},{8,0},{9,1},... | collective-permute-start | bytes 135176 | tf_op jit(solution)/shard_map/ppermute | solution.py:241
  72.4 6.4 %collective-permute-start.17 = (bf16[64,352]{1,0:T(8,128)(2,1)S(1)}, bf16[64,352]{1,0:T(8,128)(2,1)S(1)}, u32[]{:S(2)}, u32[]{:S(2)}) collective-permute-start(bf16[64,352]{1,0:T(8,128)(2,1)S(1)} %shard_map.61), channel_id=1, source_target_pairs={{0,4},{1,5},{2,6},{3,7},{4,0},{5,1},{6,2},{7,3},{8,12},{9,13},{10,... | collective-permute-start | bytes 135176 | tf_op jit(solution)/shard_map/ppermute | solution.py:241
  78.9 1.5 %collective-permute-start.20 = (bf16[4,64,352]{2,1,0:T(8,128)(2,1)S(1)}, bf16[4,64,352]{2,1,0:T(8,128)(2,1)S(1)}, u32[]{:S(2)}, u32[]{:S(2)}) collective-permute-start(bf16[4,64,352]{2,1,0:T(8,128)(2,1)S(1)} %pad_maximum_fusion.3.same_ref), channel_id=1, source_target_pairs={{0,1},{1,0},{2,3},{3,2},{4,5},{5,4},{6,7},{7,6},{8,9},{9,8},{10,11... | collective-permute-start | bytes 540680 | tf_op jit(solution)/shard_map/ppermute | solution.py:243

commit v3 on v2

--- a/solution.py
+++ b/solution.py
@@ -84,17 +84,30 @@
                 out_ref[h, :, at : at + 88] = piece.astype(jnp.bfloat16)
 
 
+def pack_near_kernel(at_ref, w_ref, own_ref, near_ref, mid_ref, far_ref, all_ref):
+    z, k = at_ref[1], at_ref[2]
+    for g in range(11):
+        rows = w_ref[8 * g : 8 * (g + 1), :].astype(jnp.float32)
+        for h in range(HEADS):
+            for c in range(3):
+                at = 264 * g + 88 * c
+                piece = rows[:, 704 * c + 88 * h : 704 * c + 88 * (h + 1)]
+                all_ref[(h // 2) ^ z, (h % 2) ^ k, :, at : at + 88] = piece.astype(jnp.bfloat16)
+    for d, ref in enumerate((own_ref, near_ref, mid_ref, far_ref)):
+        ref[...] = all_ref[d]
+
+
 def pack_call(w):
     return kernel_call(pack_kernel, jax.ShapeDtypeStruct((HEADS, 8, 11 * 264), jnp.bfloat16), 1)(w)
 
 
-def unpack(y, mine_ref, theirs_ref, wide_ref):
-    for half, ref in ((y, mine_ref), (1 - y, theirs_ref)):
-        for j in range(8):
-            slab = ref[j].astype(jnp.float32)
-            first = pl.multiple_of(88 * (4 * (j // 2) + 2 * half + j % 2), 8)
-            for g in range(11):
-                wide_ref[pl.ds(first + 8 * g, 8), :] = slab[:, 264 * g : 264 * (g + 1)]
+def unpack(at_ref, pieces, wide_ref):
+    y, z, k = at_ref[0], at_ref[1], at_ref[2]
+    for dz, dy, dk, piece in pieces:
+        slab = piece.astype(jnp.float32)
+        first = pl.multiple_of(88 * (4 * (z ^ dz) + 2 * (y ^ dy) + (k ^ dk)), 8)
+        for g in range(11):
+            wide_ref[pl.ds(first + 8 * g, 8), :] = slab[:, 264 * g : 264 * (g + 1)]
     return wide_ref[...].astype(jnp.bfloat16)
 
 
@@ -141,8 +154,12 @@
     picked_ref[...] = jnp.dot(tokens, chosen, preferred_element_type=jnp.float32).astype(jnp.bfloat16)
 
 
-def spatial_kernel(at_ref, normed_ref, mine_ref, theirs_ref, out_ref, wide_ref):
-    w = unpack(at_ref[0], mine_ref, theirs_ref, wide_ref)
+def spatial_kernel(at_ref, normed_ref, same_ref, cross_ref, same_y_ref, cross_y_ref, out_ref, wide_ref):
+    pieces = []
+    for dy, same, cross in ((0, same_ref, cross_ref), (1, same_y_ref, cross_y_ref)):
+        for d in range(4):
+            pieces += [(d, dy, 0, same[d, 0]), (d, dy, 1, cross[d])]
+    w = unpack(at_ref, pieces, wide_ref)
     packed = jnp.dot(normed_ref[...], w, preferred_element_type=jnp.float32).astype(jnp.bfloat16)
     n = packed.shape[0]
     row = lax.broadcasted_iota(jnp.int32, (n, n), 0) // 32
@@ -150,15 +167,17 @@
     out_ref[...] = fold(masked_attention(packed, row == col))
 
 
-def columns(y, own_ref, other_ref):
-    own, other = own_ref[...], other_ref[...]
+def project(y, heads, own_ref, other_ref):
+    own, other = (
+        lax.dot_general(heads, ref[...], (((1,), (1,)), ((), ())), preferred_element_type=jnp.float32) for ref in (own_ref, other_ref)
+    )
     return jnp.concatenate([jnp.where(y == 0, own, other), jnp.where(y == 0, other, own)], axis=1)
 
 
 def mixed_kernel(at_ref, same_ref, cross_ref, picked_ref, own_ref, other_ref, keep_ref, send_ref, all_ref):
     y = at_ref[0]
     assemble(at_ref, same_ref, cross_ref, all_ref)
-    update = jnp.dot(heads_of(all_ref), columns(y, own_ref, other_ref), preferred_element_type=jnp.float32)
+    update = project(y, heads_of(all_ref), own_ref, other_ref)
     mixed = picked_ref[...].astype(jnp.float32) + update
     for j in range(8):
         low, high = mixed[32 * j : 32 * j + 16], mixed[32 * j + 16 : 32 * j + 32]
@@ -192,13 +211,14 @@
 def result_kernel(at_ref, same_ref, cross_ref, mixed_ref, own_ref, other_ref, out_ref, all_ref):
     y = at_ref[0]
     assemble(at_ref, same_ref, cross_ref, all_ref)
-    update = jnp.dot(heads_of(all_ref), columns(y, own_ref, other_ref), preferred_element_type=jnp.float32)
+    update = project(y, heads_of(all_ref), own_ref, other_ref)
     for half in range(2):
         for j in range(8):
             frame = 4 * (j // 2) + 2 * (y if half == 0 else 1 - y) + j % 2
             residual = mixed_ref[16 * j : 16 * j + 16, 176 * half : 176 * (half + 1)].astype(jnp.float32)
             at = 128 * half + 16 * j
-            out_ref[frame] = (residual + update[at : at + 16]).astype(jnp.bfloat16)
+            rows = (residual + update[at : at + 16]).astype(jnp.bfloat16)
+            out_ref[frame] = jnp.concatenate([rows[:8], rows[8:]], axis=1)
 
 
 def finish_kernel(blocks_ref, out_ref):
@@ -207,7 +227,9 @@
         block = blocks_ref[i]
         for other in range(2):
             at = 88 * (4 * z + 2 * other + k)
-            out_ref[16 * y : 16 * y + 16, at : at + 88] = block[:, 88 * other : 88 * (other + 1)]
+            for half in range(2):
+                first = 16 * y + 8 * half
+                out_ref[first : first + 8, at : at + 88] = block[:, 176 * half + 88 * other : 176 * half + 88 * (other + 1)]
 
 
 VM = pl.BlockSpec(memory_space=pltpu.VMEM)
@@ -249,16 +271,25 @@
     wide = pltpu.VMEM((D, 264), jnp.float32)
     heads = pltpu.VMEM((8, 64, 352), bf)
 
-    so, to_ = spatial_out, temporal_out
-    packed_one, frame = lax.optimization_barrier((pack_call(spatial_qkv), video.reshape(patches, D)))
-    one = scatter(packed_one)
-    tokens = gather(frame)
+    so, to_ = spatial_out.T, temporal_out.T
+    part = S(2, 8, 11 * 264)
+    parts = call(pack_near_kernel, (part,) * 4, spatial_qkv, scratch=[pltpu.VMEM((4, 2, 8, 11 * 264), bf)])
+    near, mid, far = (lax.ppermute(p, "seq", to(m)) for p, m in zip(parts[1:], (4, 8, 12)))
     so_o, to_o = across(so), across(to_)
+    near, mid, far, so_o, to_o, frame, packed_two = lax.optimization_barrier(
+        (near, mid, far, so_o, to_o, video.reshape(patches, D), pack_call(temporal_qkv))
+    )
+    all_w = jnp.stack([parts[0], near, mid, far])
+    all_y = across(all_w)
+    cross_w = lax.ppermute(all_w[:, 1], "seq", to(1))
+    two_w = scatter(packed_two)
+    t_far, t_mid, t_near = (lax.ppermute(frame, "seq", to(m)) for m in (12, 8, 4))
+    same = jnp.stack([frame, t_near, t_mid, t_far])
+    same, all_y = lax.optimization_barrier((same, all_y))
+    tokens = same, lax.ppermute(same, "seq", to(1))
+    cross_y = lax.ppermute(all_y[:, 1], "seq", to(1))
     normed, picked = call(tokens_kernel, (S(256, D), S(256, 176)), *tokens, scratch=[pltpu.VMEM((8, patches, D), bf)])
-    one, so_o, to_o, normed, two_r = lax.optimization_barrier((one, so_o, to_o, normed, temporal_qkv))
-    one_o = across(one)
-    two_w = scatter(pack_call(two_r))
-    spatial = call(spatial_kernel, S(64, 352), normed, one, one_o, scratch=[wide])
+    spatial = call(spatial_kernel, S(64, 352), normed, all_w, cross_w, all_y, cross_y, scratch=[wide])
     same, cross = gather(spatial)
     same, two_w = lax.optimization_barrier((same, two_w))
     two_o = across(two_w)
@@ -268,7 +299,7 @@
     temporal = call(
         temporal_kernel, S(64, 352), *gather(mixed), rows, scratch=[pltpu.VMEM((8, 128, 352), bf)]
     )
-    result = call(result_kernel, S(16, 16, 176), *gather(temporal), mixed, to_, to_o, scratch=[heads])
+    result = call(result_kernel, S(16, 8, 352), *gather(temporal), mixed, to_, to_o, scratch=[heads])
     result = lax.all_to_all(result, "seq", 0, 0, tiled=True)
     return kernel_call(finish_kernel, S(patches, D), 1)(result).reshape(1, patches, D)
 

time: 93.3 us -> 88.8 us (0.952)
  waiting for transfers between devices: 34.6 us -> 28.5 us
  blocking collectives: 10.5 us -> 11.5 us
    ppermute x0 -> x9, starting transfers between devices: none -> 9.77 us  [the longest x3 4.68 us: head_body(): lax.ppermute(p, 'seq', to(m))]
    ppermute x5, waiting for transfers between devices: 14.2 us -> 5.28 us  [head_body(): across = lambda a: lax.ppermute(a, 'seq', ACROSS_Y)]
    ppermute x0 -> x9, waiting for transfers between devices: none -> 6.19 us  [the longest x3 4.91 us: head_body(): lax.ppermute(p, 'seq', to(m))]
    ppermute x12 -> x9, starting transfers between devices: 18.9 us -> 13.3 us  [gather(): far, mid, near = (lax.ppermute(a, 'seq', to(m)) for m in (12, 8, 4))]
    all_to_all x2 -> x1, starting transfers between devices: 8.9 us -> 3.85 us  [head_body(): lax.all_to_all(a, 'seq', 0, 0, tiled=True, axis_index_groups=COLUMNS)]
    ppermute x12 -> x9, waiting for transfers between devices: 16.9 us -> 13.5 us  [gather(): far, mid, near = (lax.ppermute(a, 'seq', to(m)) for m in (12, 8, 4))]
    pallas_call x2 -> x1, Pallas kernels: 2.17 us -> 1.06 us  [pack_call(): kernel_call(pack_kernel, jax.ShapeDtypeStruct((HEADS, 8, 11 * 264), jnp.b...]
    pallas_call x6 -> x7, Pallas kernels: 8.99 us -> 10 us  [call(): return kernel_call(body, shapes, len(args), list(scratch), True)(at, *args)]
  transfers between devices with their start and end apart: 23 -> 27, of which waited for: 14 -> 15; matrix products, arithmetic and copies ran while one was open for 1% -> 1% of each run, Pallas kernels for 6% -> 7%
where the time goes in v3:
time: 88.8 us; the launch traced here: 88.5 us
  starting transfers between devices  33.8 us (38%)
  waiting for transfers between devices  28.5 us (32%)
  Pallas kernels  11.8 us (13%)
  blocking collectives  11.5 us (13%)
  local copies, waits for them, and re-layouts  2.08 us (2%)
    ppermute x9, waiting for transfers between devices, gather(): far, mid, near = (lax.ppermute(a, 'seq', to(m)) for m in (12, 8, 4))  13.5 us
    ppermute x9, starting transfers between devices, gather(): far, mid, near = (lax.ppermute(a, 'seq', to(m)) for m in (12, 8, 4))  13.3 us
    all_to_all x1, blocking collectives, head_body(): result = lax.all_to_all(result, 'seq', 0, 0, tiled=True)  11.5 us
    pallas_call x7, Pallas kernels, call(): return kernel_call(body, shapes, len(args), list(scratch), True)(at, *args)  10 us
    ppermute x5, starting transfers between devices, head_body(): across = lambda a: lax.ppermute(a, 'seq', ACROSS_Y)  6.71 us
    ppermute x5, waiting for transfers between devices, head_body(): across = lambda a: lax.ppermute(a, 'seq', ACROSS_Y)  5.28 us
    ppermute x3, waiting for transfers between devices, head_body(): lax.ppermute(p, 'seq', to(m))  4.91 us
    ppermute x3, starting transfers between devices, head_body(): lax.ppermute(p, 'seq', to(m))  4.68 us
  transfers between devices with their start and end apart: 27, of which 15 were waited for; matrix products, arithmetic and copies ran while one was open for 1% of the time, Pallas kernels for 7%

profile of v3, /device:TPU:0, one launch (start us, length us, event | category | flops | bytes accessed | tf_op | source)
XLA Modules:
  0.0 88.5 jit_solution(7283251559163975271)
XLA Ops:
  0.0 3.0 %collective-permute-start.3 = (bf16[88,704]{1,0:T(8,128)(2,1)}, bf16[88,704]{1,0:T(8,128)(2,1)S(1)}, u32[]{:S(2)}, u32[]{:S(2)}) collective-permute-start(bf16[88,704]{1,0:T(8,128)(2,1)} %bitcast.34), channel_id=1, source_target_pairs={{0,2},{1,3},{2,0},{3,1},{4,6},{5,7},{6,4},{7,5},{8,10},{9,11},{10,... | collective-permute-start | bytes 371720 | tf_op jit(solution)/shard_map/ppermute | solution.py:260
  3.0 0.1 collective-permute-start.4
  3.0 0.1 pad_add_fusion.at_ref
  3.1 1.0 %copy-done = bf16[88,2112]{1,0:T(8,128)(2,1)S(1)} copy-done((bf16[88,2112]{1,0:T(8,128)(2,1)S(1)}, bf16[88,2112]{1,0:T(8,128)(2,1)}, u32[]{:S(2)}) %copy-start) | copy-done | bytes 371736
  4.1 0.9 %shard_map.55 = (bf16[2,8,2904]{2,1,0:T(8,128)(2,1)S(1)}, bf16[2,8,2904]{2,1,0:T(8,128)(2,1)S(1)}, bf16[2,8,2904]{2,1,0:T(8,128)(2,1)S(1)}, bf16[2,8,2904]{2,1,0:T(8,128)(2,1)S(1)}) custom-call(s32[3]{0:T(128)S(1)} %pad_add_fusion.at_ref, bf16[88,2112]{1,0:T(8,128)(2,1)S(1)} %copy-done), custom_call_target="tpu_custom_call" | custom-call | tf_op jit(solution)/shard_map/pallas_call | solution.py:268
  5.0 2.1 %collective-permute-start = (bf16[2,8,2904]{2,1,0:T(8,128)(2,1)S(1)}, bf16[2,8,2904]{2,1,0:T(8,128)(2,1)S(1)}, u32[]{:S(2)}, u32[]{:S(2)}) collective-permute-start(bf16[2,8,2904]{2,1,0:T(8,128)(2,1)S(1)} %get-tuple-element.24), channel_id=1, source_target_pairs={{0,4},{1,5},{2,6},{3,7},{4,0},{5,1},{6,2},{7,3},{8,12},{9,13},{10,... | collective-permute-start | bytes 278792 | tf_op jit(solution)/shard_map/ppermute | solution.py:277
  7.1 2.6 %collective-permute-start.1 = (bf16[2,8,2904]{2,1,0:T(8,128)(2,1)S(1)}, bf16[2,8,2904]{2,1,0:T(8,128)(2,1)S(1)}, u32[]{:S(2)}, u32[]{:S(2)}) collective-permute-start(bf16[2,8,2904]{2,1,0:T(8,128)(2,1)S(1)} %get-tuple-element.25), channel_id=1, source_target_pairs={{0,8},{1,9},{2,10},{3,11},{4,12},{5,13},{6,14},{7,15},{8,0},{9,1},... | collective-permute-start | bytes 278792 | tf_op jit(solution)/shard_map/ppermute | solution.py:277
  9.7 0.0 collective-permute-start.2
  9.7 1.0 %copy-done.1 = bf16[88,2112]{1,0:T(8,128)(2,1)S(1)} copy-done((bf16[88,2112]{1,0:T(8,128)(2,1)S(1)}, bf16[88,2112]{1,0:T(8,128)(2,1)}, u32[]{:S(2)}) %copy-start.1) | copy-done | bytes 371736
  10.7 1.1 %shard_map.56 = bf16[8,8,2904]{2,1,0:T(8,128)(2,1)} custom-call(bf16[88,2112]{1,0:T(8,128)(2,1)S(1)} %copy-done.1), custom_call_target="tpu_custom_call" | custom-call | tf_op jit(solution)/shard_map/pallas_call | solution.py:101
  11.7 0.0 collective-permute-done
  11.7 4.9 %collective-permute-done.1 = bf16[2,8,2904]{2,1,0:T(8,128)(2,1)S(1)} collective-permute-done((bf16[2,8,2904]{2,1,0:T(8,128)(2,1)S(1)}, bf16[2,8,2904]{2,1,0:T(8,128)(2,1)S(1)}, u32[]{:S(2)}, u32[]{:S(2)}) %collective-permute-start.1) | collective-permute-done | bytes 92960 | tf_op jit(solution)/shard_map/ppermute | solution.py:277
  16.6 0.0 collective-permute-done.2
  16.7 1.6 %collective-permute-start.5 = (bf16[32,1408]{1,0:T(8,128)(2,1)S(1)}, bf16[32,1408]{1,0:T(8,128)(2,1)S(1)}, u32[]{:S(2)}, u32[]{:S(2)}) collective-permute-start(bf16[32,1408]{1,0:T(8,128)(2,1)S(1)} %bitcast.45), channel_id=1, source_target_pairs={{0,4},{1,5},{2,6},{3,7},{4,0},{5,1},{6,2},{7,3},{8,12},{9,13},{10,... | collective-permute-start | bytes 270344 | tf_op jit(solution)/shard_map/ppermute | solution.py:286
  18.3 1.5 %collective-permute-start.6 = (bf16[32,1408]{1,0:T(8,128)(2,1)S(1)}, bf16[32,1408]{1,0:T(8,128)(2,1)S(1)}, u32[]{:S(2)}, u32[]{:S(2)}) collective-permute-start(bf16[32,1408]{1,0:T(8,128)(2,1)S(1)} %bitcast.46), channel_id=1, source_target_pairs={{0,8},{1,9},{2,10},{3,11},{4,12},{5,13},{6,14},{7,15},{8,0},{9,1},... | collective-permute-start | bytes 270344 | tf_op jit(solution)/shard_map/ppermute | solution.py:286
  19.8 1.3 %collective-permute-start.7 = (bf16[32,1408]{1,0:T(8,128)(2,1)S(1)}, bf16[32,1408]{1,0:T(8,128)(2,1)S(1)}, u32[]{:S(2)}, u32[]{:S(2)}) collective-permute-start(bf16[32,1408]{1,0:T(8,128)(2,1)S(1)} %bitcast.47), channel_id=1, source_target_pairs={{0,12},{1,13},{2,14},{3,15},{4,8},{5,9},{6,10},{7,11},{8,4},{9,5},... | collective-permute-start | bytes 270344 | tf_op jit(solution)/shard_map/ppermute | solution.py:286
  21.1 0.1 pad_maximum_fusion.1
  21.2 1.6 %collective-permute-start.8 = (bf16[4,2,8,2904]{3,2,0,1:T(8,128)(2,1)S(1)}, bf16[4,2,8,2904]{3,2,0,1:T(8,128)(2,1)S(1)}, u32[]{:S(2)}, u32[]{:S(2)}) collective-permute-start(bf16[4,2,8,2904]{3,2,0,1:T(8,128)(2,1)S(1)} %pad_maximum_fusion.1), channel_id=1, source_target_pairs={{0,2},{1,3},{2,0},{3,1},{4,6},{5,7},{6,4},{7,5},{8,10},{9,11},{10,... | collective-permute-start | bytes 1115144 | tf_op jit(solution)/shard_map/ppermute | solution.py:260
  22.8 0.1 collective-permute-start.10
  22.9 3.9 %all-to-all-start = ((bf16[8,8,2904]{2,1,0:T(8,128)(2,1)}), bf16[8,8,2904]{2,1,0:T(8,128)(2,1)S(1)}, u32[]{:S(2)}, u32[]{:S(2)}) async-start(bf16[8,8,2904]{2,1,0:T(8,128)(2,1)} %shard_map.56), calls=%async_computation | async-start | bytes 753664 | tf_op jit(solution)/shard_map/all_to_all | solution.py:259
  26.7 0.3 collective-permute-done.6
  27.0 0.1 pad_maximum_fusion.2.same_ref
  27.0 2.7 %collective-permute-done.8 = bf16[4,2,8,2904]{3,2,0,1:T(8,128)(2,1)S(1)} collective-permute-done((bf16[4,2,8,2904]{3,2,0,1:T(8,128)(2,1)S(1)}, bf16[4,2,8,2904]{3,2,0,1:T(8,128)(2,1)S(1)}, u32[]{:S(2)}, u32[]{:S(2)}) %collective-permute-start.8) | collective-permute-done | bytes 371744 | tf_op jit(solution)/shard_map/ppermute | solution.py:260
  29.7 0.6 collective-permute-start.11
  30.4 1.0 %collective-permute-done.9.cross_ref = bf16[4,32,1408]{2,1,0:T(8,128)(2,1)S(1)} collective-permute-done((bf16[4,32,1408]{2,1,0:T(8,128)(2,1)S(1)}, bf16[4,32,1408]{2,1,0:T(8,128)(2,1)S(1)}, u32[]{:S(2)}, u32[]{:S(2)}) %collective-permute-start.9) | collective-permute-done | bytes 360480 | tf_op jit(solution)/shard_map/ppermute | solution.py:289
  31.4 1.2 %shard_map.57 = (bf16[256,1408]{1,0:T(8,128)(2,1)S(1)}, bf16[256,176]{1,0:T(8,128)(2,1)S(1)}) custom-call(s32[3]{0:T(128)S(1)} %pad_add_fusion.at_ref, bf16[4,32,1408]{2,1,0:T(8,128)(2,1)S(1)} %pad_maximum_fusion.2.same_ref, bf16[4,32,1408]{2,1,0:T(8,128)(2,1)S(1)} %collective-permute-done.9.cross_ref), custom_call_target="tpu_custom_call" | custom-call | tf_op jit(solution)/shard_map/pallas_call | solution.py:268
  32.6 0.0 copy-start.2
  32.6 2.1 %shard_map.58 = bf16[64,352]{1,0:T(8,128)(2,1)S(1)} custom-call(s32[3]{0:T(128)S(1)} %pad_add_fusion.at_ref, bf16[256,1408]{1,0:T(8,128)(2,1)S(1)} %get-tuple-element.33.normed_ref, bf16[4,2,8,2904]{3,2,1,0:T(8,128)(2,1)S(1)} %copy.6.same_ref, bf16[4,8,2904]{2,1,0:T(8,128)(2,1)S(1)} %collective-permute-done.10.cross_ref, ...), custom_call_target="tpu_custom_call" | custom-call | tf_op jit(solution)/shard_map/pallas_call | solution.py:268
  34.7 0.8 collective-permute-start.12
  35.5 1.9 %collective-permute-start.13 = (bf16[64,352]{1,0:T(8,128)(2,1)S(1)}, bf16[64,352]{1,0:T(8,128)(2,1)S(1)}, u32[]{:S(2)}, u32[]{:S(2)}) collective-permute-start(bf16[64,352]{1,0:T(8,128)(2,1)S(1)} %shard_map.58), channel_id=1, source_target_pairs={{0,8},{1,9},{2,10},{3,11},{4,12},{5,13},{6,14},{7,15},{8,0},{9,1},... | collective-permute-start | bytes 135176 | tf_op jit(solution)/shard_map/ppermute | solution.py:263
  37.4 1.7 %collective-permute-start.14 = (bf16[64,352]{1,0:T(8,128)(2,1)S(1)}, bf16[64,352]{1,0:T(8,128)(2,1)S(1)}, u32[]{:S(2)}, u32[]{:S(2)}) collective-permute-start(bf16[64,352]{1,0:T(8,128)(2,1)S(1)} %shard_map.58), channel_id=1, source_target_pairs={{0,12},{1,13},{2,14},{3,15},{4,8},{5,9},{6,10},{7,11},{8,4},{9,5},... | collective-permute-start | bytes 135176 | tf_op jit(solution)/shard_map/ppermute | solution.py:263
  39.1 0.9 %collective-permute-done.12 = bf16[64,352]{1,0:T(8,128)(2,1)S(1)} collective-permute-done((bf16[64,352]{1,0:T(8,128)(2,1)S(1)}, bf16[64,352]{1,0:T(8,128)(2,1)S(1)}, u32[]{:S(2)}, u32[]{:S(2)}) %collective-permute-start.12) | collective-permute-done | bytes 45088 | tf_op jit(solution)/shard_map/ppermute | solution.py:263
  40.0 2.2 %collective-permute-done.13 = bf16[64,352]{1,0:T(8,128)(2,1)S(1)} collective-permute-done((bf16[64,352]{1,0:T(8,128)(2,1)S(1)}, bf16[64,352]{1,0:T(8,128)(2,1)S(1)}, u32[]{:S(2)}, u32[]{:S(2)}) %collective-permute-start.13) | collective-permute-done | bytes 45088 | tf_op jit(solution)/shard_map/ppermute | solution.py:263
  42.2 1.1 %collective-permute-done.14 = bf16[64,352]{1,0:T(8,128)(2,1)S(1)} collective-permute-done((bf16[64,352]{1,0:T(8,128)(2,1)S(1)}, bf16[64,352]{1,0:T(8,128)(2,1)S(1)}, u32[]{:S(2)}, u32[]{:S(2)}) %collective-permute-start.14) | collective-permute-done | bytes 45088 | tf_op jit(solution)/shard_map/ppermute | solution.py:263
  43.4 0.1 collective-permute-start.15
  43.4 1.4 %collective-permute-done.15.cross_ref = bf16[4,64,352]{2,1,0:T(8,128)(2,1)S(1)} collective-permute-done((bf16[4,64,352]{2,1,0:T(8,128)(2,1)S(1)}, bf16[4,64,352]{2,1,0:T(8,128)(2,1)S(1)}, u32[]{:S(2)}, u32[]{:S(2)}) %collective-permute-start.15) | collective-permute-done | bytes 180256 | tf_op jit(solution)/shard_map/ppermute | solution.py:265
  44.9 1.1 %shard_map.59 = (bf16[128,176]{1,0:T(8,128)(2,1)S(1)}, bf16[128,176]{1,0:T(8,128)(2,1)S(1)}) custom-call(s32[3]{0:T(128)S(1)} %pad_add_fusion.at_ref, bf16[4,64,352]{2,1,0:T(8,128)(2,1)S(1)} %pad_maximum_fusion.3.same_ref, bf16[4,64,352]{2,1,0:T(8,128)(2,1)S(1)} %collective-permute-done.15.cross_ref, bf16[256,176]{1,0:T(8,128)(2,1)S(1)} %get-tuple-element.37.picked_ref, ...), custom_call_target="tpu_custom_call" | custom-call | tf_op jit(solution)/shard_map/pallas_call | solution.py:268
  45.9 1.6 %collective-permute-start.16 = (bf16[128,176]{1,0:T(8,128)(2,1)S(1)}, bf16[128,176]{1,0:T(8,128)(2,1)S(1)}, u32[]{:S(2)}, u32[]{:S(2)}) collective-permute-start(bf16[128,176]{1,0:T(8,128)(2,1)S(1)} %get-tuple-element.40), channel_id=1, source_target_pairs={{0,2},{1,3},{2,0},{3,1},{4,6},{5,7},{6,4},{7,5},{8,10},{9,11},{10,... | collective-permute-start | bytes 135176 | tf_op jit(solution)/shard_map/ppermute | solution.py:260
  47.5 0.5 collective-permute-start.21
  48.0 2.6 %collective-permute-done.16 = bf16[128,176]{1,0:T(8,128)(2,1)S(1)} collective-permute-done((bf16[128,176]{1,0:T(8,128)(2,1)S(1)}, bf16[128,176]{1,0:T(8,128)(2,1)S(1)}, u32[]{:S(2)}, u32[]{:S(2)}) %collective-permute-start.16) | collective-permute-done | bytes 45088 | tf_op jit(solution)/shard_map/ppermute | solution.py:260
  50.6 0.1 pad_maximum_fusion.5.mixed_ref
  50.7 0.1 collective-permute-start.17
  50.8 2.3 %collective-permute-start.18 = (bf16[128,352]{1,0:T(8,128)(2,1)S(1)}, bf16[128,352]{1,0:T(8,128)(2,1)S(1)}, u32[]{:S(2)}, u32[]{:S(2)}) collective-permute-start(bf16[128,352]{1,0:T(8,128)(2,1)S(1)} %pad_maximum_fusion.5.mixed_ref), channel_id=1, source_target_pairs={{0,8},{1,9},{2,10},{3,11},{4,12},{5,13},{6,14},{7,15},{8,0},{9,1},... | collective-permute-start | bytes 270344 | tf_op jit(solution)/shard_map/ppermute | solution.py:263
  53.2 2.0 %collective-permute-start.19 = (bf16[128,352]{1,0:T(8,128)(2,1)S(1)}, bf16[128,352]{1,0:T(8,128)(2,1)S(1)}, u32[]{:S(2)}, u32[]{:S(2)}) collective-permute-start(bf16[128,352]{1,0:T(8,128)(2,1)S(1)} %pad_maximum_fusion.5.mixed_ref), channel_id=1, source_target_pairs={{0,12},{1,13},{2,14},{3,15},{4,8},{5,9},{6,10},{7,11},{8,4},{9,5},... | collective-permute-start | bytes 270344 | tf_op jit(solution)/shard_map/ppermute | solution.py:263
  55.2 0.1 fusion
  55.3 0.1 collective-permute-done.17
  55.4 5.0 %collective-permute-done.18 = bf16[128,352]{1,0:T(8,128)(2,1)S(1)} collective-permute-done((bf16[128,352]{1,0:T(8,128)(2,1)S(1)}, bf16[128,352]{1,0:T(8,128)(2,1)S(1)}, u32[]{:S(2)}, u32[]{:S(2)}) %collective-permute-start.18) | collective-permute-done | bytes 90144 | tf_op jit(solution)/shard_map/ppermute | solution.py:263
  60.4 0.1 pad_maximum_fusion.same_ref
  60.5 0.1 collective-permute-start.20
  60.6 1.0 %shard_map.60.w_ref = bf16[1408,264]{1,0:T(8,128)(2,1)S(1)} custom-call(s32[3]{0:T(128)S(1)} %pad_add_fusion.at_ref, bf16[8,8,2904]{2,1,0:T(8,128)(2,1)S(1)} %all-to-all-done.mine_ref, bf16[8,8,2904]{2,1,0:T(8,128)(2,1)S(1)} %collective-permute-done.21.theirs_ref), custom_call_target="tpu_custom_call" | custom-call | tf_op jit(solution)/shard_map/pallas_call | solution.py:268
  61.6 0.0 copy-start.3
  61.6 0.6 collective-permute-done.20.cross_ref
  62.3 2.5 %shard_map.61 = bf16[64,352]{1,0:T(8,128)(2,1)S(1)} custom-call(s32[3]{0:T(128)S(1)} %pad_add_fusion.at_ref, bf16[4,128,352]{2,1,0:T(8,128)(2,1)S(1)} %pad_maximum_fusion.same_ref, bf16[4,128,352]{2,1,0:T(8,128)(2,1)S(1)} %collective-permute-done.20.cross_ref, bf16[1408,264]{1,0:T(8,128)(2,1)S(1)} %shard_map.60.w_ref), custom_call_target="tpu_custom_call" | custom-call | tf_op jit(solution)/shard_map/pallas_call | solution.py:268
  64.8 1.6 %collective-permute-start.22 = (bf16[64,352]{1,0:T(8,128)(2,1)S(1)}, bf16[64,352]{1,0:T(8,128)(2,1)S(1)}, u32[]{:S(2)}, u32[]{:S(2)}) collective-permute-start(bf16[64,352]{1,0:T(8,128)(2,1)S(1)} %shard_map.61), channel_id=1, source_target_pairs={{0,4},{1,5},{2,6},{3,7},{4,0},{5,1},{6,2},{7,3},{8,12},{9,13},{10,... | collective-permute-start | bytes 135176 | tf_op jit(solution)/shard_map/ppermute | solution.py:263
  66.4 1.0 %collective-permute-start.23 = (bf16[64,352]{1,0:T(8,128)(2,1)S(1)}, bf16[64,352]{1,0:T(8,128)(2,1)S(1)}, u32[]{:S(2)}, u32[]{:S(2)}) collective-permute-start(bf16[64,352]{1,0:T(8,128)(2,1)S(1)} %shard_map.61), channel_id=1, source_target_pairs={{0,8},{1,9},{2,10},{3,11},{4,12},{5,13},{6,14},{7,15},{8,0},{9,1},... | collective-permute-start | bytes 135176 | tf_op jit(solution)/shard_map/ppermute | solution.py:263
  67.5 1.8 %collective-permute-start.24 = (bf16[64,352]{1,0:T(8,128)(2,1)S(1)}, bf16[64,352]{1,0:T(8,128)(2,1)S(1)}, u32[]{:S(2)}, u32[]{:S(2)}) collective-permute-start(bf16[64,352]{1,0:T(8,128)(2,1)S(1)} %shard_map.61), channel_id=1, source_target_pairs={{0,12},{1,13},{2,14},{3,15},{4,8},{5,9},{6,10},{7,11},{8,4},{9,5},... | collective-permute-start | bytes 135176 | tf_op jit(solution)/shard_map/ppermute | solution.py:263
  69.2 3.7 %collective-permute-done.23 = bf16[64,352]{1,0:T(8,128)(2,1)S(1)} collective-permute-done((bf16[64,352]{1,0:T(8,128)(2,1)S(1)}, bf16[64,352]{1,0:T(8,128)(2,1)S(1)}, u32[]{:S(2)}, u32[]{:S(2)}) %collective-permute-start.23) | collective-permute-done | bytes 45088 | tf_op jit(solution)/shard_map/ppermute | solution.py:263
  72.9 0.5 collective-permute-done.24
  73.4 0.1 pad_maximum_fusion.4.same_ref
  73.5 0.1 collective-permute-start.25
  73.6 1.4 %collective-permute-done.25.cross_ref = bf16[4,64,352]{2,1,0:T(8,128)(2,1)S(1)} collective-permute-done((bf16[4,64,352]{2,1,0:T(8,128)(2,1)S(1)}, bf16[4,64,352]{2,1,0:T(8,128)(2,1)S(1)}, u32[]{:S(2)}, u32[]{:S(2)}) %collective-permute-start.25) | collective-permute-done | bytes 180256 | tf_op jit(solution)/shard_map/ppermute | solution.py:265
  75.0 1.2 %shard_map.62 = bf16[16,8,352]{2,1,0:T(8,128)(2,1)S(1)} custom-call(s32[3]{0:T(128)S(1)} %pad_add_fusion.at_ref, bf16[4,64,352]{2,1,0:T(8,128)(2,1)S(1)} %pad_maximum_fusion.4.same_ref, bf16[4,64,352]{2,1,0:T(8,128)(2,1)S(1)} %collective-permute-done.25.cross_ref, bf16[128,352]{1,0:T(8,128)(2,1)S(1)} %pad_maximum_fusion.5.mixed_ref, ...), custom_call_target="tpu_custom_call" | custom-call | tf_op jit(solution)/shard_map/pallas_call | solution.py:268
  76.2 11.5 %all_to_all.10.blocks_ref = bf16[16,8,352]{2,1,0:T(8,128)(2,1)S(1)} all-to-all(bf16[16,8,352]{2,1,0:T(8,128)(2,1)S(1)} %shard_map.62), channel_id=1, replica_groups=mesh['groups'=2,'seq'=16] {'seq'}, dimensions={0} | all-to-all | bytes 180224 | tf_op jit(solution)/shard_map/all_to_all | solution.py:303
  87.7 0.8 shard_map.63
  (22 shorter events, 0.2 us)
Async XLA Ops:
  0.0 16.7 %copy-start.4 = (bf16[1,32,1408]{2,1,0:T(8,128)(2,1)S(1)}, bf16[1,32,1408]{2,1,0:T(8,128)(2,1)}, u32[]{:S(2)}) copy-start(bf16[1,32,1408]{2,1,0:T(8,128)(2,1)} %param.5) | copy-start | bytes 270340
  0.0 16.6 %collective-permute-start.3 = (bf16[88,704]{1,0:T(8,128)(2,1)}, bf16[88,704]{1,0:T(8,128)(2,1)S(1)}, u32[]{:S(2)}, u32[]{:S(2)}) collective-permute-start(bf16[88,704]{1,0:T(8,128)(2,1)} %bitcast.34), channel_id=1, source_target_pairs={{0,2},{1,3},{2,0},{3,1},{4,6},{5,7},{6,4},{7,5},{8,10},{9,11},{10,... | collective-permute-start | bytes 371720 | tf_op jit(solution)/shard_map/ppermute | solution.py:260
  3.0 13.7 %collective-permute-start.4 = (bf16[88,704]{1,0:T(8,128)(2,1)}, bf16[88,704]{1,0:T(8,128)(2,1)S(1)}, u32[]{:S(2)}, u32[]{:S(2)}) collective-permute-start(bf16[88,704]{1,0:T(8,128)(2,1)} %bitcast.36), channel_id=1, source_target_pairs={{0,2},{1,3},{2,0},{3,1},{4,6},{5,7},{6,4},{7,5},{8,10},{9,11},{10,... | collective-permute-start | bytes 371720 | tf_op jit(solution)/shard_map/ppermute | solution.py:260
  3.1 1.0 %copy-start = (bf16[88,2112]{1,0:T(8,128)(2,1)S(1)}, bf16[88,2112]{1,0:T(8,128)(2,1)}, u32[]{:S(2)}) copy-start(bf16[88,2112]{1,0:T(8,128)(2,1)} %w_ref.2) | copy-start | bytes 1115140
  5.0 6.7 %collective-permute-start = (bf16[2,8,2904]{2,1,0:T(8,128)(2,1)S(1)}, bf16[2,8,2904]{2,1,0:T(8,128)(2,1)S(1)}, u32[]{:S(2)}, u32[]{:S(2)}) collective-permute-start(bf16[2,8,2904]{2,1,0:T(8,128)(2,1)S(1)} %get-tuple-element.24), channel_id=1, source_target_pairs={{0,4},{1,5},{2,6},{3,7},{4,0},{5,1},{6,2},{7,3},{8,12},{9,13},{10,... | collective-permute-start | bytes 278792 | tf_op jit(solution)/shard_map/ppermute | solution.py:277
  7.1 9.6 %collective-permute-start.1 = (bf16[2,8,2904]{2,1,0:T(8,128)(2,1)S(1)}, bf16[2,8,2904]{2,1,0:T(8,128)(2,1)S(1)}, u32[]{:S(2)}, u32[]{:S(2)}) collective-permute-start(bf16[2,8,2904]{2,1,0:T(8,128)(2,1)S(1)} %get-tuple-element.25), channel_id=1, source_target_pairs={{0,8},{1,9},{2,10},{3,11},{4,12},{5,13},{6,14},{7,15},{8,0},{9,1},... | collective-permute-start | bytes 278792 | tf_op jit(solution)/shard_map/ppermute | solution.py:277
  9.7 7.0 %collective-permute-start.2 = (bf16[2,8,2904]{2,1,0:T(8,128)(2,1)S(1)}, bf16[2,8,2904]{2,1,0:T(8,128)(2,1)S(1)}, u32[]{:S(2)}, u32[]{:S(2)}) collective-permute-start(bf16[2,8,2904]{2,1,0:T(8,128)(2,1)S(1)} %get-tuple-element.26), channel_id=1, source_target_pairs={{0,12},{1,13},{2,14},{3,15},{4,8},{5,9},{6,10},{7,11},{8,4},{9,5},... | collective-permute-start | bytes 278792 | tf_op jit(solution)/shard_map/ppermute | solution.py:277
  9.7 1.0 %copy-start.1 = (bf16[88,2112]{1,0:T(8,128)(2,1)S(1)}, bf16[88,2112]{1,0:T(8,128)(2,1)}, u32[]{:S(2)}) copy-start(bf16[88,2112]{1,0:T(8,128)(2,1)} %w_ref.3) | copy-start | bytes 1115140
  16.7 10.1 %collective-permute-start.5 = (bf16[32,1408]{1,0:T(8,128)(2,1)S(1)}, bf16[32,1408]{1,0:T(8,128)(2,1)S(1)}, u32[]{:S(2)}, u32[]{:S(2)}) collective-permute-start(bf16[32,1408]{1,0:T(8,128)(2,1)S(1)} %bitcast.45), channel_id=1, source_target_pairs={{0,4},{1,5},{2,6},{3,7},{4,0},{5,1},{6,2},{7,3},{8,12},{9,13},{10,... | collective-permute-start | bytes 270344 | tf_op jit(solution)/shard_map/ppermute | solution.py:286
  18.3 8.7 %collective-permute-start.6 = (bf16[32,1408]{1,0:T(8,128)(2,1)S(1)}, bf16[32,1408]{1,0:T(8,128)(2,1)S(1)}, u32[]{:S(2)}, u32[]{:S(2)}) collective-permute-start(bf16[32,1408]{1,0:T(8,128)(2,1)S(1)} %bitcast.46), channel_id=1, source_target_pairs={{0,8},{1,9},{2,10},{3,11},{4,12},{5,13},{6,14},{7,15},{8,0},{9,1},... | collective-permute-start | bytes 270344 | tf_op jit(solution)/shard_map/ppermute | solution.py:286
  19.8 7.2 %collective-permute-start.7 = (bf16[32,1408]{1,0:T(8,128)(2,1)S(1)}, bf16[32,1408]{1,0:T(8,128)(2,1)S(1)}, u32[]{:S(2)}, u32[]{:S(2)}) collective-permute-start(bf16[32,1408]{1,0:T(8,128)(2,1)S(1)} %bitcast.47), channel_id=1, source_target_pairs={{0,12},{1,13},{2,14},{3,15},{4,8},{5,9},{6,10},{7,11},{8,4},{9,5},... | collective-permute-start | bytes 270344 | tf_op jit(solution)/shard_map/ppermute | solution.py:286
  21.2 8.5 %collective-permute-start.8 = (bf16[4,2,8,2904]{3,2,0,1:T(8,128)(2,1)S(1)}, bf16[4,2,8,2904]{3,2,0,1:T(8,128)(2,1)S(1)}, u32[]{:S(2)}, u32[]{:S(2)}) collective-permute-start(bf16[4,2,8,2904]{3,2,0,1:T(8,128)(2,1)S(1)} %pad_maximum_fusion.1), channel_id=1, source_target_pairs={{0,2},{1,3},{2,0},{3,1},{4,6},{5,7},{6,4},{7,5},{8,10},{9,11},{10,... | collective-permute-start | bytes 1115144 | tf_op jit(solution)/shard_map/ppermute | solution.py:260
  22.8 9.8 %collective-permute-start.10 = (bf16[4,8,2904]{2,1,0:T(8,128)(2,1)S(1)}, bf16[4,8,2904]{2,1,0:T(8,128)(2,1)S(1)}, u32[]{:S(2)}, u32[]{:S(2)}) collective-permute-start(bf16[4,8,2904]{2,1,0:T(8,128)(2,1)S(1)} %slice_bitcast_fusion), channel_id=1, source_target_pairs={{0,1},{1,0},{2,3},{3,2},{4,5},{5,4},{6,7},{7,6},{8,9},{9,8},{10,11... | collective-permute-start | bytes 557576 | tf_op jit(solution)/shard_map/ppermute | solution.py:284
  22.9 20.6 %all-to-all-start = ((bf16[8,8,2904]{2,1,0:T(8,128)(2,1)}), bf16[8,8,2904]{2,1,0:T(8,128)(2,1)S(1)}, u32[]{:S(2)}, u32[]{:S(2)}) async-start(bf16[8,8,2904]{2,1,0:T(8,128)(2,1)} %shard_map.56), calls=%async_computation | async-start | bytes 753664 | tf_op jit(solution)/shard_map/all_to_all | solution.py:259
  29.7 1.7 %collective-permute-start.9 = (bf16[4,32,1408]{2,1,0:T(8,128)(2,1)S(1)}, bf16[4,32,1408]{2,1,0:T(8,128)(2,1)S(1)}, u32[]{:S(2)}, u32[]{:S(2)}) collective-permute-start(bf16[4,32,1408]{2,1,0:T(8,128)(2,1)S(1)} %pad_maximum_fusion.2.same_ref), channel_id=1, source_target_pairs={{0,1},{1,0},{2,3},{3,2},{4,5},{5,4},{6,7},{7,6},{8,9},{9,8},{10,11... | collective-permute-start | bytes 1081352 | tf_op jit(solution)/shard_map/ppermute | solution.py:289
  29.7 2.8 %collective-permute-start.11 = (bf16[4,8,2904]{2,1,0:T(8,128)(2,1)S(1)}, bf16[4,8,2904]{2,1,0:T(8,128)(2,1)S(1)}, u32[]{:S(2)}, u32[]{:S(2)}) collective-permute-start(bf16[4,8,2904]{2,1,0:T(8,128)(2,1)S(1)} %slice_bitcast_fusion.1), channel_id=1, source_target_pairs={{0,1},{1,0},{2,3},{3,2},{4,5},{5,4},{6,7},{7,6},{8,9},{9,8},{10,11... | collective-permute-start | bytes 557576 | tf_op jit(solution)/shard_map/ppermute | solution.py:290
  32.6 12.3 %copy-start.2 = (bf16[704,88]{0,1:T(8,128)(2,1)S(1)}, bf16[704,88]{0,1:T(8,128)(2,1)}, u32[]{:S(2)}) copy-start(bf16[704,88]{0,1:T(8,128)(2,1)} %param.7) | copy-start | bytes 371716
  34.7 5.3 %collective-permute-start.12 = (bf16[64,352]{1,0:T(8,128)(2,1)S(1)}, bf16[64,352]{1,0:T(8,128)(2,1)S(1)}, u32[]{:S(2)}, u32[]{:S(2)}) collective-permute-start(bf16[64,352]{1,0:T(8,128)(2,1)S(1)} %shard_map.58), channel_id=1, source_target_pairs={{0,4},{1,5},{2,6},{3,7},{4,0},{5,1},{6,2},{7,3},{8,12},{9,13},{10,... | collective-permute-start | bytes 135176 | tf_op jit(solution)/shard_map/ppermute | solution.py:263
  35.5 6.7 %collective-permute-start.13 = (bf16[64,352]{1,0:T(8,128)(2,1)S(1)}, bf16[64,352]{1,0:T(8,128)(2,1)S(1)}, u32[]{:S(2)}, u32[]{:S(2)}) collective-permute-start(bf16[64,352]{1,0:T(8,128)(2,1)S(1)} %shard_map.58), channel_id=1, source_target_pairs={{0,8},{1,9},{2,10},{3,11},{4,12},{5,13},{6,14},{7,15},{8,0},{9,1},... | collective-permute-start | bytes 135176 | tf_op jit(solution)/shard_map/ppermute | solution.py:263
  37.4 5.9 %collective-permute-start.14 = (bf16[64,352]{1,0:T(8,128)(2,1)S(1)}, bf16[64,352]{1,0:T(8,128)(2,1)S(1)}, u32[]{:S(2)}, u32[]{:S(2)}) collective-permute-start(bf16[64,352]{1,0:T(8,128)(2,1)S(1)} %shard_map.58), channel_id=1, source_target_pairs={{0,12},{1,13},{2,14},{3,15},{4,8},{5,9},{6,10},{7,11},{8,4},{9,5},... | collective-permute-start | bytes 135176 | tf_op jit(solution)/shard_map/ppermute | solution.py:263
  43.4 1.5 %collective-permute-start.15 = (bf16[4,64,352]{2,1,0:T(8,128)(2,1)S(1)}, bf16[4,64,352]{2,1,0:T(8,128)(2,1)S(1)}, u32[]{:S(2)}, u32[]{:S(2)}) collective-permute-start(bf16[4,64,352]{2,1,0:T(8,128)(2,1)S(1)} %pad_maximum_fusion.3.same_ref), channel_id=1, source_target_pairs={{0,1},{1,0},{2,3},{3,2},{4,5},{5,4},{6,7},{7,6},{8,9},{9,8},{10,11... | collective-permute-start | bytes 540680 | tf_op jit(solution)/shard_map/ppermute | solution.py:265
  45.9 4.7 %collective-permute-start.16 = (bf16[128,176]{1,0:T(8,128)(2,1)S(1)}, bf16[128,176]{1,0:T(8,128)(2,1)S(1)}, u32[]{:S(2)}, u32[]{:S(2)}) collective-permute-start(bf16[128,176]{1,0:T(8,128)(2,1)S(1)} %get-tuple-element.40), channel_id=1, source_target_pairs={{0,2},{1,3},{2,0},{3,1},{4,6},{5,7},{6,4},{7,5},{8,10},{9,11},{10,... | collective-permute-start | bytes 135176 | tf_op jit(solution)/shard_map/ppermute | solution.py:260
  47.5 13.0 %collective-permute-start.21 = (bf16[8,8,2904]{2,1,0:T(8,128)(2,1)S(1)}, bf16[8,8,2904]{2,1,0:T(8,128)(2,1)S(1)}, u32[]{:S(2)}, u32[]{:S(2)}) collective-permute-start(bf16[8,8,2904]{2,1,0:T(8,128)(2,1)S(1)} %all-to-all-done.mine_ref), channel_id=1, source_target_pairs={{0,2},{1,3},{2,0},{3,1},{4,6},{5,7},{6,4},{7,5},{8,10},{9,11},{10,... | collective-permute-start | bytes 1115144 | tf_op jit(solution)/shard_map/ppermute | solution.py:260
  50.7 4.7 %collective-permute-start.17 = (bf16[128,352]{1,0:T(8,128)(2,1)S(1)}, bf16[128,352]{1,0:T(8,128)(2,1)S(1)}, u32[]{:S(2)}, u32[]{:S(2)}) collective-permute-start(bf16[128,352]{1,0:T(8,128)(2,1)S(1)} %pad_maximum_fusion.5.mixed_ref), channel_id=1, source_target_pairs={{0,4},{1,5},{2,6},{3,7},{4,0},{5,1},{6,2},{7,3},{8,12},{9,13},{10,... | collective-permute-start | bytes 270344 | tf_op jit(solution)/shard_map/ppermute | solution.py:263
  50.8 9.5 %collective-permute-start.18 = (bf16[128,352]{1,0:T(8,128)(2,1)S(1)}, bf16[128,352]{1,0:T(8,128)(2,1)S(1)}, u32[]{:S(2)}, u32[]{:S(2)}) collective-permute-start(bf16[128,352]{1,0:T(8,128)(2,1)S(1)} %pad_maximum_fusion.5.mixed_ref), channel_id=1, source_target_pairs={{0,8},{1,9},{2,10},{3,11},{4,12},{5,13},{6,14},{7,15},{8,0},{9,1},... | collective-permute-start | bytes 270344 | tf_op jit(solution)/shard_map/ppermute | solution.py:263
  53.2 7.2 %collective-permute-start.19 = (bf16[128,352]{1,0:T(8,128)(2,1)S(1)}, bf16[128,352]{1,0:T(8,128)(2,1)S(1)}, u32[]{:S(2)}, u32[]{:S(2)}) collective-permute-start(bf16[128,352]{1,0:T(8,128)(2,1)S(1)} %pad_maximum_fusion.5.mixed_ref), channel_id=1, source_target_pairs={{0,12},{1,13},{2,14},{3,15},{4,8},{5,9},{6,10},{7,11},{8,4},{9,5},... | collective-permute-start | bytes 270344 | tf_op jit(solution)/shard_map/ppermute | solution.py:263
  60.5 1.8 %collective-permute-start.20 = (bf16[4,128,352]{2,1,0:T(8,128)(2,1)S(1)}, bf16[4,128,352]{2,1,0:T(8,128)(2,1)S(1)}, u32[]{:S(2)}, u32[]{:S(2)}) collective-permute-start(bf16[4,128,352]{2,1,0:T(8,128)(2,1)S(1)} %pad_maximum_fusion.same_ref), channel_id=1, source_target_pairs={{0,1},{1,0},{2,3},{3,2},{4,5},{5,4},{6,7},{7,6},{8,9},{9,8},{10,11... | collective-permute-start | bytes 1081352 | tf_op jit(solution)/shard_map/ppermute | solution.py:265
  61.6 13.4 %copy-start.3 = (bf16[704,88]{0,1:T(8,128)(2,1)S(1)}, bf16[704,88]{0,1:T(8,128)(2,1)}, u32[]{:S(2)}) copy-start(bf16[704,88]{0,1:T(8,128)(2,1)} %param.9) | copy-start | bytes 371716
  64.8 4.4 %collective-permute-start.22 = (bf16[64,352]{1,0:T(8,128)(2,1)S(1)}, bf16[64,352]{1,0:T(8,128)(2,1)S(1)}, u32[]{:S(2)}, u32[]{:S(2)}) collective-permute-start(bf16[64,352]{1,0:T(8,128)(2,1)S(1)} %shard_map.61), channel_id=1, source_target_pairs={{0,4},{1,5},{2,6},{3,7},{4,0},{5,1},{6,2},{7,3},{8,12},{9,13},{10,... | collective-permute-start | bytes 135176 | tf_op jit(solution)/shard_map/ppermute | solution.py:263
  66.4 6.5 %collective-permute-start.23 = (bf16[64,352]{1,0:T(8,128)(2,1)S(1)}, bf16[64,352]{1,0:T(8,128)(2,1)S(1)}, u32[]{:S(2)}, u32[]{:S(2)}) collective-permute-start(bf16[64,352]{1,0:T(8,128)(2,1)S(1)} %shard_map.61), channel_id=1, source_target_pairs={{0,8},{1,9},{2,10},{3,11},{4,12},{5,13},{6,14},{7,15},{8,0},{9,1},... | collective-permute-start | bytes 135176 | tf_op jit(solution)/shard_map/ppermute | solution.py:263
  67.5 6.0 %collective-permute-start.24 = (bf16[64,352]{1,0:T(8,128)(2,1)S(1)}, bf16[64,352]{1,0:T(8,128)(2,1)S(1)}, u32[]{:S(2)}, u32[]{:S(2)}) collective-permute-start(bf16[64,352]{1,0:T(8,128)(2,1)S(1)} %shard_map.61), channel_id=1, source_target_pairs={{0,12},{1,13},{2,14},{3,15},{4,8},{5,9},{6,10},{7,11},{8,4},{9,5},... | collective-permute-start | bytes 135176 | tf_op jit(solution)/shard_map/ppermute | solution.py:263
  73.5 1.5 %collective-permute-start.25 = (bf16[4,64,352]{2,1,0:T(8,128)(2,1)S(1)}, bf16[4,64,352]{2,1,0:T(8,128)(2,1)S(1)}, u32[]{:S(2)}, u32[]{:S(2)}) collective-permute-start(bf16[4,64,352]{2,1,0:T(8,128)(2,1)S(1)} %pad_maximum_fusion.4.same_ref), channel_id=1, source_target_pairs={{0,1},{1,0},{2,3},{3,2},{4,5},{5,4},{6,7},{7,6},{8,9},{9,8},{10,11... | collective-permute-start | bytes 540680 | tf_op jit(solution)/shard_map/ppermute | solution.py:265

commit v4 on v3

--- a/solution.py
+++ b/solution.py
@@ -154,7 +154,8 @@
     picked_ref[...] = jnp.dot(tokens, chosen, preferred_element_type=jnp.float32).astype(jnp.bfloat16)
 
 
-def spatial_kernel(at_ref, normed_ref, same_ref, cross_ref, same_y_ref, cross_y_ref, out_ref, wide_ref):
+def spatial_kernel(at_ref, tokens_same_ref, tokens_cross_ref, same_ref, cross_ref, same_y_ref, cross_y_ref, out_ref, picked_ref, wide_ref, normed_ref, all_ref):
+    tokens_kernel(at_ref, tokens_same_ref, tokens_cross_ref, normed_ref, picked_ref, all_ref)
     pieces = []
     for dy, same, cross in ((0, same_ref, cross_ref), (1, same_y_ref, cross_y_ref)):
         for d in range(4):
@@ -288,8 +289,10 @@
     same, all_y = lax.optimization_barrier((same, all_y))
     tokens = same, lax.ppermute(same, "seq", to(1))
     cross_y = lax.ppermute(all_y[:, 1], "seq", to(1))
-    normed, picked = call(tokens_kernel, (S(256, D), S(256, 176)), *tokens, scratch=[pltpu.VMEM((8, patches, D), bf)])
-    spatial = call(spatial_kernel, S(64, 352), normed, all_w, cross_w, all_y, cross_y, scratch=[wide])
+    spatial, picked = call(
+        spatial_kernel, (S(64, 352), S(256, 176)), *tokens, all_w, cross_w, all_y, cross_y,
+        scratch=[wide, pltpu.VMEM((256, D), bf), pltpu.VMEM((8, patches, D), bf)],
+    )
     same, cross = gather(spatial)
     same, two_w = lax.optimization_barrier((same, two_w))
     two_o = across(two_w)

time: 88.8 us -> 87.2 us (0.982)
  blocking collectives: 11.5 us -> 10.4 us
    ppermute x1, waiting for transfers between devices: 0.01 us -> 1.26 us  [head_body(): cross_y = lax.ppermute(all_y[:, 1], 'seq', to(1))]
    all_to_all x1, blocking collectives: 11.5 us -> 10.4 us  [head_body(): result = lax.all_to_all(result, 'seq', 0, 0, tiled=True)]
    ppermute x1, waiting for transfers between devices: 1.02 us -> 0.01 us  [head_body(): tokens = (same, lax.ppermute(same, 'seq', to(1)))]
    pallas_call x7 -> x6, Pallas kernels: 10 us -> 9.27 us  [call(): return kernel_call(body, shapes, len(args), list(scratch), True)(at, *args)]
  transfers between devices with their start and end apart: 27 -> 27, of which waited for: 15 -> 13; matrix products, arithmetic and copies ran while one was open for 1% -> 1% of each run, Pallas kernels for 7% -> 6%
where the time goes in v4:
time: 87.2 us; the launch traced here: 86.9 us
  starting transfers between devices  34.2 us (39%)
  waiting for transfers between devices  28.4 us (33%)
  Pallas kernels  11.1 us (13%)
  blocking collectives  10.4 us (12%)
  local copies, waits for them, and re-layouts  2.08 us (2%)
    ppermute x9, waiting for transfers between devices, gather(): far, mid, near = (lax.ppermute(a, 'seq', to(m)) for m in (12, 8, 4))  14.1 us
    ppermute x9, starting transfers between devices, gather(): far, mid, near = (lax.ppermute(a, 'seq', to(m)) for m in (12, 8, 4))  13.3 us
    all_to_all x1, blocking collectives, head_body(): result = lax.all_to_all(result, 'seq', 0, 0, tiled=True)  10.4 us
    pallas_call x6, Pallas kernels, call(): return kernel_call(body, shapes, len(args), list(scratch), True)(at, *args)  9.27 us
    ppermute x5, starting transfers between devices, head_body(): across = lambda a: lax.ppermute(a, 'seq', ACROSS_Y)  6.72 us
    ppermute x3, waiting for transfers between devices, head_body(): lax.ppermute(p, 'seq', to(m))  4.91 us
    ppermute x3, starting transfers between devices, head_body(): lax.ppermute(p, 'seq', to(m))  4.68 us
    ppermute x5, waiting for transfers between devices, head_body(): across = lambda a: lax.ppermute(a, 'seq', ACROSS_Y)  4.64 us
  transfers between devices with their start and end apart: 27, of which 13 were waited for; matrix products, arithmetic and copies ran while one was open for 1% of the time, Pallas kernels for 6%

profile of v4, /device:TPU:0, one launch (start us, length us, event | category | flops | bytes accessed | tf_op | source)
XLA Modules:
  0.0 86.9 jit_solution(13945350805798237500)
XLA Ops:
  0.0 3.0 %collective-permute-start.3 = (bf16[88,704]{1,0:T(8,128)(2,1)}, bf16[88,704]{1,0:T(8,128)(2,1)S(1)}, u32[]{:S(2)}, u32[]{:S(2)}) collective-permute-start(bf16[88,704]{1,0:T(8,128)(2,1)} %bitcast.33), channel_id=1, source_target_pairs={{0,2},{1,3},{2,0},{3,1},{4,6},{5,7},{6,4},{7,5},{8,10},{9,11},{10,... | collective-permute-start | bytes 371720 | tf_op jit(solution)/shard_map/ppermute | solution.py:261
  3.0 0.1 collective-permute-start.4
  3.0 0.1 pad_add_fusion.at_ref
  3.1 1.0 %copy-done = bf16[88,2112]{1,0:T(8,128)(2,1)S(1)} copy-done((bf16[88,2112]{1,0:T(8,128)(2,1)S(1)}, bf16[88,2112]{1,0:T(8,128)(2,1)}, u32[]{:S(2)}) %copy-start) | copy-done | bytes 371736
  4.1 0.9 %shard_map.55 = (bf16[2,8,2904]{2,1,0:T(8,128)(2,1)S(1)}, bf16[2,8,2904]{2,1,0:T(8,128)(2,1)S(1)}, bf16[2,8,2904]{2,1,0:T(8,128)(2,1)S(1)}, bf16[2,8,2904]{2,1,0:T(8,128)(2,1)S(1)}) custom-call(s32[3]{0:T(128)S(1)} %pad_add_fusion.at_ref, bf16[88,2112]{1,0:T(8,128)(2,1)S(1)} %copy-done), custom_call_target="tpu_custom_call" | custom-call | tf_op jit(solution)/shard_map/pallas_call | solution.py:269
  5.0 2.1 %collective-permute-start = (bf16[2,8,2904]{2,1,0:T(8,128)(2,1)S(1)}, bf16[2,8,2904]{2,1,0:T(8,128)(2,1)S(1)}, u32[]{:S(2)}, u32[]{:S(2)}) collective-permute-start(bf16[2,8,2904]{2,1,0:T(8,128)(2,1)S(1)} %get-tuple-element.24), channel_id=1, source_target_pairs={{0,4},{1,5},{2,6},{3,7},{4,0},{5,1},{6,2},{7,3},{8,12},{9,13},{10,... | collective-permute-start | bytes 278792 | tf_op jit(solution)/shard_map/ppermute | solution.py:278
  7.1 2.6 %collective-permute-start.1 = (bf16[2,8,2904]{2,1,0:T(8,128)(2,1)S(1)}, bf16[2,8,2904]{2,1,0:T(8,128)(2,1)S(1)}, u32[]{:S(2)}, u32[]{:S(2)}) collective-permute-start(bf16[2,8,2904]{2,1,0:T(8,128)(2,1)S(1)} %get-tuple-element.25), channel_id=1, source_target_pairs={{0,8},{1,9},{2,10},{3,11},{4,12},{5,13},{6,14},{7,15},{8,0},{9,1},... | collective-permute-start | bytes 278792 | tf_op jit(solution)/shard_map/ppermute | solution.py:278
  9.7 0.0 collective-permute-start.2
  9.7 1.0 %copy-done.1 = bf16[88,2112]{1,0:T(8,128)(2,1)S(1)} copy-done((bf16[88,2112]{1,0:T(8,128)(2,1)S(1)}, bf16[88,2112]{1,0:T(8,128)(2,1)}, u32[]{:S(2)}) %copy-start.1) | copy-done | bytes 371736
  10.7 1.1 %shard_map.56 = bf16[8,8,2904]{2,1,0:T(8,128)(2,1)} custom-call(bf16[88,2112]{1,0:T(8,128)(2,1)S(1)} %copy-done.1), custom_call_target="tpu_custom_call" | custom-call | tf_op jit(solution)/shard_map/pallas_call | solution.py:101
  11.7 0.0 collective-permute-done
  11.7 4.9 %collective-permute-done.1 = bf16[2,8,2904]{2,1,0:T(8,128)(2,1)S(1)} collective-permute-done((bf16[2,8,2904]{2,1,0:T(8,128)(2,1)S(1)}, bf16[2,8,2904]{2,1,0:T(8,128)(2,1)S(1)}, u32[]{:S(2)}, u32[]{:S(2)}) %collective-permute-start.1) | collective-permute-done | bytes 92960 | tf_op jit(solution)/shard_map/ppermute | solution.py:278
  16.6 0.0 collective-permute-done.2
  16.6 0.0 collective-permute-done.3.other_ref
  16.6 0.0 collective-permute-done.4.other_ref
  16.7 2.5 %collective-permute-start.7 = (bf16[32,1408]{1,0:T(8,128)(2,1)S(1)}, bf16[32,1408]{1,0:T(8,128)(2,1)S(1)}, u32[]{:S(2)}, u32[]{:S(2)}) collective-permute-start(bf16[32,1408]{1,0:T(8,128)(2,1)S(1)} %bitcast.45), channel_id=1, source_target_pairs={{0,12},{1,13},{2,14},{3,15},{4,8},{5,9},{6,10},{7,11},{8,4},{9,5},... | collective-permute-start | bytes 270344 | tf_op jit(solution)/shard_map/ppermute | solution.py:287
  19.2 0.6 collective-permute-start.6
  19.8 1.4 %collective-permute-start.5 = (bf16[32,1408]{1,0:T(8,128)(2,1)S(1)}, bf16[32,1408]{1,0:T(8,128)(2,1)S(1)}, u32[]{:S(2)}, u32[]{:S(2)}) collective-permute-start(bf16[32,1408]{1,0:T(8,128)(2,1)S(1)} %bitcast.47), channel_id=1, source_target_pairs={{0,4},{1,5},{2,6},{3,7},{4,0},{5,1},{6,2},{7,3},{8,12},{9,13},{10,... | collective-permute-start | bytes 270344 | tf_op jit(solution)/shard_map/ppermute | solution.py:287
  21.1 0.1 pad_maximum_fusion.1
  21.2 1.6 %collective-permute-start.8 = (bf16[4,2,8,2904]{3,2,0,1:T(8,128)(2,1)S(1)}, bf16[4,2,8,2904]{3,2,0,1:T(8,128)(2,1)S(1)}, u32[]{:S(2)}, u32[]{:S(2)}) collective-permute-start(bf16[4,2,8,2904]{3,2,0,1:T(8,128)(2,1)S(1)} %pad_maximum_fusion.1), channel_id=1, source_target_pairs={{0,2},{1,3},{2,0},{3,1},{4,6},{5,7},{6,4},{7,5},{8,10},{9,11},{10,... | collective-permute-start | bytes 1115144 | tf_op jit(solution)/shard_map/ppermute | solution.py:261
  22.8 3.8 %all-to-all-start = ((bf16[8,8,2904]{2,1,0:T(8,128)(2,1)}), bf16[8,8,2904]{2,1,0:T(8,128)(2,1)S(1)}, u32[]{:S(2)}, u32[]{:S(2)}) async-start(bf16[8,8,2904]{2,1,0:T(8,128)(2,1)} %shard_map.56), calls=%async_computation | async-start | bytes 753664 | tf_op jit(solution)/shard_map/all_to_all | solution.py:260
  26.5 0.5 collective-permute-start.10
  27.1 0.0 collective-permute-done.7
  27.1 0.1 pad_maximum_fusion.2.tokens_same_ref
  27.1 1.7 %collective-permute-done.8 = bf16[4,2,8,2904]{3,2,0,1:T(8,128)(2,1)S(1)} collective-permute-done((bf16[4,2,8,2904]{3,2,0,1:T(8,128)(2,1)S(1)}, bf16[4,2,8,2904]{3,2,0,1:T(8,128)(2,1)S(1)}, u32[]{:S(2)}, u32[]{:S(2)}) %collective-permute-start.8) | collective-permute-done | bytes 371744 | tf_op jit(solution)/shard_map/ppermute | solution.py:261
  28.9 0.6 collective-permute-start.11
  29.5 0.0 copy-start.2
  29.5 1.3 %collective-permute-done.11.cross_y_ref = bf16[4,8,2904]{2,1,0:T(8,128)(2,1)S(1)} collective-permute-done((bf16[4,8,2904]{2,1,0:T(8,128)(2,1)S(1)}, bf16[4,8,2904]{2,1,0:T(8,128)(2,1)S(1)}, u32[]{:S(2)}, u32[]{:S(2)}) %collective-permute-start.11) | collective-permute-done | bytes 185888 | tf_op jit(solution)/shard_map/ppermute | solution.py:291
  30.8 2.6 %shard_map.57 = (bf16[64,352]{1,0:T(8,128)(2,1)S(1)}, bf16[256,176]{1,0:T(8,128)(2,1)S(1)}) custom-call(s32[3]{0:T(128)S(1)} %pad_add_fusion.at_ref, bf16[4,32,1408]{2,1,0:T(8,128)(2,1)S(1)} %pad_maximum_fusion.2.tokens_same_ref, bf16[4,32,1408]{2,1,0:T(8,128)(2,1)S(1)} %collective-permute-done.9.tokens_cross_ref, bf16[4,2,8,2904]{3,2,1,0:T(8,128)(2,1)S(1)} %copy.6.same_ref, ...), custom_call_target="tpu_custom_call" | custom-call | tf_op jit(solution)/shard_map/pallas_call | solution.py:269
  33.4 2.5 %collective-permute-start.14 = (bf16[64,352]{1,0:T(8,128)(2,1)S(1)}, bf16[64,352]{1,0:T(8,128)(2,1)S(1)}, u32[]{:S(2)}, u32[]{:S(2)}) collective-permute-start(bf16[64,352]{1,0:T(8,128)(2,1)S(1)} %get-tuple-element.34), channel_id=1, source_target_pairs={{0,12},{1,13},{2,14},{3,15},{4,8},{5,9},{6,10},{7,11},{8,4},{9,5},... | collective-permute-start | bytes 135176 | tf_op jit(solution)/shard_map/ppermute | solution.py:264
  35.9 0.6 collective-permute-start.13
  36.5 1.3 %collective-permute-start.12 = (bf16[64,352]{1,0:T(8,128)(2,1)S(1)}, bf16[64,352]{1,0:T(8,128)(2,1)S(1)}, u32[]{:S(2)}, u32[]{:S(2)}) collective-permute-start(bf16[64,352]{1,0:T(8,128)(2,1)S(1)} %get-tuple-element.34), channel_id=1, source_target_pairs={{0,4},{1,5},{2,6},{3,7},{4,0},{5,1},{6,2},{7,3},{8,12},{9,13},{10,... | collective-permute-start | bytes 135176 | tf_op jit(solution)/shard_map/ppermute | solution.py:264
  37.8 1.8 %collective-permute-done.14 = bf16[64,352]{1,0:T(8,128)(2,1)S(1)} collective-permute-done((bf16[64,352]{1,0:T(8,128)(2,1)S(1)}, bf16[64,352]{1,0:T(8,128)(2,1)S(1)}, u32[]{:S(2)}, u32[]{:S(2)}) %collective-permute-start.14) | collective-permute-done | bytes 45088 | tf_op jit(solution)/shard_map/ppermute | solution.py:264
  39.6 3.4 %collective-permute-done.13 = bf16[64,352]{1,0:T(8,128)(2,1)S(1)} collective-permute-done((bf16[64,352]{1,0:T(8,128)(2,1)S(1)}, bf16[64,352]{1,0:T(8,128)(2,1)S(1)}, u32[]{:S(2)}, u32[]{:S(2)}) %collective-permute-start.13) | collective-permute-done | bytes 45088 | tf_op jit(solution)/shard_map/ppermute | solution.py:264
  43.0 0.1 pad_maximum_fusion.3.same_ref
  43.0 0.1 collective-permute-start.15
  43.1 1.4 %collective-permute-done.15.cross_ref = bf16[4,64,352]{2,1,0:T(8,128)(2,1)S(1)} collective-permute-done((bf16[4,64,352]{2,1,0:T(8,128)(2,1)S(1)}, bf16[4,64,352]{2,1,0:T(8,128)(2,1)S(1)}, u32[]{:S(2)}, u32[]{:S(2)}) %collective-permute-start.15) | collective-permute-done | bytes 180256 | tf_op jit(solution)/shard_map/ppermute | solution.py:266
  44.5 1.1 %shard_map.58 = (bf16[128,176]{1,0:T(8,128)(2,1)S(1)}, bf16[128,176]{1,0:T(8,128)(2,1)S(1)}) custom-call(s32[3]{0:T(128)S(1)} %pad_add_fusion.at_ref, bf16[4,64,352]{2,1,0:T(8,128)(2,1)S(1)} %pad_maximum_fusion.3.same_ref, bf16[4,64,352]{2,1,0:T(8,128)(2,1)S(1)} %collective-permute-done.15.cross_ref, bf16[256,176]{1,0:T(8,128)(2,1)S(1)} %get-tuple-element.37.picked_ref, ...), custom_call_target="tpu_custom_call" | custom-call | tf_op jit(solution)/shard_map/pallas_call | solution.py:269
  45.6 0.6 collective-permute-start.16
  46.2 1.5 %collective-permute-start.21 = (bf16[8,8,2904]{2,1,0:T(8,128)(2,1)S(1)}, bf16[8,8,2904]{2,1,0:T(8,128)(2,1)S(1)}, u32[]{:S(2)}, u32[]{:S(2)}) collective-permute-start(bf16[8,8,2904]{2,1,0:T(8,128)(2,1)S(1)} %all-to-all-done.mine_ref), channel_id=1, source_target_pairs={{0,2},{1,3},{2,0},{3,1},{4,6},{5,7},{6,4},{7,5},{8,10},{9,11},{10,... | collective-permute-start | bytes 1115144 | tf_op jit(solution)/shard_map/ppermute | solution.py:261
  47.7 2.9 %collective-permute-done.16 = bf16[128,176]{1,0:T(8,128)(2,1)S(1)} collective-permute-done((bf16[128,176]{1,0:T(8,128)(2,1)S(1)}, bf16[128,176]{1,0:T(8,128)(2,1)S(1)}, u32[]{:S(2)}, u32[]{:S(2)}) %collective-permute-start.16) | collective-permute-done | bytes 45088 | tf_op jit(solution)/shard_map/ppermute | solution.py:261
  50.6 0.1 pad_maximum_fusion.5.mixed_ref
  50.7 1.3 %collective-permute-start.19 = (bf16[128,352]{1,0:T(8,128)(2,1)S(1)}, bf16[128,352]{1,0:T(8,128)(2,1)S(1)}, u32[]{:S(2)}, u32[]{:S(2)}) collective-permute-start(bf16[128,352]{1,0:T(8,128)(2,1)S(1)} %pad_maximum_fusion.5.mixed_ref), channel_id=1, source_target_pairs={{0,12},{1,13},{2,14},{3,15},{4,8},{5,9},{6,10},{7,11},{8,4},{9,5},... | collective-permute-start | bytes 270344 | tf_op jit(solution)/shard_map/ppermute | solution.py:264
  52.0 0.2 collective-permute-start.18
  52.2 2.9 %collective-permute-start.17 = (bf16[128,352]{1,0:T(8,128)(2,1)S(1)}, bf16[128,352]{1,0:T(8,128)(2,1)S(1)}, u32[]{:S(2)}, u32[]{:S(2)}) collective-permute-start(bf16[128,352]{1,0:T(8,128)(2,1)S(1)} %pad_maximum_fusion.5.mixed_ref), channel_id=1, source_target_pairs={{0,4},{1,5},{2,6},{3,7},{4,0},{5,1},{6,2},{7,3},{8,12},{9,13},{10,... | collective-permute-start | bytes 270344 | tf_op jit(solution)/shard_map/ppermute | solution.py:264
  55.2 0.1 fusion
  55.3 2.6 %collective-permute-done.19 = bf16[128,352]{1,0:T(8,128)(2,1)S(1)} collective-permute-done((bf16[128,352]{1,0:T(8,128)(2,1)S(1)}, bf16[128,352]{1,0:T(8,128)(2,1)S(1)}, u32[]{:S(2)}, u32[]{:S(2)}) %collective-permute-start.19) | collective-permute-done | bytes 90144 | tf_op jit(solution)/shard_map/ppermute | solution.py:264
  57.9 3.0 %collective-permute-done.18 = bf16[128,352]{1,0:T(8,128)(2,1)S(1)} collective-permute-done((bf16[128,352]{1,0:T(8,128)(2,1)S(1)}, bf16[128,352]{1,0:T(8,128)(2,1)S(1)}, u32[]{:S(2)}, u32[]{:S(2)}) %collective-permute-start.18) | collective-permute-done | bytes 90144 | tf_op jit(solution)/shard_map/ppermute | solution.py:264
  60.8 0.1 pad_maximum_fusion.same_ref
  60.9 0.1 collective-permute-start.20
  61.0 1.0 %shard_map.59.w_ref = bf16[1408,264]{1,0:T(8,128)(2,1)S(1)} custom-call(s32[3]{0:T(128)S(1)} %pad_add_fusion.at_ref, bf16[8,8,2904]{2,1,0:T(8,128)(2,1)S(1)} %all-to-all-done.mine_ref, bf16[8,8,2904]{2,1,0:T(8,128)(2,1)S(1)} %collective-permute-done.21.theirs_ref), custom_call_target="tpu_custom_call" | custom-call | tf_op jit(solution)/shard_map/pallas_call | solution.py:269
  62.1 0.0 copy-start.3
  62.1 0.6 collective-permute-done.20.cross_ref
  62.7 2.5 %shard_map.60 = bf16[64,352]{1,0:T(8,128)(2,1)S(1)} custom-call(s32[3]{0:T(128)S(1)} %pad_add_fusion.at_ref, bf16[4,128,352]{2,1,0:T(8,128)(2,1)S(1)} %pad_maximum_fusion.same_ref, bf16[4,128,352]{2,1,0:T(8,128)(2,1)S(1)} %collective-permute-done.20.cross_ref, bf16[1408,264]{1,0:T(8,128)(2,1)S(1)} %shard_map.59.w_ref), custom_call_target="tpu_custom_call" | custom-call | tf_op jit(solution)/shard_map/pallas_call | solution.py:269
  65.3 1.3 %collective-permute-start.24 = (bf16[64,352]{1,0:T(8,128)(2,1)S(1)}, bf16[64,352]{1,0:T(8,128)(2,1)S(1)}, u32[]{:S(2)}, u32[]{:S(2)}) collective-permute-start(bf16[64,352]{1,0:T(8,128)(2,1)S(1)} %shard_map.60), channel_id=1, source_target_pairs={{0,12},{1,13},{2,14},{3,15},{4,8},{5,9},{6,10},{7,11},{8,4},{9,5},... | collective-permute-start | bytes 135176 | tf_op jit(solution)/shard_map/ppermute | solution.py:264
  66.6 3.1 %collective-permute-start.22 = (bf16[64,352]{1,0:T(8,128)(2,1)S(1)}, bf16[64,352]{1,0:T(8,128)(2,1)S(1)}, u32[]{:S(2)}, u32[]{:S(2)}) collective-permute-start(bf16[64,352]{1,0:T(8,128)(2,1)S(1)} %shard_map.60), channel_id=1, source_target_pairs={{0,4},{1,5},{2,6},{3,7},{4,0},{5,1},{6,2},{7,3},{8,12},{9,13},{10,... | collective-permute-start | bytes 135176 | tf_op jit(solution)/shard_map/ppermute | solution.py:264
  69.7 2.0 %collective-permute-done.24 = bf16[64,352]{1,0:T(8,128)(2,1)S(1)} collective-permute-done((bf16[64,352]{1,0:T(8,128)(2,1)S(1)}, bf16[64,352]{1,0:T(8,128)(2,1)S(1)}, u32[]{:S(2)}, u32[]{:S(2)}) %collective-permute-start.24) | collective-permute-done | bytes 45088 | tf_op jit(solution)/shard_map/ppermute | solution.py:264
  71.7 1.2 %collective-permute-done.23 = bf16[64,352]{1,0:T(8,128)(2,1)S(1)} collective-permute-done((bf16[64,352]{1,0:T(8,128)(2,1)S(1)}, bf16[64,352]{1,0:T(8,128)(2,1)S(1)}, u32[]{:S(2)}, u32[]{:S(2)}) %collective-permute-start.23) | collective-permute-done | bytes 45088 | tf_op jit(solution)/shard_map/ppermute | solution.py:264
  73.0 0.1 pad_maximum_fusion.4.same_ref
  73.0 0.1 collective-permute-start.25
  73.1 1.4 %collective-permute-done.25.cross_ref = bf16[4,64,352]{2,1,0:T(8,128)(2,1)S(1)} collective-permute-done((bf16[4,64,352]{2,1,0:T(8,128)(2,1)S(1)}, bf16[4,64,352]{2,1,0:T(8,128)(2,1)S(1)}, u32[]{:S(2)}, u32[]{:S(2)}) %collective-permute-start.25) | collective-permute-done | bytes 180256 | tf_op jit(solution)/shard_map/ppermute | solution.py:266
  74.5 1.2 %shard_map.61 = bf16[16,8,352]{2,1,0:T(8,128)(2,1)S(1)} custom-call(s32[3]{0:T(128)S(1)} %pad_add_fusion.at_ref, bf16[4,64,352]{2,1,0:T(8,128)(2,1)S(1)} %pad_maximum_fusion.4.same_ref, bf16[4,64,352]{2,1,0:T(8,128)(2,1)S(1)} %collective-permute-done.25.cross_ref, bf16[128,352]{1,0:T(8,128)(2,1)S(1)} %pad_maximum_fusion.5.mixed_ref, ...), custom_call_target="tpu_custom_call" | custom-call | tf_op jit(solution)/shard_map/pallas_call | solution.py:269
  75.7 10.4 %all_to_all.10.blocks_ref = bf16[16,8,352]{2,1,0:T(8,128)(2,1)S(1)} all-to-all(bf16[16,8,352]{2,1,0:T(8,128)(2,1)S(1)} %shard_map.61), channel_id=1, replica_groups=mesh['groups'=2,'seq'=16] {'seq'}, dimensions={0} | all-to-all | bytes 180224 | tf_op jit(solution)/shard_map/all_to_all | solution.py:306
  86.1 0.8 shard_map.62
  (21 shorter events, 0.1 us)
Async XLA Ops:
  0.0 16.7 %copy-start.4 = (bf16[1,32,1408]{2,1,0:T(8,128)(2,1)S(1)}, bf16[1,32,1408]{2,1,0:T(8,128)(2,1)}, u32[]{:S(2)}) copy-start(bf16[1,32,1408]{2,1,0:T(8,128)(2,1)} %param.5) | copy-start | bytes 270340
  0.0 16.6 %collective-permute-start.3 = (bf16[88,704]{1,0:T(8,128)(2,1)}, bf16[88,704]{1,0:T(8,128)(2,1)S(1)}, u32[]{:S(2)}, u32[]{:S(2)}) collective-permute-start(bf16[88,704]{1,0:T(8,128)(2,1)} %bitcast.33), channel_id=1, source_target_pairs={{0,2},{1,3},{2,0},{3,1},{4,6},{5,7},{6,4},{7,5},{8,10},{9,11},{10,... | collective-permute-start | bytes 371720 | tf_op jit(solution)/shard_map/ppermute | solution.py:261
  3.0 13.7 %collective-permute-start.4 = (bf16[88,704]{1,0:T(8,128)(2,1)}, bf16[88,704]{1,0:T(8,128)(2,1)S(1)}, u32[]{:S(2)}, u32[]{:S(2)}) collective-permute-start(bf16[88,704]{1,0:T(8,128)(2,1)} %bitcast.35), channel_id=1, source_target_pairs={{0,2},{1,3},{2,0},{3,1},{4,6},{5,7},{6,4},{7,5},{8,10},{9,11},{10,... | collective-permute-start | bytes 371720 | tf_op jit(solution)/shard_map/ppermute | solution.py:261
  3.1 1.0 %copy-start = (bf16[88,2112]{1,0:T(8,128)(2,1)S(1)}, bf16[88,2112]{1,0:T(8,128)(2,1)}, u32[]{:S(2)}) copy-start(bf16[88,2112]{1,0:T(8,128)(2,1)} %w_ref.2) | copy-start | bytes 1115140
  5.0 6.7 %collective-permute-start = (bf16[2,8,2904]{2,1,0:T(8,128)(2,1)S(1)}, bf16[2,8,2904]{2,1,0:T(8,128)(2,1)S(1)}, u32[]{:S(2)}, u32[]{:S(2)}) collective-permute-start(bf16[2,8,2904]{2,1,0:T(8,128)(2,1)S(1)} %get-tuple-element.24), channel_id=1, source_target_pairs={{0,4},{1,5},{2,6},{3,7},{4,0},{5,1},{6,2},{7,3},{8,12},{9,13},{10,... | collective-permute-start | bytes 278792 | tf_op jit(solution)/shard_map/ppermute | solution.py:278
  7.1 9.6 %collective-permute-start.1 = (bf16[2,8,2904]{2,1,0:T(8,128)(2,1)S(1)}, bf16[2,8,2904]{2,1,0:T(8,128)(2,1)S(1)}, u32[]{:S(2)}, u32[]{:S(2)}) collective-permute-start(bf16[2,8,2904]{2,1,0:T(8,128)(2,1)S(1)} %get-tuple-element.25), channel_id=1, source_target_pairs={{0,8},{1,9},{2,10},{3,11},{4,12},{5,13},{6,14},{7,15},{8,0},{9,1},... | collective-permute-start | bytes 278792 | tf_op jit(solution)/shard_map/ppermute | solution.py:278
  9.7 7.0 %collective-permute-start.2 = (bf16[2,8,2904]{2,1,0:T(8,128)(2,1)S(1)}, bf16[2,8,2904]{2,1,0:T(8,128)(2,1)S(1)}, u32[]{:S(2)}, u32[]{:S(2)}) collective-permute-start(bf16[2,8,2904]{2,1,0:T(8,128)(2,1)S(1)} %get-tuple-element.26), channel_id=1, source_target_pairs={{0,12},{1,13},{2,14},{3,15},{4,8},{5,9},{6,10},{7,11},{8,4},{9,5},... | collective-permute-start | bytes 278792 | tf_op jit(solution)/shard_map/ppermute | solution.py:278
  9.7 1.0 %copy-start.1 = (bf16[88,2112]{1,0:T(8,128)(2,1)S(1)}, bf16[88,2112]{1,0:T(8,128)(2,1)}, u32[]{:S(2)}) copy-start(bf16[88,2112]{1,0:T(8,128)(2,1)} %w_ref.3) | copy-start | bytes 1115140
  16.7 10.4 %collective-permute-start.7 = (bf16[32,1408]{1,0:T(8,128)(2,1)S(1)}, bf16[32,1408]{1,0:T(8,128)(2,1)S(1)}, u32[]{:S(2)}, u32[]{:S(2)}) collective-permute-start(bf16[32,1408]{1,0:T(8,128)(2,1)S(1)} %bitcast.45), channel_id=1, source_target_pairs={{0,12},{1,13},{2,14},{3,15},{4,8},{5,9},{6,10},{7,11},{8,4},{9,5},... | collective-permute-start | bytes 270344 | tf_op jit(solution)/shard_map/ppermute | solution.py:287
  19.2 7.9 %collective-permute-start.6 = (bf16[32,1408]{1,0:T(8,128)(2,1)S(1)}, bf16[32,1408]{1,0:T(8,128)(2,1)S(1)}, u32[]{:S(2)}, u32[]{:S(2)}) collective-permute-start(bf16[32,1408]{1,0:T(8,128)(2,1)S(1)} %bitcast.46), channel_id=1, source_target_pairs={{0,8},{1,9},{2,10},{3,11},{4,12},{5,13},{6,14},{7,15},{8,0},{9,1},... | collective-permute-start | bytes 270344 | tf_op jit(solution)/shard_map/ppermute | solution.py:287
  19.8 7.3 %collective-permute-start.5 = (bf16[32,1408]{1,0:T(8,128)(2,1)S(1)}, bf16[32,1408]{1,0:T(8,128)(2,1)S(1)}, u32[]{:S(2)}, u32[]{:S(2)}) collective-permute-start(bf16[32,1408]{1,0:T(8,128)(2,1)S(1)} %bitcast.47), channel_id=1, source_target_pairs={{0,4},{1,5},{2,6},{3,7},{4,0},{5,1},{6,2},{7,3},{8,12},{9,13},{10,... | collective-permute-start | bytes 270344 | tf_op jit(solution)/shard_map/ppermute | solution.py:287
  21.2 7.7 %collective-permute-start.8 = (bf16[4,2,8,2904]{3,2,0,1:T(8,128)(2,1)S(1)}, bf16[4,2,8,2904]{3,2,0,1:T(8,128)(2,1)S(1)}, u32[]{:S(2)}, u32[]{:S(2)}) collective-permute-start(bf16[4,2,8,2904]{3,2,0,1:T(8,128)(2,1)S(1)} %pad_maximum_fusion.1), channel_id=1, source_target_pairs={{0,2},{1,3},{2,0},{3,1},{4,6},{5,7},{6,4},{7,5},{8,10},{9,11},{10,... | collective-permute-start | bytes 1115144 | tf_op jit(solution)/shard_map/ppermute | solution.py:261
  22.8 20.3 %all-to-all-start = ((bf16[8,8,2904]{2,1,0:T(8,128)(2,1)}), bf16[8,8,2904]{2,1,0:T(8,128)(2,1)S(1)}, u32[]{:S(2)}, u32[]{:S(2)}) async-start(bf16[8,8,2904]{2,1,0:T(8,128)(2,1)} %shard_map.56), calls=%async_computation | async-start | bytes 753664 | tf_op jit(solution)/shard_map/all_to_all | solution.py:260
  26.5 3.0 %collective-permute-start.10 = (bf16[4,8,2904]{2,1,0:T(8,128)(2,1)S(1)}, bf16[4,8,2904]{2,1,0:T(8,128)(2,1)S(1)}, u32[]{:S(2)}, u32[]{:S(2)}) collective-permute-start(bf16[4,8,2904]{2,1,0:T(8,128)(2,1)S(1)} %slice_bitcast_fusion), channel_id=1, source_target_pairs={{0,1},{1,0},{2,3},{3,2},{4,5},{5,4},{6,7},{7,6},{8,9},{9,8},{10,11... | collective-permute-start | bytes 557576 | tf_op jit(solution)/shard_map/ppermute | solution.py:285
  28.9 1.9 %collective-permute-start.9 = (bf16[4,32,1408]{2,1,0:T(8,128)(2,1)S(1)}, bf16[4,32,1408]{2,1,0:T(8,128)(2,1)S(1)}, u32[]{:S(2)}, u32[]{:S(2)}) collective-permute-start(bf16[4,32,1408]{2,1,0:T(8,128)(2,1)S(1)} %pad_maximum_fusion.2.tokens_same_ref), channel_id=1, source_target_pairs={{0,1},{1,0},{2,3},{3,2},{4,5},{5,4},{6,7},{7,6},{8,9},{9,8},{10,11... | collective-permute-start | bytes 1081352 | tf_op jit(solution)/shard_map/ppermute | solution.py:290
  28.9 1.9 %collective-permute-start.11 = (bf16[4,8,2904]{2,1,0:T(8,128)(2,1)S(1)}, bf16[4,8,2904]{2,1,0:T(8,128)(2,1)S(1)}, u32[]{:S(2)}, u32[]{:S(2)}) collective-permute-start(bf16[4,8,2904]{2,1,0:T(8,128)(2,1)S(1)} %slice_bitcast_fusion.1), channel_id=1, source_target_pairs={{0,1},{1,0},{2,3},{3,2},{4,5},{5,4},{6,7},{7,6},{8,9},{9,8},{10,11... | collective-permute-start | bytes 557576 | tf_op jit(solution)/shard_map/ppermute | solution.py:291
  29.5 15.0 %copy-start.2 = (bf16[704,88]{0,1:T(8,128)(2,1)S(1)}, bf16[704,88]{0,1:T(8,128)(2,1)}, u32[]{:S(2)}) copy-start(bf16[704,88]{0,1:T(8,128)(2,1)} %param.7) | copy-start | bytes 371716
  33.4 6.2 %collective-permute-start.14 = (bf16[64,352]{1,0:T(8,128)(2,1)S(1)}, bf16[64,352]{1,0:T(8,128)(2,1)S(1)}, u32[]{:S(2)}, u32[]{:S(2)}) collective-permute-start(bf16[64,352]{1,0:T(8,128)(2,1)S(1)} %get-tuple-element.34), channel_id=1, source_target_pairs={{0,12},{1,13},{2,14},{3,15},{4,8},{5,9},{6,10},{7,11},{8,4},{9,5},... | collective-permute-start | bytes 135176 | tf_op jit(solution)/shard_map/ppermute | solution.py:264
  35.9 7.1 %collective-permute-start.13 = (bf16[64,352]{1,0:T(8,128)(2,1)S(1)}, bf16[64,352]{1,0:T(8,128)(2,1)S(1)}, u32[]{:S(2)}, u32[]{:S(2)}) collective-permute-start(bf16[64,352]{1,0:T(8,128)(2,1)S(1)} %get-tuple-element.34), channel_id=1, source_target_pairs={{0,8},{1,9},{2,10},{3,11},{4,12},{5,13},{6,14},{7,15},{8,0},{9,1},... | collective-permute-start | bytes 135176 | tf_op jit(solution)/shard_map/ppermute | solution.py:264
  36.5 6.5 %collective-permute-start.12 = (bf16[64,352]{1,0:T(8,128)(2,1)S(1)}, bf16[64,352]{1,0:T(8,128)(2,1)S(1)}, u32[]{:S(2)}, u32[]{:S(2)}) collective-permute-start(bf16[64,352]{1,0:T(8,128)(2,1)S(1)} %get-tuple-element.34), channel_id=1, source_target_pairs={{0,4},{1,5},{2,6},{3,7},{4,0},{5,1},{6,2},{7,3},{8,12},{9,13},{10,... | collective-permute-start | bytes 135176 | tf_op jit(solution)/shard_map/ppermute | solution.py:264
  43.0 1.5 %collective-permute-start.15 = (bf16[4,64,352]{2,1,0:T(8,128)(2,1)S(1)}, bf16[4,64,352]{2,1,0:T(8,128)(2,1)S(1)}, u32[]{:S(2)}, u32[]{:S(2)}) collective-permute-start(bf16[4,64,352]{2,1,0:T(8,128)(2,1)S(1)} %pad_maximum_fusion.3.same_ref), channel_id=1, source_target_pairs={{0,1},{1,0},{2,3},{3,2},{4,5},{5,4},{6,7},{7,6},{8,9},{9,8},{10,11... | collective-permute-start | bytes 540680 | tf_op jit(solution)/shard_map/ppermute | solution.py:266
  45.6 5.0 %collective-permute-start.16 = (bf16[128,176]{1,0:T(8,128)(2,1)S(1)}, bf16[128,176]{1,0:T(8,128)(2,1)S(1)}, u32[]{:S(2)}, u32[]{:S(2)}) collective-permute-start(bf16[128,176]{1,0:T(8,128)(2,1)S(1)} %get-tuple-element.40), channel_id=1, source_target_pairs={{0,2},{1,3},{2,0},{3,1},{4,6},{5,7},{6,4},{7,5},{8,10},{9,11},{10,... | collective-permute-start | bytes 135176 | tf_op jit(solution)/shard_map/ppermute | solution.py:261
  46.2 14.9 %collective-permute-start.21 = (bf16[8,8,2904]{2,1,0:T(8,128)(2,1)S(1)}, bf16[8,8,2904]{2,1,0:T(8,128)(2,1)S(1)}, u32[]{:S(2)}, u32[]{:S(2)}) collective-permute-start(bf16[8,8,2904]{2,1,0:T(8,128)(2,1)S(1)} %all-to-all-done.mine_ref), channel_id=1, source_target_pairs={{0,2},{1,3},{2,0},{3,1},{4,6},{5,7},{6,4},{7,5},{8,10},{9,11},{10,... | collective-permute-start | bytes 1115144 | tf_op jit(solution)/shard_map/ppermute | solution.py:261
  50.7 7.2 %collective-permute-start.19 = (bf16[128,352]{1,0:T(8,128)(2,1)S(1)}, bf16[128,352]{1,0:T(8,128)(2,1)S(1)}, u32[]{:S(2)}, u32[]{:S(2)}) collective-permute-start(bf16[128,352]{1,0:T(8,128)(2,1)S(1)} %pad_maximum_fusion.5.mixed_ref), channel_id=1, source_target_pairs={{0,12},{1,13},{2,14},{3,15},{4,8},{5,9},{6,10},{7,11},{8,4},{9,5},... | collective-permute-start | bytes 270344 | tf_op jit(solution)/shard_map/ppermute | solution.py:264
  52.0 8.8 %collective-permute-start.18 = (bf16[128,352]{1,0:T(8,128)(2,1)S(1)}, bf16[128,352]{1,0:T(8,128)(2,1)S(1)}, u32[]{:S(2)}, u32[]{:S(2)}) collective-permute-start(bf16[128,352]{1,0:T(8,128)(2,1)S(1)} %pad_maximum_fusion.5.mixed_ref), channel_id=1, source_target_pairs={{0,8},{1,9},{2,10},{3,11},{4,12},{5,13},{6,14},{7,15},{8,0},{9,1},... | collective-permute-start | bytes 270344 | tf_op jit(solution)/shard_map/ppermute | solution.py:264
  52.2 8.6 %collective-permute-start.17 = (bf16[128,352]{1,0:T(8,128)(2,1)S(1)}, bf16[128,352]{1,0:T(8,128)(2,1)S(1)}, u32[]{:S(2)}, u32[]{:S(2)}) collective-permute-start(bf16[128,352]{1,0:T(8,128)(2,1)S(1)} %pad_maximum_fusion.5.mixed_ref), channel_id=1, source_target_pairs={{0,4},{1,5},{2,6},{3,7},{4,0},{5,1},{6,2},{7,3},{8,12},{9,13},{10,... | collective-permute-start | bytes 270344 | tf_op jit(solution)/shard_map/ppermute | solution.py:264
  60.9 1.8 %collective-permute-start.20 = (bf16[4,128,352]{2,1,0:T(8,128)(2,1)S(1)}, bf16[4,128,352]{2,1,0:T(8,128)(2,1)S(1)}, u32[]{:S(2)}, u32[]{:S(2)}) collective-permute-start(bf16[4,128,352]{2,1,0:T(8,128)(2,1)S(1)} %pad_maximum_fusion.same_ref), channel_id=1, source_target_pairs={{0,1},{1,0},{2,3},{3,2},{4,5},{5,4},{6,7},{7,6},{8,9},{9,8},{10,11... | collective-permute-start | bytes 1081352 | tf_op jit(solution)/shard_map/ppermute | solution.py:266
  62.1 12.5 %copy-start.3 = (bf16[704,88]{0,1:T(8,128)(2,1)S(1)}, bf16[704,88]{0,1:T(8,128)(2,1)}, u32[]{:S(2)}) copy-start(bf16[704,88]{0,1:T(8,128)(2,1)} %param.9) | copy-start | bytes 371716
  65.3 6.5 %collective-permute-start.24 = (bf16[64,352]{1,0:T(8,128)(2,1)S(1)}, bf16[64,352]{1,0:T(8,128)(2,1)S(1)}, u32[]{:S(2)}, u32[]{:S(2)}) collective-permute-start(bf16[64,352]{1,0:T(8,128)(2,1)S(1)} %shard_map.60), channel_id=1, source_target_pairs={{0,12},{1,13},{2,14},{3,15},{4,8},{5,9},{6,10},{7,11},{8,4},{9,5},... | collective-permute-start | bytes 135176 | tf_op jit(solution)/shard_map/ppermute | solution.py:264
  66.6 6.4 %collective-permute-start.23 = (bf16[64,352]{1,0:T(8,128)(2,1)S(1)}, bf16[64,352]{1,0:T(8,128)(2,1)S(1)}, u32[]{:S(2)}, u32[]{:S(2)}) collective-permute-start(bf16[64,352]{1,0:T(8,128)(2,1)S(1)} %shard_map.60), channel_id=1, source_target_pairs={{0,8},{1,9},{2,10},{3,11},{4,12},{5,13},{6,14},{7,15},{8,0},{9,1},... | collective-permute-start | bytes 135176 | tf_op jit(solution)/shard_map/ppermute | solution.py:264
  66.6 6.4 %collective-permute-start.22 = (bf16[64,352]{1,0:T(8,128)(2,1)S(1)}, bf16[64,352]{1,0:T(8,128)(2,1)S(1)}, u32[]{:S(2)}, u32[]{:S(2)}) collective-permute-start(bf16[64,352]{1,0:T(8,128)(2,1)S(1)} %shard_map.60), channel_id=1, source_target_pairs={{0,4},{1,5},{2,6},{3,7},{4,0},{5,1},{6,2},{7,3},{8,12},{9,13},{10,... | collective-permute-start | bytes 135176 | tf_op jit(solution)/shard_map/ppermute | solution.py:264
  73.0 1.5 %collective-permute-start.25 = (bf16[4,64,352]{2,1,0:T(8,128)(2,1)S(1)}, bf16[4,64,352]{2,1,0:T(8,128)(2,1)S(1)}, u32[]{:S(2)}, u32[]{:S(2)}) collective-permute-start(bf16[4,64,352]{2,1,0:T(8,128)(2,1)S(1)} %pad_maximum_fusion.4.same_ref), channel_id=1, source_target_pairs={{0,1},{1,0},{2,3},{3,2},{4,5},{5,4},{6,7},{7,6},{8,9},{9,8},{10,11... | collective-permute-start | bytes 540680 | tf_op jit(solution)/shard_map/ppermute | solution.py:266

commit v5 on v4

--- a/solution.py
+++ b/solution.py
@@ -197,7 +197,8 @@
     out_ref[...] = wide_ref[...].astype(jnp.bfloat16)
 
 
-def temporal_kernel(at_ref, same_ref, cross_ref, w_ref, out_ref, all_ref):
+def temporal_kernel(at_ref, same_ref, cross_ref, mine_ref, theirs_ref, out_ref, all_ref, w_ref, wide_ref):
+    rows_kernel(at_ref, mine_ref, theirs_ref, w_ref, wide_ref)
     assemble(at_ref, same_ref, cross_ref, all_ref)
     own = jnp.concatenate([all_ref[j][:, :176] for j in range(8)], axis=1)
     other = jnp.concatenate([all_ref[j][:, 176:] for j in range(8)], axis=1)
@@ -298,9 +299,8 @@
     two_o = across(two_w)
     keep, send = call(mixed_kernel, (S(128, 176), S(128, 176)), same, cross, picked, so, so_o, scratch=[heads])
     mixed = jnp.concatenate([keep, across(send)], axis=1)
-    rows = call(rows_kernel, S(D, 264), two_w, two_o, scratch=[wide])
     temporal = call(
-        temporal_kernel, S(64, 352), *gather(mixed), rows, scratch=[pltpu.VMEM((8, 128, 352), bf)]
+        temporal_kernel, S(64, 352), *gather(mixed), two_w, two_o, scratch=[pltpu.VMEM((8, 128, 352), bf), pltpu.VMEM((D, 264), bf), wide]
     )
     result = call(result_kernel, S(16, 8, 352), *gather(temporal), mixed, to_, to_o, scratch=[heads])
     result = lax.all_to_all(result, "seq", 0, 0, tiled=True)

time: 87.2 us -> 87.4 us (level)
  waiting for transfers between devices: 28.4 us -> 30.4 us
  local copies, waits for them, and re-layouts: 2.08 us -> 1.09 us
    ppermute x3, waiting for transfers between devices: 3.49 us -> 4.54 us  [gather(): return (same, lax.ppermute(same, 'seq', to(1)))]
    unnamed x10, local copies, waits for them, and re-layouts: 2 us -> 1.01 us
    ppermute x3, waiting for transfers between devices: 4.91 us -> 5.9 us  [head_body(): lax.ppermute(p, 'seq', to(m))]
    pallas_call x6 -> x5, Pallas kernels: 9.27 us -> 8.44 us  [call(): return kernel_call(body, shapes, len(args), list(scratch), True)(at, *args)]
  transfers between devices with their start and end apart: 27 -> 27, of which waited for: 13 -> 13; matrix products, arithmetic and copies ran while one was open for 1% -> 1% of each run, Pallas kernels for 6% -> 5%
where the time goes in v5:
time: 87.4 us; the launch traced here: 87.1 us
  starting transfers between devices  34.2 us (39%)
  waiting for transfers between devices  30.4 us (35%)
  blocking collectives  10.4 us (12%)
  Pallas kernels  10.3 us (12%)
  local copies, waits for them, and re-layouts  1.09 us (1%)
    ppermute x9, waiting for transfers between devices, gather(): far, mid, near = (lax.ppermute(a, 'seq', to(m)) for m in (12, 8, 4))  14.1 us
    ppermute x9, starting transfers between devices, gather(): far, mid, near = (lax.ppermute(a, 'seq', to(m)) for m in (12, 8, 4))  13.3 us
    all_to_all x1, blocking collectives, head_body(): result = lax.all_to_all(result, 'seq', 0, 0, tiled=True)  10.4 us
    pallas_call x5, Pallas kernels, call(): return kernel_call(body, shapes, len(args), list(scratch), True)(at, *args)  8.44 us
    ppermute x5, starting transfers between devices, head_body(): across = lambda a: lax.ppermute(a, 'seq', ACROSS_Y)  6.69 us
    ppermute x3, waiting for transfers between devices, head_body(): lax.ppermute(p, 'seq', to(m))  5.9 us
    ppermute x3, starting transfers between devices, head_body(): lax.ppermute(p, 'seq', to(m))  4.71 us
    ppermute x5, waiting for transfers between devices, head_body(): across = lambda a: lax.ppermute(a, 'seq', ACROSS_Y)  4.64 us
  transfers between devices with their start and end apart: 27, of which 13 were waited for; matrix products, arithmetic and copies ran while one was open for 1% of the time, Pallas kernels for 5%

profile of v5, /device:TPU:0, one launch (start us, length us, event | category | flops | bytes accessed | tf_op | source)
XLA Modules:
  0.0 87.1 jit_solution(4176695046471543050)
XLA Ops:
  0.0 3.0 %collective-permute-start.3 = (bf16[88,704]{1,0:T(8,128)(2,1)}, bf16[88,704]{1,0:T(8,128)(2,1)S(1)}, u32[]{:S(2)}, u32[]{:S(2)}) collective-permute-start(bf16[88,704]{1,0:T(8,128)(2,1)} %bitcast.33), channel_id=1, source_target_pairs={{0,2},{1,3},{2,0},{3,1},{4,6},{5,7},{6,4},{7,5},{8,10},{9,11},{10,... | collective-permute-start | bytes 371720 | tf_op jit(solution)/shard_map/ppermute | solution.py:262
  3.0 0.0 collective-permute-start.4
  3.0 0.1 pad_add_fusion.at_ref
  3.1 1.0 %copy-done = bf16[88,2112]{1,0:T(8,128)(2,1)S(1)} copy-done((bf16[88,2112]{1,0:T(8,128)(2,1)S(1)}, bf16[88,2112]{1,0:T(8,128)(2,1)}, u32[]{:S(2)}) %copy-start) | copy-done | bytes 371736
  4.1 0.9 %shard_map.55 = (bf16[2,8,2904]{2,1,0:T(8,128)(2,1)S(1)}, bf16[2,8,2904]{2,1,0:T(8,128)(2,1)S(1)}, bf16[2,8,2904]{2,1,0:T(8,128)(2,1)S(1)}, bf16[2,8,2904]{2,1,0:T(8,128)(2,1)S(1)}) custom-call(s32[3]{0:T(128)S(1)} %pad_add_fusion.at_ref, bf16[88,2112]{1,0:T(8,128)(2,1)S(1)} %copy-done), custom_call_target="tpu_custom_call" | custom-call | tf_op jit(solution)/shard_map/pallas_call | solution.py:270
  5.0 2.1 %collective-permute-start = (bf16[2,8,2904]{2,1,0:T(8,128)(2,1)S(1)}, bf16[2,8,2904]{2,1,0:T(8,128)(2,1)S(1)}, u32[]{:S(2)}, u32[]{:S(2)}) collective-permute-start(bf16[2,8,2904]{2,1,0:T(8,128)(2,1)S(1)} %get-tuple-element.24), channel_id=1, source_target_pairs={{0,4},{1,5},{2,6},{3,7},{4,0},{5,1},{6,2},{7,3},{8,12},{9,13},{10,... | collective-permute-start | bytes 278792 | tf_op jit(solution)/shard_map/ppermute | solution.py:279
  7.1 2.6 %collective-permute-start.1 = (bf16[2,8,2904]{2,1,0:T(8,128)(2,1)S(1)}, bf16[2,8,2904]{2,1,0:T(8,128)(2,1)S(1)}, u32[]{:S(2)}, u32[]{:S(2)}) collective-permute-start(bf16[2,8,2904]{2,1,0:T(8,128)(2,1)S(1)} %get-tuple-element.25), channel_id=1, source_target_pairs={{0,8},{1,9},{2,10},{3,11},{4,12},{5,13},{6,14},{7,15},{8,0},{9,1},... | collective-permute-start | bytes 278792 | tf_op jit(solution)/shard_map/ppermute | solution.py:279
  9.7 0.0 collective-permute-start.2
  9.7 1.1 %shard_map.56 = bf16[8,8,2904]{2,1,0:T(8,128)(2,1)} custom-call(bf16[88,2112]{1,0:T(8,128)(2,1)S(1)} %copy-done.1), custom_call_target="tpu_custom_call" | custom-call | tf_op jit(solution)/shard_map/pallas_call | solution.py:101
  10.8 5.9 %collective-permute-done.1 = bf16[2,8,2904]{2,1,0:T(8,128)(2,1)S(1)} collective-permute-done((bf16[2,8,2904]{2,1,0:T(8,128)(2,1)S(1)}, bf16[2,8,2904]{2,1,0:T(8,128)(2,1)S(1)}, u32[]{:S(2)}, u32[]{:S(2)}) %collective-permute-start.1) | collective-permute-done | bytes 92960 | tf_op jit(solution)/shard_map/ppermute | solution.py:279
  16.6 0.0 collective-permute-done.2
  16.6 0.0 collective-permute-done.3.other_ref
  16.6 0.0 collective-permute-done.4.other_ref
  16.7 2.5 %collective-permute-start.7 = (bf16[32,1408]{1,0:T(8,128)(2,1)S(1)}, bf16[32,1408]{1,0:T(8,128)(2,1)S(1)}, u32[]{:S(2)}, u32[]{:S(2)}) collective-permute-start(bf16[32,1408]{1,0:T(8,128)(2,1)S(1)} %bitcast.45), channel_id=1, source_target_pairs={{0,12},{1,13},{2,14},{3,15},{4,8},{5,9},{6,10},{7,11},{8,4},{9,5},... | collective-permute-start | bytes 270344 | tf_op jit(solution)/shard_map/ppermute | solution.py:288
  19.2 0.6 collective-permute-start.6
  19.8 1.4 %collective-permute-start.5 = (bf16[32,1408]{1,0:T(8,128)(2,1)S(1)}, bf16[32,1408]{1,0:T(8,128)(2,1)S(1)}, u32[]{:S(2)}, u32[]{:S(2)}) collective-permute-start(bf16[32,1408]{1,0:T(8,128)(2,1)S(1)} %bitcast.47), channel_id=1, source_target_pairs={{0,4},{1,5},{2,6},{3,7},{4,0},{5,1},{6,2},{7,3},{8,12},{9,13},{10,... | collective-permute-start | bytes 270344 | tf_op jit(solution)/shard_map/ppermute | solution.py:288
  21.1 0.1 pad_maximum_fusion.1
  21.2 1.6 %collective-permute-start.8 = (bf16[4,2,8,2904]{3,2,0,1:T(8,128)(2,1)S(1)}, bf16[4,2,8,2904]{3,2,0,1:T(8,128)(2,1)S(1)}, u32[]{:S(2)}, u32[]{:S(2)}) collective-permute-start(bf16[4,2,8,2904]{3,2,0,1:T(8,128)(2,1)S(1)} %pad_maximum_fusion.1), channel_id=1, source_target_pairs={{0,2},{1,3},{2,0},{3,1},{4,6},{5,7},{6,4},{7,5},{8,10},{9,11},{10,... | collective-permute-start | bytes 1115144 | tf_op jit(solution)/shard_map/ppermute | solution.py:262
  22.8 3.8 %all-to-all-start = ((bf16[8,8,2904]{2,1,0:T(8,128)(2,1)}), bf16[8,8,2904]{2,1,0:T(8,128)(2,1)S(1)}, u32[]{:S(2)}, u32[]{:S(2)}) async-start(bf16[8,8,2904]{2,1,0:T(8,128)(2,1)} %shard_map.56), calls=%async_computation | async-start | bytes 753664 | tf_op jit(solution)/shard_map/all_to_all | solution.py:261
  26.5 0.5 collective-permute-start.10
  27.1 0.1 pad_maximum_fusion.2.tokens_same_ref
  27.1 1.7 %collective-permute-done.8 = bf16[4,2,8,2904]{3,2,0,1:T(8,128)(2,1)S(1)} collective-permute-done((bf16[4,2,8,2904]{3,2,0,1:T(8,128)(2,1)S(1)}, bf16[4,2,8,2904]{3,2,0,1:T(8,128)(2,1)S(1)}, u32[]{:S(2)}, u32[]{:S(2)}) %collective-permute-start.8) | collective-permute-done | bytes 371744 | tf_op jit(solution)/shard_map/ppermute | solution.py:262
  28.9 0.0 collective-permute-start.9
  28.9 0.6 collective-permute-start.11
  29.5 1.3 %collective-permute-done.11.cross_y_ref = bf16[4,8,2904]{2,1,0:T(8,128)(2,1)S(1)} collective-permute-done((bf16[4,8,2904]{2,1,0:T(8,128)(2,1)S(1)}, bf16[4,8,2904]{2,1,0:T(8,128)(2,1)S(1)}, u32[]{:S(2)}, u32[]{:S(2)}) %collective-permute-start.11) | collective-permute-done | bytes 185888 | tf_op jit(solution)/shard_map/ppermute | solution.py:292
  30.8 0.0 collective-permute-done.9.tokens_cross_ref
  30.8 2.6 %shard_map.57 = (bf16[64,352]{1,0:T(8,128)(2,1)S(1)}, bf16[256,176]{1,0:T(8,128)(2,1)S(1)}) custom-call(s32[3]{0:T(128)S(1)} %pad_add_fusion.at_ref, bf16[4,32,1408]{2,1,0:T(8,128)(2,1)S(1)} %pad_maximum_fusion.2.tokens_same_ref, bf16[4,32,1408]{2,1,0:T(8,128)(2,1)S(1)} %collective-permute-done.9.tokens_cross_ref, bf16[4,2,8,2904]{3,2,1,0:T(8,128)(2,1)S(1)} %copy.6.same_ref, ...), custom_call_target="tpu_custom_call" | custom-call | tf_op jit(solution)/shard_map/pallas_call | solution.py:270
  33.4 2.5 %collective-permute-start.14 = (bf16[64,352]{1,0:T(8,128)(2,1)S(1)}, bf16[64,352]{1,0:T(8,128)(2,1)S(1)}, u32[]{:S(2)}, u32[]{:S(2)}) collective-permute-start(bf16[64,352]{1,0:T(8,128)(2,1)S(1)} %get-tuple-element.34), channel_id=1, source_target_pairs={{0,12},{1,13},{2,14},{3,15},{4,8},{5,9},{6,10},{7,11},{8,4},{9,5},... | collective-permute-start | bytes 135176 | tf_op jit(solution)/shard_map/ppermute | solution.py:265
  35.9 0.6 collective-permute-start.13
  36.5 1.3 %collective-permute-start.12 = (bf16[64,352]{1,0:T(8,128)(2,1)S(1)}, bf16[64,352]{1,0:T(8,128)(2,1)S(1)}, u32[]{:S(2)}, u32[]{:S(2)}) collective-permute-start(bf16[64,352]{1,0:T(8,128)(2,1)S(1)} %get-tuple-element.34), channel_id=1, source_target_pairs={{0,4},{1,5},{2,6},{3,7},{4,0},{5,1},{6,2},{7,3},{8,12},{9,13},{10,... | collective-permute-start | bytes 135176 | tf_op jit(solution)/shard_map/ppermute | solution.py:265
  37.8 1.8 %collective-permute-done.14 = bf16[64,352]{1,0:T(8,128)(2,1)S(1)} collective-permute-done((bf16[64,352]{1,0:T(8,128)(2,1)S(1)}, bf16[64,352]{1,0:T(8,128)(2,1)S(1)}, u32[]{:S(2)}, u32[]{:S(2)}) %collective-permute-start.14) | collective-permute-done | bytes 45088 | tf_op jit(solution)/shard_map/ppermute | solution.py:265
  39.6 3.4 %collective-permute-done.13 = bf16[64,352]{1,0:T(8,128)(2,1)S(1)} collective-permute-done((bf16[64,352]{1,0:T(8,128)(2,1)S(1)}, bf16[64,352]{1,0:T(8,128)(2,1)S(1)}, u32[]{:S(2)}, u32[]{:S(2)}) %collective-permute-start.13) | collective-permute-done | bytes 45088 | tf_op jit(solution)/shard_map/ppermute | solution.py:265
  43.0 0.0 collective-permute-done.12
  43.0 0.1 pad_maximum_fusion.3.same_ref
  43.0 0.1 collective-permute-start.15
  43.1 0.0 all-to-all-done.mine_ref
  43.1 1.4 %collective-permute-done.15.cross_ref = bf16[4,64,352]{2,1,0:T(8,128)(2,1)S(1)} collective-permute-done((bf16[4,64,352]{2,1,0:T(8,128)(2,1)S(1)}, bf16[4,64,352]{2,1,0:T(8,128)(2,1)S(1)}, u32[]{:S(2)}, u32[]{:S(2)}) %collective-permute-start.15) | collective-permute-done | bytes 180256 | tf_op jit(solution)/shard_map/ppermute | solution.py:267
  44.5 1.1 %shard_map.58 = (bf16[128,176]{1,0:T(8,128)(2,1)S(1)}, bf16[128,176]{1,0:T(8,128)(2,1)S(1)}) custom-call(s32[3]{0:T(128)S(1)} %pad_add_fusion.at_ref, bf16[4,64,352]{2,1,0:T(8,128)(2,1)S(1)} %pad_maximum_fusion.3.same_ref, bf16[4,64,352]{2,1,0:T(8,128)(2,1)S(1)} %collective-permute-done.15.cross_ref, bf16[256,176]{1,0:T(8,128)(2,1)S(1)} %get-tuple-element.37.picked_ref, ...), custom_call_target="tpu_custom_call" | custom-call | tf_op jit(solution)/shard_map/pallas_call | solution.py:270
  45.6 0.6 collective-permute-start.16
  46.2 1.5 %collective-permute-start.21 = (bf16[8,8,2904]{2,1,0:T(8,128)(2,1)S(1)}, bf16[8,8,2904]{2,1,0:T(8,128)(2,1)S(1)}, u32[]{:S(2)}, u32[]{:S(2)}) collective-permute-start(bf16[8,8,2904]{2,1,0:T(8,128)(2,1)S(1)} %all-to-all-done.mine_ref), channel_id=1, source_target_pairs={{0,2},{1,3},{2,0},{3,1},{4,6},{5,7},{6,4},{7,5},{8,10},{9,11},{10,... | collective-permute-start | bytes 1115144 | tf_op jit(solution)/shard_map/ppermute | solution.py:262
  47.7 2.9 %collective-permute-done.16 = bf16[128,176]{1,0:T(8,128)(2,1)S(1)} collective-permute-done((bf16[128,176]{1,0:T(8,128)(2,1)S(1)}, bf16[128,176]{1,0:T(8,128)(2,1)S(1)}, u32[]{:S(2)}, u32[]{:S(2)}) %collective-permute-start.16) | collective-permute-done | bytes 45088 | tf_op jit(solution)/shard_map/ppermute | solution.py:262
  50.6 0.1 pad_maximum_fusion.5.mixed_ref
  50.7 1.3 %collective-permute-start.19 = (bf16[128,352]{1,0:T(8,128)(2,1)S(1)}, bf16[128,352]{1,0:T(8,128)(2,1)S(1)}, u32[]{:S(2)}, u32[]{:S(2)}) collective-permute-start(bf16[128,352]{1,0:T(8,128)(2,1)S(1)} %pad_maximum_fusion.5.mixed_ref), channel_id=1, source_target_pairs={{0,12},{1,13},{2,14},{3,15},{4,8},{5,9},{6,10},{7,11},{8,4},{9,5},... | collective-permute-start | bytes 270344 | tf_op jit(solution)/shard_map/ppermute | solution.py:265
  52.1 0.2 collective-permute-start.18
  52.2 2.9 %collective-permute-start.17 = (bf16[128,352]{1,0:T(8,128)(2,1)S(1)}, bf16[128,352]{1,0:T(8,128)(2,1)S(1)}, u32[]{:S(2)}, u32[]{:S(2)}) collective-permute-start(bf16[128,352]{1,0:T(8,128)(2,1)S(1)} %pad_maximum_fusion.5.mixed_ref), channel_id=1, source_target_pairs={{0,4},{1,5},{2,6},{3,7},{4,0},{5,1},{6,2},{7,3},{8,12},{9,13},{10,... | collective-permute-start | bytes 270344 | tf_op jit(solution)/shard_map/ppermute | solution.py:265
  55.2 0.1 fusion
  55.3 2.6 %collective-permute-done.19 = bf16[128,352]{1,0:T(8,128)(2,1)S(1)} collective-permute-done((bf16[128,352]{1,0:T(8,128)(2,1)S(1)}, bf16[128,352]{1,0:T(8,128)(2,1)S(1)}, u32[]{:S(2)}, u32[]{:S(2)}) %collective-permute-start.19) | collective-permute-done | bytes 90144 | tf_op jit(solution)/shard_map/ppermute | solution.py:265
  57.9 3.0 %collective-permute-done.18 = bf16[128,352]{1,0:T(8,128)(2,1)S(1)} collective-permute-done((bf16[128,352]{1,0:T(8,128)(2,1)S(1)}, bf16[128,352]{1,0:T(8,128)(2,1)S(1)}, u32[]{:S(2)}, u32[]{:S(2)}) %collective-permute-start.18) | collective-permute-done | bytes 90144 | tf_op jit(solution)/shard_map/ppermute | solution.py:265
  60.9 0.1 pad_maximum_fusion.same_ref
  61.0 0.1 collective-permute-start.20
  61.0 1.7 %collective-permute-done.20.cross_ref = bf16[4,128,352]{2,1,0:T(8,128)(2,1)S(1)} collective-permute-done((bf16[4,128,352]{2,1,0:T(8,128)(2,1)S(1)}, bf16[4,128,352]{2,1,0:T(8,128)(2,1)S(1)}, u32[]{:S(2)}, u32[]{:S(2)}) %collective-permute-start.20) | collective-permute-done | bytes 360480 | tf_op jit(solution)/shard_map/ppermute | solution.py:267
  62.7 2.7 %shard_map.59 = bf16[64,352]{1,0:T(8,128)(2,1)S(1)} custom-call(s32[3]{0:T(128)S(1)} %pad_add_fusion.at_ref, bf16[4,128,352]{2,1,0:T(8,128)(2,1)S(1)} %pad_maximum_fusion.same_ref, bf16[4,128,352]{2,1,0:T(8,128)(2,1)S(1)} %collective-permute-done.20.cross_ref, bf16[8,8,2904]{2,1,0:T(8,128)(2,1)S(1)} %all-to-all-done.mine_ref, ...), custom_call_target="tpu_custom_call" | custom-call | tf_op jit(solution)/shard_map/pallas_call | solution.py:270
  65.5 1.3 %collective-permute-start.24 = (bf16[64,352]{1,0:T(8,128)(2,1)S(1)}, bf16[64,352]{1,0:T(8,128)(2,1)S(1)}, u32[]{:S(2)}, u32[]{:S(2)}) collective-permute-start(bf16[64,352]{1,0:T(8,128)(2,1)S(1)} %shard_map.59), channel_id=1, source_target_pairs={{0,12},{1,13},{2,14},{3,15},{4,8},{5,9},{6,10},{7,11},{8,4},{9,5},... | collective-permute-start | bytes 135176 | tf_op jit(solution)/shard_map/ppermute | solution.py:265
  66.8 0.0 collective-permute-start.23
  66.8 3.1 %collective-permute-start.22 = (bf16[64,352]{1,0:T(8,128)(2,1)S(1)}, bf16[64,352]{1,0:T(8,128)(2,1)S(1)}, u32[]{:S(2)}, u32[]{:S(2)}) collective-permute-start(bf16[64,352]{1,0:T(8,128)(2,1)S(1)} %shard_map.59), channel_id=1, source_target_pairs={{0,4},{1,5},{2,6},{3,7},{4,0},{5,1},{6,2},{7,3},{8,12},{9,13},{10,... | collective-permute-start | bytes 135176 | tf_op jit(solution)/shard_map/ppermute | solution.py:265
  69.9 2.0 %collective-permute-done.24 = bf16[64,352]{1,0:T(8,128)(2,1)S(1)} collective-permute-done((bf16[64,352]{1,0:T(8,128)(2,1)S(1)}, bf16[64,352]{1,0:T(8,128)(2,1)S(1)}, u32[]{:S(2)}, u32[]{:S(2)}) %collective-permute-start.24) | collective-permute-done | bytes 45088 | tf_op jit(solution)/shard_map/ppermute | solution.py:265
  71.9 1.3 %collective-permute-done.23 = bf16[64,352]{1,0:T(8,128)(2,1)S(1)} collective-permute-done((bf16[64,352]{1,0:T(8,128)(2,1)S(1)}, bf16[64,352]{1,0:T(8,128)(2,1)S(1)}, u32[]{:S(2)}, u32[]{:S(2)}) %collective-permute-start.23) | collective-permute-done | bytes 45088 | tf_op jit(solution)/shard_map/ppermute | solution.py:265
  73.2 0.0 collective-permute-done.22
  73.2 0.1 pad_maximum_fusion.4.same_ref
  73.3 0.1 collective-permute-start.25
  73.3 1.4 %collective-permute-done.25.cross_ref = bf16[4,64,352]{2,1,0:T(8,128)(2,1)S(1)} collective-permute-done((bf16[4,64,352]{2,1,0:T(8,128)(2,1)S(1)}, bf16[4,64,352]{2,1,0:T(8,128)(2,1)S(1)}, u32[]{:S(2)}, u32[]{:S(2)}) %collective-permute-start.25) | collective-permute-done | bytes 180256 | tf_op jit(solution)/shard_map/ppermute | solution.py:267
  74.8 1.2 %shard_map.60 = bf16[16,8,352]{2,1,0:T(8,128)(2,1)S(1)} custom-call(s32[3]{0:T(128)S(1)} %pad_add_fusion.at_ref, bf16[4,64,352]{2,1,0:T(8,128)(2,1)S(1)} %pad_maximum_fusion.4.same_ref, bf16[4,64,352]{2,1,0:T(8,128)(2,1)S(1)} %collective-permute-done.25.cross_ref, bf16[128,352]{1,0:T(8,128)(2,1)S(1)} %pad_maximum_fusion.5.mixed_ref, ...), custom_call_target="tpu_custom_call" | custom-call | tf_op jit(solution)/shard_map/pallas_call | solution.py:270
  76.0 10.4 %all_to_all.10.blocks_ref = bf16[16,8,352]{2,1,0:T(8,128)(2,1)S(1)} all-to-all(bf16[16,8,352]{2,1,0:T(8,128)(2,1)S(1)} %shard_map.60), channel_id=1, replica_groups=mesh['groups'=2,'seq'=16] {'seq'}, dimensions={0} | all-to-all | bytes 180224 | tf_op jit(solution)/shard_map/all_to_all | solution.py:306
  86.3 0.8 shard_map.61
  (20 shorter events, 0.1 us)
Async XLA Ops:
  0.0 16.6 %collective-permute-start.3 = (bf16[88,704]{1,0:T(8,128)(2,1)}, bf16[88,704]{1,0:T(8,128)(2,1)S(1)}, u32[]{:S(2)}, u32[]{:S(2)}) collective-permute-start(bf16[88,704]{1,0:T(8,128)(2,1)} %bitcast.33), channel_id=1, source_target_pairs={{0,2},{1,3},{2,0},{3,1},{4,6},{5,7},{6,4},{7,5},{8,10},{9,11},{10,... | collective-permute-start | bytes 371720 | tf_op jit(solution)/shard_map/ppermute | solution.py:262
  3.0 13.7 %collective-permute-start.4 = (bf16[88,704]{1,0:T(8,128)(2,1)}, bf16[88,704]{1,0:T(8,128)(2,1)S(1)}, u32[]{:S(2)}, u32[]{:S(2)}) collective-permute-start(bf16[88,704]{1,0:T(8,128)(2,1)} %bitcast.35), channel_id=1, source_target_pairs={{0,2},{1,3},{2,0},{3,1},{4,6},{5,7},{6,4},{7,5},{8,10},{9,11},{10,... | collective-permute-start | bytes 371720 | tf_op jit(solution)/shard_map/ppermute | solution.py:262
  3.1 1.0 %copy-start = (bf16[88,2112]{1,0:T(8,128)(2,1)S(1)}, bf16[88,2112]{1,0:T(8,128)(2,1)}, u32[]{:S(2)}) copy-start(bf16[88,2112]{1,0:T(8,128)(2,1)} %w_ref.2) | copy-start | bytes 1115140
  4.1 5.6 %copy-start.1 = (bf16[88,2112]{1,0:T(8,128)(2,1)S(1)}, bf16[88,2112]{1,0:T(8,128)(2,1)}, u32[]{:S(2)}) copy-start(bf16[88,2112]{1,0:T(8,128)(2,1)} %w_ref.3) | copy-start | bytes 1115140
  5.0 5.8 %collective-permute-start = (bf16[2,8,2904]{2,1,0:T(8,128)(2,1)S(1)}, bf16[2,8,2904]{2,1,0:T(8,128)(2,1)S(1)}, u32[]{:S(2)}, u32[]{:S(2)}) collective-permute-start(bf16[2,8,2904]{2,1,0:T(8,128)(2,1)S(1)} %get-tuple-element.24), channel_id=1, source_target_pairs={{0,4},{1,5},{2,6},{3,7},{4,0},{5,1},{6,2},{7,3},{8,12},{9,13},{10,... | collective-permute-start | bytes 278792 | tf_op jit(solution)/shard_map/ppermute | solution.py:279
  7.1 9.6 %collective-permute-start.1 = (bf16[2,8,2904]{2,1,0:T(8,128)(2,1)S(1)}, bf16[2,8,2904]{2,1,0:T(8,128)(2,1)S(1)}, u32[]{:S(2)}, u32[]{:S(2)}) collective-permute-start(bf16[2,8,2904]{2,1,0:T(8,128)(2,1)S(1)} %get-tuple-element.25), channel_id=1, source_target_pairs={{0,8},{1,9},{2,10},{3,11},{4,12},{5,13},{6,14},{7,15},{8,0},{9,1},... | collective-permute-start | bytes 278792 | tf_op jit(solution)/shard_map/ppermute | solution.py:279
  9.7 7.0 %copy-start.4 = (bf16[1,32,1408]{2,1,0:T(8,128)(2,1)S(1)}, bf16[1,32,1408]{2,1,0:T(8,128)(2,1)}, u32[]{:S(2)}) copy-start(bf16[1,32,1408]{2,1,0:T(8,128)(2,1)} %param.5) | copy-start | bytes 270340
  9.7 7.0 %collective-permute-start.2 = (bf16[2,8,2904]{2,1,0:T(8,128)(2,1)S(1)}, bf16[2,8,2904]{2,1,0:T(8,128)(2,1)S(1)}, u32[]{:S(2)}, u32[]{:S(2)}) collective-permute-start(bf16[2,8,2904]{2,1,0:T(8,128)(2,1)S(1)} %get-tuple-element.26), channel_id=1, source_target_pairs={{0,12},{1,13},{2,14},{3,15},{4,8},{5,9},{6,10},{7,11},{8,4},{9,5},... | collective-permute-start | bytes 278792 | tf_op jit(solution)/shard_map/ppermute | solution.py:279
  16.7 10.4 %collective-permute-start.7 = (bf16[32,1408]{1,0:T(8,128)(2,1)S(1)}, bf16[32,1408]{1,0:T(8,128)(2,1)S(1)}, u32[]{:S(2)}, u32[]{:S(2)}) collective-permute-start(bf16[32,1408]{1,0:T(8,128)(2,1)S(1)} %bitcast.45), channel_id=1, source_target_pairs={{0,12},{1,13},{2,14},{3,15},{4,8},{5,9},{6,10},{7,11},{8,4},{9,5},... | collective-permute-start | bytes 270344 | tf_op jit(solution)/shard_map/ppermute | solution.py:288
  19.2 7.9 %collective-permute-start.6 = (bf16[32,1408]{1,0:T(8,128)(2,1)S(1)}, bf16[32,1408]{1,0:T(8,128)(2,1)S(1)}, u32[]{:S(2)}, u32[]{:S(2)}) collective-permute-start(bf16[32,1408]{1,0:T(8,128)(2,1)S(1)} %bitcast.46), channel_id=1, source_target_pairs={{0,8},{1,9},{2,10},{3,11},{4,12},{5,13},{6,14},{7,15},{8,0},{9,1},... | collective-permute-start | bytes 270344 | tf_op jit(solution)/shard_map/ppermute | solution.py:288
  19.8 7.3 %collective-permute-start.5 = (bf16[32,1408]{1,0:T(8,128)(2,1)S(1)}, bf16[32,1408]{1,0:T(8,128)(2,1)S(1)}, u32[]{:S(2)}, u32[]{:S(2)}) collective-permute-start(bf16[32,1408]{1,0:T(8,128)(2,1)S(1)} %bitcast.47), channel_id=1, source_target_pairs={{0,4},{1,5},{2,6},{3,7},{4,0},{5,1},{6,2},{7,3},{8,12},{9,13},{10,... | collective-permute-start | bytes 270344 | tf_op jit(solution)/shard_map/ppermute | solution.py:288
  21.2 7.7 %collective-permute-start.8 = (bf16[4,2,8,2904]{3,2,0,1:T(8,128)(2,1)S(1)}, bf16[4,2,8,2904]{3,2,0,1:T(8,128)(2,1)S(1)}, u32[]{:S(2)}, u32[]{:S(2)}) collective-permute-start(bf16[4,2,8,2904]{3,2,0,1:T(8,128)(2,1)S(1)} %pad_maximum_fusion.1), channel_id=1, source_target_pairs={{0,2},{1,3},{2,0},{3,1},{4,6},{5,7},{6,4},{7,5},{8,10},{9,11},{10,... | collective-permute-start | bytes 1115144 | tf_op jit(solution)/shard_map/ppermute | solution.py:262
  22.8 20.3 %all-to-all-start = ((bf16[8,8,2904]{2,1,0:T(8,128)(2,1)}), bf16[8,8,2904]{2,1,0:T(8,128)(2,1)S(1)}, u32[]{:S(2)}, u32[]{:S(2)}) async-start(bf16[8,8,2904]{2,1,0:T(8,128)(2,1)} %shard_map.56), calls=%async_computation | async-start | bytes 753664 | tf_op jit(solution)/shard_map/all_to_all | solution.py:261
  26.5 3.0 %collective-permute-start.10 = (bf16[4,8,2904]{2,1,0:T(8,128)(2,1)S(1)}, bf16[4,8,2904]{2,1,0:T(8,128)(2,1)S(1)}, u32[]{:S(2)}, u32[]{:S(2)}) collective-permute-start(bf16[4,8,2904]{2,1,0:T(8,128)(2,1)S(1)} %slice_bitcast_fusion), channel_id=1, source_target_pairs={{0,1},{1,0},{2,3},{3,2},{4,5},{5,4},{6,7},{7,6},{8,9},{9,8},{10,11... | collective-permute-start | bytes 557576 | tf_op jit(solution)/shard_map/ppermute | solution.py:286
  28.9 1.9 %collective-permute-start.9 = (bf16[4,32,1408]{2,1,0:T(8,128)(2,1)S(1)}, bf16[4,32,1408]{2,1,0:T(8,128)(2,1)S(1)}, u32[]{:S(2)}, u32[]{:S(2)}) collective-permute-start(bf16[4,32,1408]{2,1,0:T(8,128)(2,1)S(1)} %pad_maximum_fusion.2.tokens_same_ref), channel_id=1, source_target_pairs={{0,1},{1,0},{2,3},{3,2},{4,5},{5,4},{6,7},{7,6},{8,9},{9,8},{10,11... | collective-permute-start | bytes 1081352 | tf_op jit(solution)/shard_map/ppermute | solution.py:291
  28.9 1.9 %collective-permute-start.11 = (bf16[4,8,2904]{2,1,0:T(8,128)(2,1)S(1)}, bf16[4,8,2904]{2,1,0:T(8,128)(2,1)S(1)}, u32[]{:S(2)}, u32[]{:S(2)}) collective-permute-start(bf16[4,8,2904]{2,1,0:T(8,128)(2,1)S(1)} %slice_bitcast_fusion.1), channel_id=1, source_target_pairs={{0,1},{1,0},{2,3},{3,2},{4,5},{5,4},{6,7},{7,6},{8,9},{9,8},{10,11... | collective-permute-start | bytes 557576 | tf_op jit(solution)/shard_map/ppermute | solution.py:292
  33.4 6.2 %collective-permute-start.14 = (bf16[64,352]{1,0:T(8,128)(2,1)S(1)}, bf16[64,352]{1,0:T(8,128)(2,1)S(1)}, u32[]{:S(2)}, u32[]{:S(2)}) collective-permute-start(bf16[64,352]{1,0:T(8,128)(2,1)S(1)} %get-tuple-element.34), channel_id=1, source_target_pairs={{0,12},{1,13},{2,14},{3,15},{4,8},{5,9},{6,10},{7,11},{8,4},{9,5},... | collective-permute-start | bytes 135176 | tf_op jit(solution)/shard_map/ppermute | solution.py:265
  35.9 7.1 %collective-permute-start.13 = (bf16[64,352]{1,0:T(8,128)(2,1)S(1)}, bf16[64,352]{1,0:T(8,128)(2,1)S(1)}, u32[]{:S(2)}, u32[]{:S(2)}) collective-permute-start(bf16[64,352]{1,0:T(8,128)(2,1)S(1)} %get-tuple-element.34), channel_id=1, source_target_pairs={{0,8},{1,9},{2,10},{3,11},{4,12},{5,13},{6,14},{7,15},{8,0},{9,1},... | collective-permute-start | bytes 135176 | tf_op jit(solution)/shard_map/ppermute | solution.py:265
  36.5 6.5 %collective-permute-start.12 = (bf16[64,352]{1,0:T(8,128)(2,1)S(1)}, bf16[64,352]{1,0:T(8,128)(2,1)S(1)}, u32[]{:S(2)}, u32[]{:S(2)}) collective-permute-start(bf16[64,352]{1,0:T(8,128)(2,1)S(1)} %get-tuple-element.34), channel_id=1, source_target_pairs={{0,4},{1,5},{2,6},{3,7},{4,0},{5,1},{6,2},{7,3},{8,12},{9,13},{10,... | collective-permute-start | bytes 135176 | tf_op jit(solution)/shard_map/ppermute | solution.py:265
  43.0 1.6 %copy-start.2 = (bf16[704,88]{0,1:T(8,128)(2,1)S(1)}, bf16[704,88]{0,1:T(8,128)(2,1)}, u32[]{:S(2)}) copy-start(bf16[704,88]{0,1:T(8,128)(2,1)} %param.7) | copy-start | bytes 371716
  43.0 1.5 %collective-permute-start.15 = (bf16[4,64,352]{2,1,0:T(8,128)(2,1)S(1)}, bf16[4,64,352]{2,1,0:T(8,128)(2,1)S(1)}, u32[]{:S(2)}, u32[]{:S(2)}) collective-permute-start(bf16[4,64,352]{2,1,0:T(8,128)(2,1)S(1)} %pad_maximum_fusion.3.same_ref), channel_id=1, source_target_pairs={{0,1},{1,0},{2,3},{3,2},{4,5},{5,4},{6,7},{7,6},{8,9},{9,8},{10,11... | collective-permute-start | bytes 540680 | tf_op jit(solution)/shard_map/ppermute | solution.py:267
  45.6 5.0 %collective-permute-start.16 = (bf16[128,176]{1,0:T(8,128)(2,1)S(1)}, bf16[128,176]{1,0:T(8,128)(2,1)S(1)}, u32[]{:S(2)}, u32[]{:S(2)}) collective-permute-start(bf16[128,176]{1,0:T(8,128)(2,1)S(1)} %get-tuple-element.40), channel_id=1, source_target_pairs={{0,2},{1,3},{2,0},{3,1},{4,6},{5,7},{6,4},{7,5},{8,10},{9,11},{10,... | collective-permute-start | bytes 135176 | tf_op jit(solution)/shard_map/ppermute | solution.py:262
  46.2 14.9 %collective-permute-start.21 = (bf16[8,8,2904]{2,1,0:T(8,128)(2,1)S(1)}, bf16[8,8,2904]{2,1,0:T(8,128)(2,1)S(1)}, u32[]{:S(2)}, u32[]{:S(2)}) collective-permute-start(bf16[8,8,2904]{2,1,0:T(8,128)(2,1)S(1)} %all-to-all-done.mine_ref), channel_id=1, source_target_pairs={{0,2},{1,3},{2,0},{3,1},{4,6},{5,7},{6,4},{7,5},{8,10},{9,11},{10,... | collective-permute-start | bytes 1115144 | tf_op jit(solution)/shard_map/ppermute | solution.py:262
  50.7 7.2 %collective-permute-start.19 = (bf16[128,352]{1,0:T(8,128)(2,1)S(1)}, bf16[128,352]{1,0:T(8,128)(2,1)S(1)}, u32[]{:S(2)}, u32[]{:S(2)}) collective-permute-start(bf16[128,352]{1,0:T(8,128)(2,1)S(1)} %pad_maximum_fusion.5.mixed_ref), channel_id=1, source_target_pairs={{0,12},{1,13},{2,14},{3,15},{4,8},{5,9},{6,10},{7,11},{8,4},{9,5},... | collective-permute-start | bytes 270344 | tf_op jit(solution)/shard_map/ppermute | solution.py:265
  52.1 8.8 %collective-permute-start.18 = (bf16[128,352]{1,0:T(8,128)(2,1)S(1)}, bf16[128,352]{1,0:T(8,128)(2,1)S(1)}, u32[]{:S(2)}, u32[]{:S(2)}) collective-permute-start(bf16[128,352]{1,0:T(8,128)(2,1)S(1)} %pad_maximum_fusion.5.mixed_ref), channel_id=1, source_target_pairs={{0,8},{1,9},{2,10},{3,11},{4,12},{5,13},{6,14},{7,15},{8,0},{9,1},... | collective-permute-start | bytes 270344 | tf_op jit(solution)/shard_map/ppermute | solution.py:265
  52.2 8.6 %collective-permute-start.17 = (bf16[128,352]{1,0:T(8,128)(2,1)S(1)}, bf16[128,352]{1,0:T(8,128)(2,1)S(1)}, u32[]{:S(2)}, u32[]{:S(2)}) collective-permute-start(bf16[128,352]{1,0:T(8,128)(2,1)S(1)} %pad_maximum_fusion.5.mixed_ref), channel_id=1, source_target_pairs={{0,4},{1,5},{2,6},{3,7},{4,0},{5,1},{6,2},{7,3},{8,12},{9,13},{10,... | collective-permute-start | bytes 270344 | tf_op jit(solution)/shard_map/ppermute | solution.py:265
  61.0 1.8 %collective-permute-start.20 = (bf16[4,128,352]{2,1,0:T(8,128)(2,1)S(1)}, bf16[4,128,352]{2,1,0:T(8,128)(2,1)S(1)}, u32[]{:S(2)}, u32[]{:S(2)}) collective-permute-start(bf16[4,128,352]{2,1,0:T(8,128)(2,1)S(1)} %pad_maximum_fusion.same_ref), channel_id=1, source_target_pairs={{0,1},{1,0},{2,3},{3,2},{4,5},{5,4},{6,7},{7,6},{8,9},{9,8},{10,11... | collective-permute-start | bytes 1081352 | tf_op jit(solution)/shard_map/ppermute | solution.py:267
  65.5 6.5 %collective-permute-start.24 = (bf16[64,352]{1,0:T(8,128)(2,1)S(1)}, bf16[64,352]{1,0:T(8,128)(2,1)S(1)}, u32[]{:S(2)}, u32[]{:S(2)}) collective-permute-start(bf16[64,352]{1,0:T(8,128)(2,1)S(1)} %shard_map.59), channel_id=1, source_target_pairs={{0,12},{1,13},{2,14},{3,15},{4,8},{5,9},{6,10},{7,11},{8,4},{9,5},... | collective-permute-start | bytes 135176 | tf_op jit(solution)/shard_map/ppermute | solution.py:265
  66.8 6.4 %collective-permute-start.23 = (bf16[64,352]{1,0:T(8,128)(2,1)S(1)}, bf16[64,352]{1,0:T(8,128)(2,1)S(1)}, u32[]{:S(2)}, u32[]{:S(2)}) collective-permute-start(bf16[64,352]{1,0:T(8,128)(2,1)S(1)} %shard_map.59), channel_id=1, source_target_pairs={{0,8},{1,9},{2,10},{3,11},{4,12},{5,13},{6,14},{7,15},{8,0},{9,1},... | collective-permute-start | bytes 135176 | tf_op jit(solution)/shard_map/ppermute | solution.py:265
  66.8 6.4 %collective-permute-start.22 = (bf16[64,352]{1,0:T(8,128)(2,1)S(1)}, bf16[64,352]{1,0:T(8,128)(2,1)S(1)}, u32[]{:S(2)}, u32[]{:S(2)}) collective-permute-start(bf16[64,352]{1,0:T(8,128)(2,1)S(1)} %shard_map.59), channel_id=1, source_target_pairs={{0,4},{1,5},{2,6},{3,7},{4,0},{5,1},{6,2},{7,3},{8,12},{9,13},{10,... | collective-permute-start | bytes 135176 | tf_op jit(solution)/shard_map/ppermute | solution.py:265
  73.2 1.6 %copy-start.3 = (bf16[704,88]{0,1:T(8,128)(2,1)S(1)}, bf16[704,88]{0,1:T(8,128)(2,1)}, u32[]{:S(2)}) copy-start(bf16[704,88]{0,1:T(8,128)(2,1)} %param.9) | copy-start | bytes 371716
  73.3 1.5 %collective-permute-start.25 = (bf16[4,64,352]{2,1,0:T(8,128)(2,1)S(1)}, bf16[4,64,352]{2,1,0:T(8,128)(2,1)S(1)}, u32[]{:S(2)}, u32[]{:S(2)}) collective-permute-start(bf16[4,64,352]{2,1,0:T(8,128)(2,1)S(1)} %pad_maximum_fusion.4.same_ref), channel_id=1, source_target_pairs={{0,1},{1,0},{2,3},{3,2},{4,5},{5,4},{6,7},{7,6},{8,9},{9,8},{10,11... | collective-permute-start | bytes 540680 | tf_op jit(solution)/shard_map/ppermute | solution.py:267
